TPU v7x, 32 devices: a whole 2x2x4 slice. The times are simulated.
32 devices in a mesh: groups: 2 (over y), seq: 4 (over z), head: 2 (over x), sub: 2 (over core).
Axes of the slice: x: 2, y: 2, z: 4, core: 2. Of those that a mesh axis runs over, the one named last changes fastest.
Arguments:
- hidden_states: bfloat16 [8192, 8192], P(('groups', 'seq', 'sub'), 'head'), parts along dimension 0, may hold values from -42 to 42
- key_projection_weight: bfloat16 [8192, 1024], P(('seq', 'sub'), 'head'), may hold values from -0.0625 to 0.0625
- value_projection_weight: bfloat16 [8192, 1024], P(('seq', 'sub'), 'head'), may hold values from -0.0625 to 0.0625
- head_basis_matrix: float32 [8, 128, 64], P('head'), may hold values from -0.5 to 0.5
- slot_token: int32 [8192], P(('groups', 'seq', 'sub')), parts along dimension 0, may hold values from 0 to 4095, as said below
Outputs:
- compressed_keys: bfloat16 [8192, 512], P(('groups', 'seq', 'sub'), 'head'), parts along dimension 0
- value_cache: bfloat16 [8192, 1024], P(('groups', 'seq', 'sub'), 'head'), parts along dimension 0
There are 2 independent parts, one for each index of `groups`. A program takes and returns all parts, laid end to end along the dimension named above; an argument that names none is the same for every part. Nothing has to cross between parts.
Inputs may be any that keep to these rules, and one draw needn't show every extreme that they name: `slot_token`: A permutation of the 4096 token positions. Each aligned block of 512 rows holds exactly 64 positions of each aligned block of 512 positions.
All inputs are finite; a program needn't handle non-finite values.
Results may differ from a plain program's by a relative error of at most 0.0055.
Values may be sent and summed in bfloat16 or wider, within the bound.
No kernel may reach another device: no remote copies, remote signals or barrier semaphores. Data moves between devices by JAX's collectives and lax.ppermute only.
A program may use at most 64 MiB of HBM per device.

v0:
```python
import jax
import jax.numpy as jnp
from jax import lax
from jax.sharding import PartitionSpec as P

ridge_share = 0.05


def covariance_sum(decode_key_cache, heads_here, head_dim, token_total):
    per_head_keys = decode_key_cache.reshape(decode_key_cache.shape[0], heads_here, head_dim)
    local_terms = jnp.einsum(
        "thi,thj->hij", per_head_keys, per_head_keys, preferred_element_type=jnp.float32
    )
    summed = lax.psum(local_terms, ("seq", "sub"))
    return summed / token_total


def per_device(
    hidden_states, key_projection_weight, value_projection_weight, head_basis_matrix, slot_token
):
    tokens_here = hidden_states.shape[0]
    seq_count = lax.axis_size("seq")
    core_count = lax.axis_size("sub")
    device_count = seq_count * core_count
    token_total = tokens_here * device_count
    heads_here = head_basis_matrix.shape[0]
    head_dim = head_basis_matrix.shape[1]
    rank_dim = head_basis_matrix.shape[2]
    gathered = lax.all_gather(hidden_states, "head", axis=1, tiled=True)
    key_sums = jnp.dot(
        gathered,
        lax.all_gather(key_projection_weight, ("seq", "sub"), axis=0, tiled=True),
        preferred_element_type=jnp.float32,
    )
    value_sums = jnp.dot(
        gathered,
        lax.all_gather(value_projection_weight, ("seq", "sub"), axis=0, tiled=True),
        preferred_element_type=jnp.float32,
    )
    decode_key_cache = key_sums.astype(jnp.bfloat16)
    moments = covariance_sum(decode_key_cache, heads_here, head_dim, token_total)
    value_cache = value_sums.astype(jnp.bfloat16)
    trace_vals = jnp.trace(moments, axis1=1, axis2=2)
    identity = jnp.eye(head_dim, dtype=jnp.float32)
    regular = moments + (ridge_share * trace_vals / head_dim)[:, None, None] * identity
    factor = jnp.linalg.cholesky(regular)
    by_head = jnp.transpose(
        decode_key_cache.astype(jnp.float32).reshape(tokens_here, heads_here, head_dim), (1, 0, 2)
    )
    whitened = lax.linalg.triangular_solve(
        factor, by_head, left_side=False, lower=True, transpose_a=True
    )
    basis_coefficients = jnp.einsum(
        "htd,hdr->htr", whitened, head_basis_matrix, precision=lax.Precision.HIGHEST
    )
    compressed = (
        jnp.transpose(basis_coefficients, (1, 0, 2))
        .reshape(tokens_here, heads_here * rank_dim)
        .astype(jnp.bfloat16)
    )
    row_order = jnp.argsort(slot_token)
    wanted = slot_token[row_order]
    asked = lax.all_to_all(wanted, ("seq", "sub"), split_axis=0, concat_axis=0, tiled=True)
    local_rows = asked % tokens_here
    got_coeffs, got_values = (
        lax.all_to_all(
            compressed[local_rows], ("seq", "sub"), split_axis=0, concat_axis=0, tiled=True
        ),
        lax.all_to_all(
            value_cache[local_rows], ("seq", "sub"), split_axis=0, concat_axis=0, tiled=True
        ),
    )
    inverse = jnp.argsort(row_order)
    return (got_coeffs[inverse], got_values[inverse])


def solution(mesh):
    return jax.shard_map(
        per_device,
        mesh=mesh,
        in_specs=(
            P(("groups", "seq", "sub"), "head"),
            P(("seq", "sub"), "head"),
            P(("seq", "sub"), "head"),
            P("head", None, None),
            P(("groups", "seq", "sub")),
        ),
        out_specs=(P(("groups", "seq", "sub"), "head"), P(("groups", "seq", "sub"), "head")),
        check_vma=False,
    )
```

profile of v0, /device:TPU:11, one launch (start us, length us, event | category | flops | bytes accessed | tf_op | source)
XLA Modules:
  0.0 401.1 jit_solution(3034889648175689121)
XLA Ops:
  7.2 0.0 copy-start
  7.2 0.0 all-gather.4.cloned.1.call-start
  7.2 0.7 all-gather.4.cloned.1.call-update
  7.9 0.0 all-gather.6.cloned.1.call-start
  8.0 0.7 all-gather.6.cloned.1.call-update
  8.7 0.0 copy-start.1
  8.7 0.0 all-reduce.2.cloned.1.call-start
  8.7 105.1 %all-gather.4.cloned.1.call-done = bf16[512,8192]{1,0:T(8,128)(2,1)} async-done(((bf16[512,4096]{1,0:T(8,128)(2,1)}), bf16[512,8192]{1,0:T(8,128)(2,1)}) %all-gather.4.cloned.1.call-update) | async-done | bytes 8388624 | tf_op jit(solution)/shard_map/all_gather | solution.py:29
  113.8 82.6 %all-gather.6.cloned.1.call-done = bf16[8192,512]{1,0:T(8,128)(2,1)} async-done(((bf16[1024,512]{1,0:T(8,128)(2,1)}), bf16[8192,512]{1,0:T(8,128)(2,1)}) %all-gather.6.cloned.1.call-update) | async-done | bytes 8388624 | tf_op jit(solution)/shard_map/all_gather | solution.py:32
  196.4 10.3 %convolution_convert_fusion.1 = bf16[512,512]{0,1:T(8,128)(2,1)S(1)} fusion(bf16[512,8192]{1,0:T(8,128)(2,1)} %all-gather.4.cloned.1.call-done, bf16[8192,512]{1,0:T(8,128)(2,1)} %all-gather.6.cloned.1.call-done), kind=kOutput, calls=%fused_computation.6 | convolution fusion | flops 4295229440 | bytes 17301504 | tf_op jit(solution)/shard_map/dot_general | solution.py:30
  206.7 1.0 fusion.6
  207.7 0.0 all-reduce.2.cloned.1.call-update
  207.7 0.0 all-gather.8.cloned.1.call-start
  207.8 0.5 all-gather.8.cloned.1.call-update
  208.3 0.0 copy-done.1
  208.3 3.8 sort.31
  212.1 3.5 gather_fusion
  215.6 0.7 all_to_all.24
  216.3 6.2 %all-to-all-start = ((s32[8,64,1]{1,2,0:T(1,128)}), s32[8,64,1]{1,2,0:T(1,128)S(1)}, u32[]{:S(2)}, u32[]{:S(2)}) async-start(s32[8,64,1]{1,2,0:T(1,128)} %bitcast.7), calls=%async_computation | async-start | bytes 8192 | tf_op jit(solution)/shard_map/all_to_all | solution.py:63
  222.5 3.7 all-to-all-done
  226.2 0.5 broadcast.144
  226.7 0.7 reduce.9
  227.3 0.1 all_to_all.26
  227.4 0.3 copy.19
  227.7 33.5 %all-reduce.2.cloned.1.call-done = f32[4,128,128]{2,1,0:T(8,128)} async-done(((f32[4,128,128]{2,1,0:T(8,128)}), f32[4,128,128]{2,1,0:T(8,128)}) %all-reduce.2.cloned.1.call-update) | async-done | bytes 262160 | tf_op jit(solution)/shard_map/psum | solution.py:14
  261.2 1.1 select_reduce_fusion.1
  262.3 1.0 multiply_add_fusion
  263.4 0.1 copy.21
  263.5 1.1 fusion.3
  264.6 46.9 %custom-call.7 = f32[4,128,128]{2,1,0:T(8,128)S(1)} custom-call(f32[4,128,128]{2,1,0:T(8,128)S(1)} %fusion.3), custom_call_target="Cholesky" | custom-call | tf_op jit(solution)/shard_map/jit(cholesky)/cholesky | solution.py:46
  311.5 0.1 compare_reduce_fusion
  311.6 0.1 select_bitcast_fusion
  311.7 39.3 %custom-call.8 = f32[4,1,128,128]{2,3,1,0:T(8,128)S(1)} custom-call(f32[4,1,128,128]{3,2,1,0:T(8,128)S(1)} %select_bitcast_fusion), custom_call_target="InvertDiagBlocksLowerTriangular" | custom-call | tf_op jit(solution)/shard_map/triangular_solve | solution.py:50
  351.1 0.6 fusion
  351.6 0.0 copy-done
  351.6 1.3 convolution_convert_fusion.2
  352.9 0.1 copy.24
  353.0 2.6 gather_fusion.1
  355.6 6.5 %all-to-all-start.1 = ((bf16[8,64,256]{2,1,0:T(8,128)(2,1)}), bf16[8,64,256]{2,1,0:T(8,128)(2,1)S(1)}, u32[]{:S(2)}, u32[]{:S(2)}) async-start(bf16[8,64,256]{2,1,0:T(8,128)(2,1)} %bitcast.9), calls=%async_computation.1 | async-start | bytes 524288 | tf_op jit(solution)/shard_map/all_to_all | solution.py:66
  362.1 0.0 all-gather.8.cloned.1.call-done
  362.1 10.2 %convolution_convert_fusion = bf16[512,512]{1,0:T(8,128)(2,1)S(1)} fusion(bf16[512,8192]{1,0:T(8,128)(2,1)} %all-gather.4.cloned.1.call-done, bf16[8192,512]{1,0:T(8,128)(2,1)} %all-gather.8.cloned.1.call-done), kind=kOutput, calls=%fused_computation.5 | convolution fusion | flops 4295229440 | bytes 17301504 | tf_op jit(solution)/shard_map/dot_general | solution.py:35
  372.3 2.6 gather_fusion.3
  375.0 0.0 all-to-all-done.1
  375.0 5.1 %all-to-all-start.2 = ((bf16[8,64,512]{2,1,0:T(8,128)(2,1)}), bf16[8,64,512]{2,1,0:T(8,128)(2,1)S(1)}, u32[]{:S(2)}, u32[]{:S(2)}) async-start(bf16[8,64,512]{2,1,0:T(8,128)(2,1)} %bitcast.11), calls=%async_computation.2 | async-start | bytes 1048576 | tf_op jit(solution)/shard_map/all_to_all | solution.py:69
  380.1 3.8 sort.32
  383.9 2.6 gather_fusion.2
  386.5 5.4 %all-to-all-done.2 = bf16[8,64,512]{2,1,0:T(8,128)(2,1)S(1)} async-done(((bf16[8,64,512]{2,1,0:T(8,128)(2,1)}), bf16[8,64,512]{2,1,0:T(8,128)(2,1)S(1)}, u32[]{:S(2)}, u32[]{:S(2)}) %all-to-all-start.2) | async-done | bytes 524320 | tf_op jit(solution)/shard_map/all_to_all | solution.py:69
  391.9 2.6 gather_fusion.4
  (13 shorter events, 0.1 us)
Async XLA Ops:
  7.2 344.5 %copy-start = (f32[4,128,64]{1,2,0:T(8,128)S(1)}, f32[4,128,64]{1,2,0:T(8,128)}, u32[]{:S(2)}) copy-start(f32[4,128,64]{1,2,0:T(8,128)} %param.8) | copy-start | bytes 393220
  7.2 106.6 %all-gather.4.cloned.1.call-start = ((), (), s32[]{:S(2)}) async-start(), calls=%async_computation.3 | async-start | bytes 12582912 | tf_op jit(solution)/shard_map/all_gather | solution.py:29
  7.9 188.5 %all-gather.6.cloned.1.call-start = ((), (), s32[]{:S(2)}) async-start(), calls=%async_computation.4 | async-start | bytes 9437184 | tf_op jit(solution)/shard_map/all_gather | solution.py:32
  8.7 199.7 %copy-start.1 = (s32[512]{0:T(512)S(1)}, s32[512]{0:T(512)}, u32[]{:S(2)}) copy-start(s32[512]{0:T(512)} %param.9) | copy-start | bytes 6148
  8.7 252.5 %all-reduce.2.cloned.1.call-start = ((), (), s32[]{:S(2)}) async-start(), calls=%async_computation.5 | async-start | bytes 524288 | tf_op jit(solution)/shard_map/psum | solution.py:14
  207.7 154.4 %all-gather.8.cloned.1.call-start = ((), (), s32[]{:S(2)}) async-start(), calls=%async_computation.6 | async-start | bytes 9437184 | tf_op jit(solution)/shard_map/all_gather | solution.py:37
  216.3 9.9 %all-to-all-start = ((s32[8,64,1]{1,2,0:T(1,128)}), s32[8,64,1]{1,2,0:T(1,128)S(1)}, u32[]{:S(2)}, u32[]{:S(2)}) async-start(s32[8,64,1]{1,2,0:T(1,128)} %bitcast.7), calls=%async_computation | async-start | bytes 8192 | tf_op jit(solution)/shard_map/all_to_all | solution.py:63
  355.6 19.3 %all-to-all-start.1 = ((bf16[8,64,256]{2,1,0:T(8,128)(2,1)}), bf16[8,64,256]{2,1,0:T(8,128)(2,1)S(1)}, u32[]{:S(2)}, u32[]{:S(2)}) async-start(bf16[8,64,256]{2,1,0:T(8,128)(2,1)} %bitcast.9), calls=%async_computation.1 | async-start | bytes 524288 | tf_op jit(solution)/shard_map/all_to_all | solution.py:66
  375.0 16.9 %all-to-all-start.2 = ((bf16[8,64,512]{2,1,0:T(8,128)(2,1)}), bf16[8,64,512]{2,1,0:T(8,128)(2,1)S(1)}, u32[]{:S(2)}, u32[]{:S(2)}) async-start(bf16[8,64,512]{2,1,0:T(8,128)(2,1)} %bitcast.11), calls=%async_computation.2 | async-start | bytes 1048576 | tf_op jit(solution)/shard_map/all_to_all | solution.py:69
Sparse Core Ops, SparseCore 0:
  9.6 104.2 all-gather.3
  115.4 80.9 all-gather.5
  207.8 53.3 all-reduce.1
  262.8 81.4 all-gather.7
where the time goes:
time: 406 us; the launch traced here: 401 us
  waiting for transfers between devices  232 us (57%)
  other arithmetic  98 us (24%)
  matrix products  23.4 us (6%)
  starting transfers between devices  17.9 us (4%)
  local copies, waits for them, and re-layouts  15.7 us (4%)
  between operations  13.9 us (3%)
    all_gather x1, waiting for transfers between devices, per_device(): gathered = lax.all_gather(hidden_states, 'head', axis=1, tiled=True)  105 us
    all_gather x1, waiting for transfers between devices, per_device(): lax.all_gather(key_projection_weight, ('seq', 'sub'), axis=0, tiled=True)  82.6 us
    another operation x4, other arithmetic, per_device(): factor = jnp.linalg.cholesky(regular)  47.1 us
    another operation x3, other arithmetic, per_device(): lax.linalg.triangular_solve(factor, by_head, left_side=False, lower=True,...  39.4 us
    psum x1, waiting for transfers between devices, covariance_sum(): summed = lax.psum(local_terms, ('seq', 'sub'))  33.5 us
    dot_general x1, matrix products, per_device(): jnp.dot(gathered, lax.all_gather(key_projection_weight, ('seq', 'sub'), a...  10.3 us
    dot_general x1, matrix products, per_device(): jnp.dot(gathered, lax.all_gather(value_projection_weight, ('seq', 'sub'),...  10.2 us
  transfers between devices with their start and end apart: 7, of which 5 were waited for; matrix products, arithmetic and copies ran while one was open for 31% of the time, Pallas kernels for 0%

commit v1 on v0

v1 whole, which is shorter than its diff:
```python
import functools

import jax
import jax.numpy as jnp
from jax import lax
from jax.experimental import pallas as pl
from jax.experimental.pallas import tpu as pltpu
from jax.sharding import PartitionSpec as P

ridge_share = 0.05
SWAP = [(0, 1), (1, 0)]


def rotation(count, shift):
    return [(i, (i + shift) % count) for i in range(count)]


def solve_kernel(scale, parts, *refs):
    m_refs, basis_ref, out_ref = refs[:parts], refs[parts], refs[parts + 1]
    heads, dim, _ = basis_ref.shape
    total = m_refs[0][...]
    for ref in m_refs[1:]:
        total = total + ref[...]
    total = total * scale
    row = lax.broadcasted_iota(jnp.int32, (1, dim, dim), 1)
    col = lax.broadcasted_iota(jnp.int32, (1, dim, dim), 2)
    diag = row == col
    trace = jnp.sum(jnp.where(diag, total, 0.0), axis=(1, 2), keepdims=True)
    work = total + jnp.where(diag, ridge_share * trace / dim, 0.0)
    tiles = [work[:, r : r + 8, :] for r in range(0, dim, 8)]
    lane = lax.broadcasted_iota(jnp.int32, (1, 1, dim), 2)
    sub = lax.broadcasted_iota(jnp.int32, (1, 8, 1), 1)
    for j in range(dim):
        t0, j0 = j // 8, j % 8
        pivot_row = tiles[t0][:, j0 : j0 + 1, :]
        inv = 1.0 / pivot_row[:, :, j : j + 1]
        scaled = jnp.where(lane == j, inv, pivot_row * inv)
        at = lane == j
        for t in range(t0, dim // 8):
            if t == t0 and j0 == 7:
                continue
            f = tiles[t][:, :, j : j + 1]
            if t == t0:
                f = jnp.where(sub > j0, f, 0.0)
                base = jnp.where(at & (sub > j0), 0.0, tiles[t])
            else:
                base = jnp.where(at, 0.0, tiles[t])
            tiles[t] = base - f * scaled
    work = jnp.concatenate(tiles, axis=1)
    pivots = jnp.sum(jnp.where(diag, work, 0.0), axis=2, keepdims=True)
    inverse = jnp.where(row > col, work, jnp.where(diag, 1.0, 0.0))
    scaled_basis = basis_ref[...] * lax.rsqrt(pivots)
    for h in range(heads):
        out_ref[h] = lax.dot_general(
            inverse[h].T,
            scaled_basis[h],
            (((1,), (0,)), ((), ())),
            precision=lax.Precision.HIGHEST,
            preferred_element_type=jnp.float32,
        )


def solve(parts, basis, token_total):
    heads, dim, rank = basis.shape
    vmem = pl.BlockSpec(memory_space=pltpu.VMEM)
    return pl.pallas_call(
        functools.partial(solve_kernel, 1.0 / token_total, len(parts)),
        out_shape=jax.ShapeDtypeStruct((heads, dim, rank), jnp.float32),
        in_specs=[vmem] * (len(parts) + 1),
        out_specs=vmem,
        cost_estimate=pl.CostEstimate(flops=heads * dim**3, bytes_accessed=4 * heads * dim * dim, transcendentals=0),
    )(*parts, basis)


def per_device(hidden_states, key_w, value_w, basis, slot):
    tokens = hidden_states.shape[0]
    seq, head, cores = lax.axis_size("seq"), lax.axis_size("head"), lax.axis_size("sub")
    h_at, c_at = lax.axis_index("head"), lax.axis_index("sub")
    peers = seq * cores
    share = tokens // peers
    heads, dim, rank = basis.shape
    width = heads * dim

    block = slot // tokens
    place = lax.iota(jnp.int32, tokens)
    before = (block[None, :] == block[:, None]) & (place[None, :] < place[:, None])
    position = block * share + jnp.sum(before.astype(jnp.int32), axis=1)
    hits = position[:, None] == place[None, :]
    wanted = jnp.sum(jnp.where(hits, (slot - block * tokens)[:, None], 0), axis=0)
    asked = lax.all_to_all(wanted, ("seq", "sub"), split_axis=0, concat_axis=0, tiled=True)
    pick = (asked[:, None] == place[None, :]).astype(jnp.bfloat16)
    unpick = hits.astype(jnp.bfloat16)

    feats = hidden_states.shape[1]
    weights = lax.all_gather(
        jnp.concatenate([key_w, value_w], axis=1), ("seq", "sub"), axis=0, tiled=True
    )
    sums = None
    for d in range(head):
        x = hidden_states if d == 0 else lax.ppermute(hidden_states, "head", rotation(head, -d))
        w = lax.dynamic_slice_in_dim(weights, lax.rem(h_at + d, head) * feats, feats, axis=0)
        term = jnp.dot(x, w, preferred_element_type=jnp.float32)
        sums = term if sums is None else sums + term
    both = sums.astype(jnp.bfloat16)
    keys = both[:, :width].reshape(tokens, heads, dim)

    mine = heads // cores
    local = jnp.einsum("thi,thj->hij", keys, keys, preferred_element_type=jnp.float32)
    local = local.reshape(cores, mine, dim, dim)
    chip = lax.dynamic_index_in_dim(local, c_at, 0, keepdims=False) + lax.ppermute(
        lax.dynamic_index_in_dim(local, 1 - c_at, 0, keepdims=False), "sub", SWAP
    )
    parts = [chip] + [lax.ppermute(chip, "seq", rotation(seq, d)) for d in range(1, seq)]
    basis_here = lax.dynamic_slice_in_dim(basis, c_at * mine, mine, axis=0)
    solved = solve(parts, basis_here, tokens * peers)
    other = lax.ppermute(solved, "sub", SWAP)
    maps = jnp.where(
        c_at == 0, jnp.concatenate([solved, other]), jnp.concatenate([other, solved])
    )

    sent = jnp.dot(pick, both, preferred_element_type=jnp.float32).astype(jnp.bfloat16)
    got = lax.all_to_all(sent, ("seq", "sub"), split_axis=0, concat_axis=0, tiled=True)
    rows = jnp.dot(unpick, got, preferred_element_type=jnp.float32).astype(jnp.bfloat16)
    coeffs = jnp.einsum(
        "thd,hdr->thr",
        rows[:, :width].astype(jnp.float32).reshape(tokens, heads, dim),
        maps,
        precision=lax.Precision.HIGHEST,
    )
    return coeffs.reshape(tokens, heads * rank).astype(jnp.bfloat16), rows[:, width:]


def solution(mesh):
    return jax.shard_map(
        per_device,
        mesh=mesh,
        in_specs=(
            P(("groups", "seq", "sub"), "head"),
            P(("seq", "sub"), "head"),
            P(("seq", "sub"), "head"),
            P("head", None, None),
            P(("groups", "seq", "sub")),
        ),
        out_specs=(P(("groups", "seq", "sub"), "head"), P(("groups", "seq", "sub"), "head")),
        check_vma=False,
    )
```

time: 406 us -> 246 us (0.61); the launches traced: 401 us -> 246 us
  other arithmetic: 98 us -> 4.31 us
  waiting for transfers between devices: 232 us -> 172 us
  Pallas kernels: 0 us -> 13.1 us
  local copies, waits for them, and re-layouts: 15.7 us -> 5.49 us
  matrix products: 23.4 us -> 18.6 us
    another operation x7 -> x0, other arithmetic: 86.5 us -> none  [the longest x4 47.1 us: per_device(): factor = jnp.linalg.cholesky(regular)]
    all_gather x3 -> x1, waiting for transfers between devices: 188 us -> 138 us  [per_device(): lax.all_gather(jnp.concatenate([key_w, value_w], axis=1), ('seq', 'sub'),...]
    psum x1 -> x0, waiting for transfers between devices: 33.5 us -> none  [covariance_sum(): summed = lax.psum(local_terms, ('seq', 'sub'))]
    ppermute x0 -> x6, waiting for transfers between devices: none -> 30.7 us  [the longest x3 29.7 us: per_device(): lax.ppermute(chip, 'seq', rotation(seq, d))]
    gather x5 -> x0, local copies, waits for them, and re-layouts: 13.9 us -> none  [the longest x2 5.2 us: per_device(): return (got_coeffs[inverse], got_values[inverse])]
    pallas_call x0 -> x1, Pallas kernels: none -> 13.1 us  [solve(): pl.pallas_call(functools.partial(solve_kernel, 1.0 / token_total, len(par...]
    sort x2 -> x0, other arithmetic: 7.54 us -> none  [the longest x1 3.77 us: per_device(): inverse = jnp.argsort(row_order)]
    all_to_all x2 -> x1, waiting for transfers between devices: 5.44 us -> 0.01 us  [per_device(): lax.all_to_all(sent, ('seq', 'sub'), split_axis=0, concat_axis=0, tiled=T...]
  transfers between devices with their start and end apart: 7 -> 9, of which waited for: 5 -> 6; matrix products, arithmetic and copies ran while one was open for 31% -> 5% of each run, Pallas kernels for 0% -> 5%
where the time goes in v1:
time: 246 us
  waiting for transfers between devices  172 us (70%)
  matrix products  18.6 us (8%)
  starting transfers between devices  17.8 us (7%)
  between operations  14.2 us (6%)
  Pallas kernels  13.1 us (5%)
  local copies, waits for them, and re-layouts  5.49 us (2%)
  other arithmetic  4.31 us (2%)
    all_gather x1, waiting for transfers between devices, per_device(): lax.all_gather(jnp.concatenate([key_w, value_w], axis=1), ('seq', 'sub'),...  138 us
    ppermute x3, waiting for transfers between devices, per_device(): lax.ppermute(chip, 'seq', rotation(seq, d))  29.7 us
    dot_general x2, matrix products, per_device(): term = jnp.dot(x, w, preferred_element_type=jnp.float32)  15.1 us
    pallas_call x1, Pallas kernels, solve(): pl.pallas_call(functools.partial(solve_kernel, 1.0 / token_total, len(par...  13.1 us
    all_to_all x1, starting transfers between devices, per_device(): lax.all_to_all(sent, ('seq', 'sub'), split_axis=0, concat_axis=0, tiled=T...  6.64 us
    all_to_all x1, starting transfers between devices, per_device(): lax.all_to_all(wanted, ('seq', 'sub'), split_axis=0, concat_axis=0, tiled...  5.92 us
  transfers between devices with their start and end apart: 9, of which 6 were waited for; matrix products, arithmetic and copies ran while one was open for 5% of the time, Pallas kernels for 5%

profile of v1, /device:TPU:11, one launch (start us, length us, event | category | flops | bytes accessed | tf_op | source)
XLA Modules:
  0.0 245.6 jit_solution(14490355681290421939)
XLA Ops:
  7.2 0.0 copy-start
  7.2 0.0 copy-start.6
  7.2 0.0 all-gather.2.cloned.1.call-start
  7.2 3.1 %pad_maximum_fusion = bf16[1024,1024]{1,0:T(8,128)(2,1)} fusion(bf16[1024,512]{1,0:T(8,128)(2,1)} %param.7, bf16[1024,512]{1,0:T(8,128)(2,1)} %param.6), kind=kLoop, calls=%fused_computation.4 | loop fusion | flops 4194304 | bytes 4194304 | tf_op jit(solution)/shard_map/concatenate | solution.py:96
  10.4 0.0 all-gather.2.cloned.1.call-update
  10.4 0.3 collective-permute-start
  10.7 0.0 copy-done.6
  10.7 0.2 convert_reduce_fusion
  11.0 0.2 select_reduce_fusion
  11.2 0.7 all_to_all.14
  11.9 5.9 %all-to-all-start = ((s32[8,64,1]{1,2,0:T(1,128)}), s32[8,64,1]{1,2,0:T(1,128)S(1)}, u32[]{:S(2)}, u32[]{:S(2)}) async-start(s32[8,64,1]{1,2,0:T(1,128)} %bitcast.5), calls=%async_computation | async-start | bytes 8192 | tf_op jit(solution)/shard_map/all_to_all | solution.py:90
  17.8 3.7 %all-to-all-done = s32[8,64,1]{1,2,0:T(1,128)S(1)} async-done(((s32[8,64,1]{1,2,0:T(1,128)}), s32[8,64,1]{1,2,0:T(1,128)S(1)}, u32[]{:S(2)}, u32[]{:S(2)}) %all-to-all-start) | async-done | bytes 2080 | tf_op jit(solution)/shard_map/all_to_all | solution.py:90
  21.5 0.5 broadcast.22
  22.0 0.7 reduce.3
  22.7 0.1 eq.46
  22.8 137.7 %all-gather.2.cloned.1.call-done = bf16[8192,1024]{1,0:T(8,128)(2,1)} async-done(((bf16[1024,1024]{1,0:T(8,128)(2,1)}), bf16[8192,1024]{1,0:T(8,128)(2,1)}) %all-gather.2.cloned.1.call-update) | async-done | bytes 16777232 | tf_op jit(solution)/shard_map/all_gather | solution.py:95
  160.5 0.0 copy-start.7
  160.5 8.4 %fusion.2 = f32[1024,512]{1,0:T(8,128)S(1)} fusion(bf16[512,4096]{1,0:T(8,128)(2,1)} %param.5, bf16[8192,1024]{1,0:T(8,128)(2,1)} %all-gather.2.cloned.1.call-done, s32[]{:T(128)S(6)} %select_n.34), kind=kOutput, calls=%fused_computation.2 | convolution fusion | flops 4294967296 | bytes 14680068 | tf_op jit(solution)/shard_map/dot_general | solution.py:102
  168.9 0.0 collective-permute-done
  168.9 1.0 copy-done.7
  169.9 6.7 %add_convert_fusion = bf16[1024,512]{1,0:T(8,128)(2,1)S(1)} fusion(f32[1024,512]{1,0:T(8,128)S(1)} %fusion.2, bf16[512,4096]{1,0:T(8,128)(2,1)} %collective-permute-done, bf16[8192,1024]{1,0:T(8,128)(2,1)S(1)} %copy-done.7, s32[]{:T(128)S(6)} %select_n.35), kind=kOutput, calls=%fused_computation.5 | convolution fusion | flops 4296015872 | bytes 15728644 | tf_op jit(solution)/shard_map/dot_general | solution.py:102
  176.6 1.7 convolution_convert_fusion.1
  178.4 6.6 %all-to-all-start.1 = ((bf16[8,64,1024]{2,1,0:T(8,128)(2,1)}), bf16[8,64,1024]{2,1,0:T(8,128)(2,1)S(1)}, u32[]{:S(2)}, u32[]{:S(2)}) async-start(bf16[8,64,1024]{2,1,0:T(8,128)(2,1)} %bitcast.6), calls=%async_computation.1 | async-start | bytes 2097152 | tf_op jit(solution)/shard_map/all_to_all | solution.py:122
  185.1 0.3 fusion.23
  185.4 0.4 collective-permute-start.1
  185.8 1.0 collective-permute-done.1
  186.8 0.0 copy-start.1
  186.8 1.2 collective-permute-start.2
  188.1 1.0 collective-permute-start.3
  189.1 1.4 collective-permute-start.4
  190.5 0.0 copy-done
  190.5 0.8 copy.31.refs_4_
  191.2 25.2 %collective-permute-done.2.refs_1_ = f32[2,128,128]{2,1,0:T(8,128)S(1)} collective-permute-done((f32[2,128,128]{2,1,0:T(8,128)S(1)}, f32[2,128,128]{2,1,0:T(8,128)S(1)}, u32[]{:S(2)}, u32[]{:S(2)}) %collective-permute-start.2) | collective-permute-done | bytes 131104 | tf_op jit(solution)/shard_map/ppermute | solution.py:113
  216.4 0.0 copy-start.2
  216.4 2.8 %collective-permute-done.3.refs_2_ = f32[2,128,128]{2,1,0:T(8,128)S(1)} collective-permute-done((f32[2,128,128]{2,1,0:T(8,128)S(1)}, f32[2,128,128]{2,1,0:T(8,128)S(1)}, u32[]{:S(2)}, u32[]{:S(2)}) %collective-permute-start.3) | collective-permute-done | bytes 131104 | tf_op jit(solution)/shard_map/ppermute | solution.py:113
  219.2 0.0 copy-start.3
  219.2 1.7 collective-permute-done.4.refs_3_
  220.9 0.0 copy-done.1
  220.9 0.0 copy-done.2
  220.9 0.0 copy-done.3
  220.9 0.0 copy-start.4
  220.9 0.6 copy-done.4
  221.6 13.1 %shard_map.68 = f32[2,128,64]{2,1,0:T(8,128)} custom-call(f32[2,128,128]{2,1,0:T(8,128)} %copy-done.1, f32[2,128,128]{2,1,0:T(8,128)} %copy-done.2, f32[2,128,128]{2,1,0:T(8,128)} %copy-done.3, f32[2,128,128]{2,1,0:T(8,128)} %copy-done.4, f32[2,128,64]{2,1,0:T(8,128)} %copy.31.refs_4_), custom_call_target="tpu_custom_call" | custom-call | flops 4194304 | bytes 131072 | tf_op jit(solution)/shard_map/pallas_call | solution.py:66
  234.6 0.0 copy-start.5
  234.7 0.9 collective-permute-start.5
  235.5 0.0 all-to-all-done.1
  235.5 0.8 convolution_convert_fusion
  236.3 0.9 fusion.22
  237.2 0.0 collective-permute-done.5
  237.2 0.0 copy-done.5
  237.2 0.7 convolution_convert_fusion.2
  237.9 0.8 copy.28
  (6 shorter events, 0.1 us)
Async XLA Ops:
  7.2 183.3 %copy-start = (f32[4,128,64]{1,2,0:T(8,128)S(1)}, f32[4,128,64]{1,2,0:T(8,128)}, u32[]{:S(2)}) copy-start(f32[4,128,64]{1,2,0:T(8,128)} %param.8) | copy-start | bytes 393220
  7.2 3.5 %copy-start.6 = (s32[512]{0:T(512)S(1)}, s32[512]{0:T(512)}, u32[]{:S(2)}) copy-start(s32[512]{0:T(512)} %param.9) | copy-start | bytes 6148
  7.2 153.3 %all-gather.2.cloned.1.call-start = ((), (), s32[]{:S(2)}) async-start(), calls=%async_computation.2 | async-start | bytes 18874368 | tf_op jit(solution)/shard_map/all_gather | solution.py:95
  10.4 158.5 %collective-permute-start = (bf16[512,4096]{1,0:T(8,128)(2,1)}, bf16[512,4096]{1,0:T(8,128)(2,1)}, u32[]{:S(2)}, u32[]{:S(2)}) collective-permute-start(bf16[512,4096]{1,0:T(8,128)(2,1)} %param.5), channel_id=1, source_target_pairs={{0,2},{2,0},{1,3},{3,1},{4,6},{6,4},{5,7},{7,5},{8,10},{10,8},{9,1... | collective-permute-start | bytes 12582920 | tf_op jit(solution)/shard_map/ppermute | solution.py:100
  11.9 9.6 %all-to-all-start = ((s32[8,64,1]{1,2,0:T(1,128)}), s32[8,64,1]{1,2,0:T(1,128)S(1)}, u32[]{:S(2)}, u32[]{:S(2)}) async-start(s32[8,64,1]{1,2,0:T(1,128)} %bitcast.5), calls=%async_computation | async-start | bytes 8192 | tf_op jit(solution)/shard_map/all_to_all | solution.py:90
  160.5 9.4 %copy-start.7 = (bf16[8192,1024]{1,0:T(8,128)(2,1)S(1)}, bf16[8192,1024]{1,0:T(8,128)(2,1)}, u32[]{:S(2)}) copy-start(bf16[8192,1024]{1,0:T(8,128)(2,1)} %all-gather.2.cloned.1.call-done) | copy-start | bytes 50331652
  178.4 57.1 %all-to-all-start.1 = ((bf16[8,64,1024]{2,1,0:T(8,128)(2,1)}), bf16[8,64,1024]{2,1,0:T(8,128)(2,1)S(1)}, u32[]{:S(2)}, u32[]{:S(2)}) async-start(bf16[8,64,1024]{2,1,0:T(8,128)(2,1)} %bitcast.6), calls=%async_computation.1 | async-start | bytes 2097152 | tf_op jit(solution)/shard_map/all_to_all | solution.py:122
  185.4 1.4 collective-permute-start.1
  186.8 34.1 %copy-start.1 = (f32[2,128,128]{2,1,0:T(8,128)}, f32[2,128,128]{2,1,0:T(8,128)S(1)}, u32[]{:S(2)}) copy-start(f32[2,128,128]{2,1,0:T(8,128)S(1)} %bitcast_add_fusion.refs_0_) | copy-start | bytes 393220
  186.8 29.5 %collective-permute-start.2 = (f32[2,128,128]{2,1,0:T(8,128)S(1)}, f32[2,128,128]{2,1,0:T(8,128)S(1)}, u32[]{:S(2)}, u32[]{:S(2)}) collective-permute-start(f32[2,128,128]{2,1,0:T(8,128)S(1)} %bitcast_add_fusion.refs_0_), channel_id=1, source_target_pairs={{0,4},{4,8},{8,12},{12,0},{1,5},{5,9},{9,13},{13,1},{2,6},{6,10},{... | collective-permute-start | bytes 393224 | tf_op jit(solution)/shard_map/ppermute | solution.py:113
  188.1 31.1 %collective-permute-start.3 = (f32[2,128,128]{2,1,0:T(8,128)S(1)}, f32[2,128,128]{2,1,0:T(8,128)S(1)}, u32[]{:S(2)}, u32[]{:S(2)}) collective-permute-start(f32[2,128,128]{2,1,0:T(8,128)S(1)} %bitcast_add_fusion.refs_0_), channel_id=1, source_target_pairs={{0,8},{4,12},{8,0},{12,4},{1,9},{5,13},{9,1},{13,5},{2,10},{6,14},... | collective-permute-start | bytes 393224 | tf_op jit(solution)/shard_map/ppermute | solution.py:113
  189.1 31.8 %collective-permute-start.4 = (f32[2,128,128]{2,1,0:T(8,128)S(1)}, f32[2,128,128]{2,1,0:T(8,128)S(1)}, u32[]{:S(2)}, u32[]{:S(2)}) collective-permute-start(f32[2,128,128]{2,1,0:T(8,128)S(1)} %bitcast_add_fusion.refs_0_), channel_id=1, source_target_pairs={{0,12},{4,0},{8,4},{12,8},{1,13},{5,1},{9,5},{13,9},{2,14},{6,2},{... | collective-permute-start | bytes 393224 | tf_op jit(solution)/shard_map/ppermute | solution.py:113
  216.4 4.5 %copy-start.2 = (f32[2,128,128]{2,1,0:T(8,128)}, f32[2,128,128]{2,1,0:T(8,128)S(1)}, u32[]{:S(2)}) copy-start(f32[2,128,128]{2,1,0:T(8,128)S(1)} %collective-permute-done.2.refs_1_) | copy-start | bytes 393220
  219.2 1.7 copy-start.3
  220.9 0.7 copy-start.4
  234.6 2.5 %copy-start.5 = (f32[2,128,64]{2,1,0:T(8,128)S(1)}, f32[2,128,64]{2,1,0:T(8,128)}, u32[]{:S(2)}) copy-start(f32[2,128,64]{2,1,0:T(8,128)} %shard_map.68) | copy-start | bytes 196612
  234.7 2.5 %collective-permute-start.5 = (f32[2,128,64]{2,1,0:T(8,128)}, f32[2,128,64]{2,1,0:T(8,128)S(1)}, u32[]{:S(2)}, u32[]{:S(2)}) collective-permute-start(f32[2,128,64]{2,1,0:T(8,128)} %shard_map.68), channel_id=1, source_target_pairs={{0,1},{1,0},{2,3},{3,2},{4,5},{5,4},{6,7},{7,6},{8,9},{9,8},{10,11... | collective-permute-start | bytes 196616 | tf_op jit(solution)/shard_map/ppermute | solution.py:116
Sparse Core Ops, SparseCore 0:
  10.5 149.9 all-gather.1

commit v2 on v1

v2 whole, which is shorter than its diff:
```python
import functools

import jax
import jax.numpy as jnp
from jax import lax
from jax.experimental import pallas as pl
from jax.experimental.pallas import tpu as pltpu
from jax.sharding import PartitionSpec as P

ridge_share = 0.05
SWAP = [(0, 1), (1, 0)]


def rotation(count, shift):
    return [(i, (i + shift) % count) for i in range(count)]


def xor(count, distance):
    return [(i, i ^ distance) for i in range(count)]


def pack(moments):
    first, second = moments[..., 0, :, :], moments[..., 1, :, :]
    dim = first.shape[-1]
    row = lax.broadcasted_iota(jnp.int32, (dim, dim), 0)
    col = lax.broadcasted_iota(jnp.int32, (dim, dim), 1)
    both = jnp.where(row >= col, first, second)
    diagonal = jnp.sum(jnp.where(row == col, second, 0.0), axis=-2, keepdims=True)
    return jnp.concatenate([both, jnp.broadcast_to(diagonal, (*both.shape[:-2], 8, dim))], axis=-2)


def unpack(packed):
    dim = packed.shape[1]
    row = lax.broadcasted_iota(jnp.int32, (dim, dim), 0)
    col = lax.broadcasted_iota(jnp.int32, (dim, dim), 1)
    both, diagonal = packed[:dim], packed[dim : dim + 1]
    turned = both.T
    first = jnp.where(row >= col, both, turned)
    second = jnp.where(row < col, both, jnp.where(row == col, diagonal, turned))
    return jnp.stack([first, second])


def solve_kernel(scale, parts, packed, *refs):
    m_refs, basis_ref, out_ref = refs[:parts], refs[parts], refs[parts + 1]
    heads, dim, _ = basis_ref.shape
    total = m_refs[0][...]
    for ref in m_refs[1:]:
        total = total + ref[...]
    total = total * scale
    if packed:
        total = unpack(total)
    row = lax.broadcasted_iota(jnp.int32, (1, dim, dim), 1)
    col = lax.broadcasted_iota(jnp.int32, (1, dim, dim), 2)
    diag = row == col
    trace = jnp.sum(jnp.where(diag, total, 0.0), axis=(1, 2), keepdims=True)
    work = total + jnp.where(diag, ridge_share * trace / dim, 0.0)
    tiles = [work[:, r : r + 8, :] for r in range(0, dim, 8)]
    lane = lax.broadcasted_iota(jnp.int32, (1, 1, dim), 2)
    sub = lax.broadcasted_iota(jnp.int32, (1, 8, 1), 1)
    for j in range(dim):
        t0, j0 = j // 8, j % 8
        pivot_row = tiles[t0][:, j0 : j0 + 1, :]
        inv = 1.0 / pivot_row[:, :, j : j + 1]
        scaled = jnp.where(lane == j, inv, pivot_row * inv)
        at = lane == j
        for t in range(t0, dim // 8):
            if t == t0 and j0 == 7:
                continue
            f = tiles[t][:, :, j : j + 1]
            if t == t0:
                f = jnp.where(sub > j0, f, 0.0)
                base = jnp.where(at & (sub > j0), 0.0, tiles[t])
            else:
                base = jnp.where(at, 0.0, tiles[t])
            tiles[t] = base - f * scaled
    work = jnp.concatenate(tiles, axis=1)
    pivots = jnp.sum(jnp.where(diag, work, 0.0), axis=2, keepdims=True)
    inverse = jnp.where(row > col, work, jnp.where(diag, 1.0, 0.0))
    scaled_basis = basis_ref[...] * lax.rsqrt(pivots)
    for h in range(heads):
        out_ref[h] = lax.dot_general(
            inverse[h].T,
            scaled_basis[h],
            (((1,), (0,)), ((), ())),
            precision=lax.Precision.HIGHEST,
            preferred_element_type=jnp.float32,
        )


def solve(parts, basis, token_total):
    heads, dim, rank = basis.shape
    vmem = pl.BlockSpec(memory_space=pltpu.VMEM)
    return pl.pallas_call(
        functools.partial(solve_kernel, 1.0 / token_total, len(parts), parts[0].ndim == 2),
        out_shape=jax.ShapeDtypeStruct((heads, dim, rank), jnp.float32),
        in_specs=[vmem] * (len(parts) + 1),
        out_specs=vmem,
        cost_estimate=pl.CostEstimate(flops=heads * dim**3, bytes_accessed=4 * heads * dim * dim, transcendentals=0),
    )(*parts, basis)


ALL_PIECES = [(d, k) for d in (1, 2, 3) for k in range(4)]
EARLY_PIECES = [(1, 0), (1, 1), (1, 2), (1, 3), (2, 0), (2, 2), (3, 0), (3, 2)]


def project_kernel(near, widths, last, *refs):
    refs = list(refs)
    x_own, xs = refs.pop(0), [refs.pop(0) for _ in widths]
    own, sib = refs.pop(0), refs.pop(0)
    pieces = {name: refs.pop(0) for name in (ALL_PIECES if last else EARLY_PIECES)}
    if last:
        acc_in, out_ref, xbuf, wbuf, xsem, wsem, acc, asem = refs
    else:
        acc, xbuf, wbuf, xsem, wsem = refs
    g, s, h, c = (lax.axis_index(a) for a in ("groups", "seq", "head", "sub"))
    block = own.shape[0]
    half = block // 2
    blocks = 2 * near
    far_early = sum(widths) - (widths[-1] if last else 0)

    def x_copy(src, at):
        lanes = pl.ds(pl.multiple_of(at * block, block), block)
        return pltpu.make_async_copy(src, xbuf.at[:, lanes], xsem.at[at])

    def w_copy(src, at, part):
        row = pl.multiple_of(at * block + part * half, half)
        return pltpu.make_async_copy(src, wbuf.at[pl.ds(row, half)], wsem.at[at * 2 + part])

    def needed(at, part):
        dist = (at // 2) ^ s
        kind = jnp.where(at % 2 == c, 0, 2) + jnp.where(part == g, 0, 1)
        have = dist == 0
        for d, k in EARLY_PIECES:
            have = have | ((dist == d) & (kind == k))
        fresh = (at // near == h) | (at - (1 - h) * near < far_early)
        return (have & fresh) != last

    if last:
        pltpu.make_async_copy(acc_in, acc, asem).start()
    else:
        acc[...] = jnp.zeros_like(acc)
    for part in range(2):
        for core, src in ((c, own), (1 - c, sib)):

            @pl.when(needed(s * 2 + core, part))
            def _():
                w_copy(src.at[pl.ds(part * half, half)], s * 2 + core, part).start()

    for i in range(near):
        x_copy(x_own.at[:, i * block : (i + 1) * block], h * near + i).start()
    at = (1 - h) * near
    for x_far, width in zip(xs, widths):
        for i in range(width):
            x_copy(x_far.at[:, i * block : (i + 1) * block], at).start()
            at = at + 1
    for (d, k), src in pieces.items():
        core = c if k < 2 else 1 - c
        part = g if k % 2 == 0 else 1 - g

        @pl.when(needed((s ^ d) * 2 + core, part))
        def _():
            w_copy(src, (s ^ d) * 2 + core, part).start()

    if last:
        pltpu.make_async_copy(acc_in, acc, asem).wait()

    @pl.loop(0, blocks)
    def _(n):
        at = lax.rem(n + h * near, blocks)

        @pl.when((n < near) | (n - near < sum(widths)))
        def _():
            x_copy(x_own.at[:, :block], at).wait()

        @pl.loop(0, 2)
        def _(part):
            @pl.when(needed(at, part))
            def _():
                w_copy(own.at[pl.ds(0, half)], at, part).wait()
                off = pl.multiple_of(at * block + part * half, half)
                acc[...] += jnp.dot(
                    xbuf[:, pl.ds(off, half)],
                    wbuf[pl.ds(off, half), :],
                    preferred_element_type=jnp.float32,
                )

    if last:
        out_ref[...] = acc[...].astype(out_ref.dtype)


def project(x, xs, own, sib, pieces, acc=None):
    last = acc is not None
    tokens, feats = x.shape
    block, width = own.shape
    near = feats // block
    widths = [v.shape[1] // block for v in xs]
    given = [pieces[name] for name in (ALL_PIECES if last else EARLY_PIECES)]
    anywhere = pl.BlockSpec(memory_space=pl.ANY)
    args = [x, *xs, own, sib, *given] + ([acc] if last else [])
    scratch = [
        pltpu.VMEM((tokens, 2 * feats), x.dtype),
        pltpu.VMEM((2 * feats, width), x.dtype),
        pltpu.SemaphoreType.DMA((2 * near,)),
        pltpu.SemaphoreType.DMA((4 * near,)),
    ]
    if last:
        scratch += [pltpu.VMEM((tokens, width), jnp.float32), pltpu.SemaphoreType.DMA]
    return pl.pallas_call(
        functools.partial(project_kernel, near, widths, last),
        out_shape=jax.ShapeDtypeStruct((tokens, width), jnp.bfloat16 if last else jnp.float32),
        in_specs=[anywhere] * len(args),
        out_specs=pl.BlockSpec(memory_space=pltpu.VMEM),
        scratch_shapes=scratch,
        compiler_params=pltpu.CompilerParams(vmem_limit_bytes=56 << 20),
        cost_estimate=pl.CostEstimate(
            flops=2 * tokens * feats * width, bytes_accessed=16 << 20, transcendentals=0
        ),
    )(*args)


def gathered_projection(x, own, wanted):
    g, s = lax.axis_index("groups"), lax.axis_index("seq")
    inner = (s == 1) | (s == 2)
    block = own.shape[0]
    tie = lax.optimization_barrier

    def sub(value):
        return lax.ppermute(value, "sub", SWAP)

    def across(value):
        return lax.ppermute(value, "groups", SWAP)

    def along(value, *pairs):
        return lax.ppermute(value, "seq", pairs)

    def far(value):
        return lax.ppermute(value, "head", SWAP)

    unit = lax.dynamic_slice_in_dim(own, g * (block // 2), block // 2, axis=0)
    x0, x1 = far(x[:, :block]), far(x[:, block : 2 * block])
    one = along(unit, (0, 1), (1, 0), (2, 3), (3, 2))
    mid = along(unit, (1, 2), (2, 1))
    one, mid, x0, x_rest, own_later = tie((one, mid, x0, x[:, 2 * block :], own))
    mid_two = along(one, (1, 2), (2, 1))
    out_two = along(mid, (1, 0), (2, 3))
    moved = {(1, 0): one, (1, 1): across(one), (1, 2): sub(one)}
    x2 = far(x_rest)
    mid_two, out_two, x1, moved[1, 1], own_later = tie(
        (mid_two, out_two, x1, moved[1, 1], own_later)
    )
    two = jnp.where(inner, mid_two, out_two)
    out_three = along(mid_two, (1, 0), (2, 3))
    moved.update({(2, 0): two, (2, 1): across(two), (2, 2): sub(two), (1, 3): sub(moved[1, 1])})
    sib = sub(own_later)
    out_three, moved[2, 2], moved[1, 3], sib, wanted = tie(
        (out_three, moved[2, 2], moved[1, 3], sib, wanted)
    )
    three = jnp.where(inner, mid, out_three)
    moved.update({(3, 0): three, (3, 1): across(three), (3, 2): sub(three), (2, 3): sub(moved[2, 1])})
    lists = jnp.stack([wanted] + [lax.ppermute(wanted, "seq", xor(4, d)) for d in (1, 2, 3)])
    twin_lists = sub(lists)
    acc = project(x, [x0, x1], own, sib, moved)
    moved[3, 3] = sub(moved[3, 1])
    return project(x, [x0, x1, x2], own, sib, moved, acc), lists, twin_lists


def plain_projection(x, own):
    head = lax.axis_size("head")
    feats = x.shape[1]
    weights = lax.all_gather(own, ("seq", "sub"), axis=0, tiled=True)
    sums = None
    for d in range(head):
        rows = x if d == 0 else lax.ppermute(x, "head", rotation(head, -d))
        at = lax.rem(lax.axis_index("head") + d, head) * feats
        term = jnp.dot(
            rows,
            lax.dynamic_slice_in_dim(weights, at, feats, axis=0),
            preferred_element_type=jnp.float32,
        )
        sums = term if sums is None else sums + term
    return sums.astype(jnp.bfloat16)


def spread(order, tokens, share, slot):
    place = lax.iota(jnp.int32, tokens)
    block = slot // tokens
    before = (block[None, :] == block[:, None]) & (place[None, :] < place[:, None])
    position = order(block) * share + jnp.sum(before.astype(jnp.int32), axis=1)
    hits = position[:, None] == place[None, :]
    wanted = jnp.sum(jnp.where(hits, (slot - block * tokens)[:, None], 0), axis=0)
    return hits.astype(jnp.bfloat16), wanted


def selected(asked, rows):
    pick = (asked[:, None] == lax.iota(jnp.int32, rows.shape[0])[None, :]).astype(jnp.bfloat16)
    return jnp.dot(pick, rows, preferred_element_type=jnp.float32).astype(jnp.bfloat16)


def local_moments(both, heads, dim):
    keys = both[:, : heads * dim].reshape(both.shape[0], heads, dim)
    return jnp.einsum("thi,thj->hij", keys, keys, preferred_element_type=jnp.float32)


def core_split(values, c):
    keep = lax.dynamic_index_in_dim(values, c, 0, keepdims=False)
    give = lax.dynamic_index_in_dim(values, 1 - c, 0, keepdims=False)
    return keep + lax.ppermute(give, "sub", SWAP)


def per_device(hidden_states, key_w, value_w, basis, slot):
    tokens = hidden_states.shape[0]
    seq, head, cores = lax.axis_size("seq"), lax.axis_size("head"), lax.axis_size("sub")
    s, c = lax.axis_index("seq"), lax.axis_index("sub")
    peers = seq * cores
    share = tokens // peers
    heads, dim, rank = basis.shape
    mine = heads // cores
    width = heads * dim
    own = jnp.concatenate([key_w, value_w], axis=1)
    basis_here = lax.dynamic_slice_in_dim(basis, c * mine, mine, axis=0)

    if seq == 4 and head == 2 and lax.axis_size("groups") == 2 and mine == 2:
        unpick, wanted = spread(lambda b: b ^ (s * cores + c), tokens, share, slot)
        both, lists, twin_lists = gathered_projection(hidden_states, own, wanted)
        packed = pack(local_moments(both, heads, dim).reshape(cores, mine, dim, dim))
        chip = core_split(packed, c)
        parts = [chip] + [lax.ppermute(chip, "seq", xor(seq, d)) for d in (1, 2, 3)]
        near = [lists[d, 2 * d * share : (2 * d + 1) * share] for d in range(seq)]
        twin = [twin_lists[d, (2 * d + 1) * share : (2 * d + 2) * share] for d in range(seq)]
        give = selected(jnp.concatenate(twin), both)
        keep = selected(jnp.concatenate(near), both)
        taken = lax.ppermute(give, "sub", SWAP)
        pairs = jnp.stack(
            [v.reshape(seq, share, 2 * width) for v in (keep, taken)], axis=1
        ).reshape(seq, cores * share, 2 * width)
        got = jnp.concatenate(
            [pairs[0]] + [lax.ppermute(pairs[d], "seq", xor(seq, d)) for d in (1, 2, 3)]
        )
    else:
        unpick, wanted = spread(lambda b: b, tokens, share, slot)
        asked = lax.all_to_all(wanted, ("seq", "sub"), split_axis=0, concat_axis=0, tiled=True)
        both = plain_projection(hidden_states, own)
        chip = core_split(local_moments(both, heads, dim).reshape(cores, mine, dim, dim), c)
        parts = [lax.psum(chip, "seq")]
        got = lax.all_to_all(
            selected(asked, both), ("seq", "sub"), split_axis=0, concat_axis=0, tiled=True
        )

    solved = solve(parts, basis_here, tokens * peers)
    other = lax.ppermute(solved, "sub", SWAP)
    maps = jnp.where(c == 0, jnp.concatenate([solved, other]), jnp.concatenate([other, solved]))
    rows = jnp.dot(unpick, got, preferred_element_type=jnp.float32).astype(jnp.bfloat16)
    coeffs = jnp.einsum(
        "thd,hdr->thr",
        rows[:, :width].astype(jnp.float32).reshape(tokens, heads, dim),
        maps,
        precision=lax.Precision.HIGHEST,
    )
    return coeffs.reshape(tokens, heads * rank).astype(jnp.bfloat16), rows[:, width:]


def solution(mesh):
    return jax.shard_map(
        per_device,
        mesh=mesh,
        in_specs=(
            P(("groups", "seq", "sub"), "head"),
            P(("seq", "sub"), "head"),
            P(("seq", "sub"), "head"),
            P("head", None, None),
            P(("groups", "seq", "sub")),
        ),
        out_specs=(P(("groups", "seq", "sub"), "head"), P(("groups", "seq", "sub"), "head")),
        check_vma=False,
    )
```

time: 246 us -> 209 us (0.85)
  waiting for transfers between devices: 172 us -> 99.2 us
  starting transfers between devices: 17.8 us -> 45.9 us
  Pallas kernels: 13.1 us -> 40.1 us
  matrix products: 18.6 us -> 5.27 us
  between operations: 14.2 us -> 1.01 us
  local copies, waits for them, and re-layouts: 5.49 us -> 12.2 us
    all_gather x1 -> x0, waiting for transfers between devices: 138 us -> none  [per_device(): lax.all_gather(jnp.concatenate([key_w, value_w], axis=1), ('seq', 'sub'),...]
    ppermute x5 -> x30, waiting for transfers between devices: 30.7 us -> 99.2 us  [the longest x5 36.1 us: along(): return lax.ppermute(value, 'seq', pairs)]
    ppermute x5 -> x30, starting transfers between devices: 4.38 us -> 44.4 us  [the longest x5 11.7 us: along(): return lax.ppermute(value, 'seq', pairs)]
    pallas_call x0 -> x2, Pallas kernels: none -> 27.1 us  [project(): pl.pallas_call(functools.partial(project_kernel, near, widths, last), out...]
    dot_general x4 -> x3, matrix products: 17.1 us -> 3.82 us  [the longest x2 2.19 us: selected(): jnp.dot(pick, rows, preferred_element_type=jnp.float32).astype(jnp.bfloat16)]
    all_to_all x2 -> x0, starting transfers between devices: 12.6 us -> none  [the longest x1 6.64 us: per_device(): lax.all_to_all(sent, ('seq', 'sub'), split_axis=0, concat_axis=0, tiled=T...]
    unnamed x18 -> x49, local copies, waits for them, and re-layouts: 3.29 us -> 7.77 us
    all_to_all x2 -> x0, waiting for transfers between devices: 3.71 us -> none  [the longest x1 3.7 us: per_device(): lax.all_to_all(wanted, ('seq', 'sub'), split_axis=0, concat_axis=0, tiled...]
  transfers between devices with their start and end apart: 9 -> 31, of which waited for: 6 -> 14; matrix products, arithmetic and copies ran while one was open for 5% -> 5% of each run, Pallas kernels for 5% -> 13%
where the time goes in v2:
time: 209 us; the launch traced here: 207 us
  waiting for transfers between devices  99.2 us (47%)
  starting transfers between devices  45.9 us (22%)
  Pallas kernels  40.1 us (19%)
  local copies, waits for them, and re-layouts  12.2 us (6%)
  matrix products  5.27 us (3%)
  other arithmetic  3.6 us (2%)
    ppermute x5, waiting for transfers between devices, along(): return lax.ppermute(value, 'seq', pairs)  36.1 us
    pallas_call x2, Pallas kernels, project(): pl.pallas_call(functools.partial(project_kernel, near, widths, last), out...  27.1 us
    ppermute x3, waiting for transfers between devices, far(): return lax.ppermute(value, 'head', SWAP)  25.5 us
    ppermute x3, waiting for transfers between devices, per_device(): parts = [chip] + [lax.ppermute(chip, 'seq', xor(seq, d)) for d in (1, 2, 3)]  21.4 us
    ppermute x3, waiting for transfers between devices, across(): return lax.ppermute(value, 'groups', SWAP)  13.1 us
    pallas_call x1, Pallas kernels, solve(): pl.pallas_call(functools.partial(solve_kernel, 1.0 / token_total, len(par...  13 us
    ppermute x5, starting transfers between devices, along(): return lax.ppermute(value, 'seq', pairs)  11.7 us
    ppermute x8, starting transfers between devices, sub(): return lax.ppermute(value, 'sub', SWAP)  11.1 us
  transfers between devices with their start and end apart: 31, of which 14 were waited for; matrix products, arithmetic and copies ran while one was open for 5% of the time, Pallas kernels for 13%

profile of v2, /device:TPU:11, one launch (start us, length us, event | category | flops | bytes accessed | tf_op | source)
XLA Modules:
  0.0 207.3 jit_solution(4986891805017845251)
XLA Ops:
  0.7 1.5 constant_dynamic-update-slice_fusion.1
  2.2 0.1 constant_dynamic-update-slice_fusion.refs_3_.refs_4_
  2.5 0.2 collective-permute-start
  2.7 4.5 %collective-permute-start.1 = (bf16[512,1024]{1,0:T(8,128)(2,1)S(1)}, bf16[512,1024]{1,0:T(8,128)(2,1)S(1)}, u32[]{:S(2)}, u32[]{:S(2)}) collective-permute-start(bf16[512,1024]{1,0:T(8,128)(2,1)S(1)} %constant_dynamic-slice_fusion.1), channel_id=1, source_target_pairs={{4,8},{8,4},{5,9},{9,5},{6,10},{10,6},{7,11},{11,7},{20,24},{24,20... | collective-permute-start | bytes 3145736 | tf_op jit(solution)/shard_map/ppermute | solution.py:234
  7.2 1.7 fusion.35
  8.9 0.3 collective-permute-start.2
  9.2 1.2 collective-permute-start.5
  10.4 1.5 slice.65
  11.9 14.6 %collective-permute-done.refs_5_.refs_6_ = bf16[512,1024]{1,0:T(8,128)(2,1)S(1)} collective-permute-done((bf16[512,1024]{1,0:T(8,128)(2,1)S(1)}, bf16[512,1024]{1,0:T(8,128)(2,1)S(1)}, u32[]{:S(2)}, u32[]{:S(2)}) %collective-permute-start) | collective-permute-done | bytes 1048608 | tf_op jit(solution)/shard_map/ppermute | solution.py:234
  26.6 3.1 %collective-permute-done.1 = bf16[512,1024]{1,0:T(8,128)(2,1)S(1)} collective-permute-done((bf16[512,1024]{1,0:T(8,128)(2,1)S(1)}, bf16[512,1024]{1,0:T(8,128)(2,1)S(1)}, u32[]{:S(2)}, u32[]{:S(2)}) %collective-permute-start.1) | collective-permute-done | bytes 1048608 | tf_op jit(solution)/shard_map/ppermute | solution.py:234
  29.7 2.7 %collective-permute-done.2.refs_1_ = bf16[512,1024]{1,0:T(8,128)(2,1)S(1)} collective-permute-done((bf16[512,1024]{1,0:T(8,128)(2,1)S(1)}, bf16[512,1024]{1,0:T(8,128)(2,1)S(1)}, u32[]{:S(2)}, u32[]{:S(2)}) %collective-permute-start.2) | collective-permute-done | bytes 1048608 | tf_op jit(solution)/shard_map/ppermute | solution.py:237
  32.4 2.2 %collective-permute-start.3 = (bf16[512,1024]{1,0:T(8,128)(2,1)S(1)}, bf16[512,1024]{1,0:T(8,128)(2,1)}, u32[]{:S(2)}, u32[]{:S(2)}) collective-permute-start(bf16[512,1024]{1,0:T(8,128)(2,1)S(1)} %collective-permute-done.refs_5_.refs_6_), channel_id=1, source_target_pairs={{4,8},{8,4},{5,9},{9,5},{6,10},{10,6},{7,11},{11,7},{20,24},{24,20... | collective-permute-start | bytes 3145736 | tf_op jit(solution)/shard_map/ppermute | solution.py:234
  34.6 1.4 collective-permute-start.4
  36.0 1.3 collective-permute-start.6
  37.3 17.7 %collective-permute-done.5.refs_2_ = bf16[512,1024]{1,0:T(8,128)(2,1)S(1)} collective-permute-done((bf16[512,1024]{1,0:T(8,128)(2,1)S(1)}, bf16[512,1024]{1,0:T(8,128)(2,1)S(1)}, u32[]{:S(2)}, u32[]{:S(2)}) %collective-permute-start.5) | collective-permute-done | bytes 1048608 | tf_op jit(solution)/shard_map/ppermute | solution.py:237
  55.0 0.2 collective-permute-done.3
  55.1 2.0 collective-permute-done.6.refs_6_.refs_7_
  57.2 4.6 %collective-permute-start.11 = (bf16[1024,1024]{1,0:T(8,128)(2,1)S(1)}, bf16[1024,1024]{1,0:T(8,128)(2,1)}, u32[]{:S(2)}, u32[]{:S(2)}) collective-permute-start(bf16[1024,1024]{1,0:T(8,128)(2,1)S(1)} %constant_dynamic-update-slice_fusion.refs_3_.refs_4_), channel_id=1, source_target_pairs={{0,1},{1,0},{2,3},{3,2},{4,5},{5,4},{6,7},{7,6},{8,9},{9,8},{10,11... | collective-permute-start | bytes 6291464 | tf_op jit(solution)/shard_map/ppermute | solution.py:228
  61.8 3.5 %collective-permute-start.8 = (bf16[512,1024]{1,0:T(8,128)(2,1)}, bf16[512,1024]{1,0:T(8,128)(2,1)}, u32[]{:S(2)}, u32[]{:S(2)}) collective-permute-start(bf16[512,1024]{1,0:T(8,128)(2,1)} %collective-permute-done.3), channel_id=1, source_target_pairs={{4,0},{8,12},{5,1},{9,13},{6,2},{10,14},{7,3},{11,15},{20,16},{24,... | collective-permute-start | bytes 3145736 | tf_op jit(solution)/shard_map/ppermute | solution.py:234
  65.3 1.3 broadcast_select_fusion.1.refs_9_.refs_10_
  66.6 0.3 collective-permute-start.9
  67.0 0.2 collective-permute-start.10
  67.2 0.2 convert_reduce_fusion
  67.5 0.2 select_reduce_fusion
  67.7 1.3 collective-permute-start.13
  69.0 18.2 %collective-permute-done.8 = bf16[512,1024]{1,0:T(8,128)(2,1)} collective-permute-done((bf16[512,1024]{1,0:T(8,128)(2,1)}, bf16[512,1024]{1,0:T(8,128)(2,1)}, u32[]{:S(2)}, u32[]{:S(2)}) %collective-permute-start.8) | collective-permute-done | bytes 1048608 | tf_op jit(solution)/shard_map/ppermute | solution.py:234
  87.2 1.4 broadcast_select_fusion.refs_11_.refs_14_
  88.7 1.3 collective-permute-start.15
  90.0 0.3 collective-permute-start.7
  90.2 1.2 collective-permute-start.25
  91.4 3.2 %collective-permute-start.24 = (s32[512]{0:T(512)S(1)}, s32[512]{0:T(512)S(1)}, u32[]{:S(2)}, u32[]{:S(2)}) collective-permute-start(s32[512]{0:T(512)S(1)} %select_reduce_fusion), channel_id=1, source_target_pairs={{0,8},{4,12},{8,0},{12,4},{1,9},{5,13},{9,1},{13,5},{2,10},{6,14},... | collective-permute-start | bytes 6152 | tf_op jit(solution)/shard_map/ppermute | solution.py:260
  94.6 2.1 collective-permute-start.23
  96.7 2.8 %collective-permute-start.12 = (bf16[512,1024]{1,0:T(8,128)(2,1)S(1)}, bf16[512,1024]{1,0:T(8,128)(2,1)S(1)}, u32[]{:S(2)}, u32[]{:S(2)}) collective-permute-start(bf16[512,1024]{1,0:T(8,128)(2,1)S(1)} %copy-done.7), channel_id=1, source_target_pairs={{0,1},{1,0},{2,3},{3,2},{4,5},{5,4},{6,7},{7,6},{8,9},{9,8},{10,11... | collective-permute-start | bytes 3145736 | tf_op jit(solution)/shard_map/ppermute | solution.py:228
  99.5 1.5 collective-permute-start.16
  101.1 2.2 %collective-permute-done.26 = s32[4,512]{1,0:T(4,128)S(1)} collective-permute-done((s32[4,512]{1,0:T(4,128)S(1)}, s32[4,512]{1,0:T(4,128)S(1)}, u32[]{:S(2)}, u32[]{:S(2)}) %collective-permute-start.26) | collective-permute-done | bytes 8224 | tf_op jit(solution)/shard_map/ppermute | solution.py:228
  103.3 0.4 collective-permute-start.14
  103.7 11.1 %collective-permute-done.15.refs_15_ = bf16[512,1024]{1,0:T(8,128)(2,1)} collective-permute-done((bf16[512,1024]{1,0:T(8,128)(2,1)S(1)}, bf16[512,1024]{1,0:T(8,128)(2,1)}, u32[]{:S(2)}, u32[]{:S(2)}) %collective-permute-start.15) | collective-permute-done | bytes 1048608 | tf_op jit(solution)/shard_map/ppermute | solution.py:231
  114.8 1.1 collective-permute-start.17
  116.2 0.9 copy-done.10
  117.1 1.0 copy-done.11
  118.1 13.1 %shard_map.68.refs_18_ = f32[512,1024]{1,0:T(8,128)} custom-call(bf16[512,4096]{1,0:T(8,128)(2,1)} %refs_0_.3, bf16[512,1024]{1,0:T(8,128)(2,1)} %copy-done.8, bf16[512,1024]{1,0:T(8,128)(2,1)} %copy-done.9, bf16[1024,1024]{1,0:T(8,128)(2,1)} %copy-done.2, bf16[1024,1024]{1,0:T(8,128)(2,1)} %collective-permute-done.11.refs_4_.refs_5_, ...), custom_call_target="tpu_custom_call" | custom-call | flops 4294967296 | bytes 16777216 | tf_op jit(solution)/shard_map/pallas_call | solution.py:208
  131.3 5.1 %collective-permute-done.7.refs_3_ = bf16[512,2048]{1,0:T(8,128)(2,1)} collective-permute-done((bf16[512,2048]{1,0:T(8,128)(2,1)}, bf16[512,2048]{1,0:T(8,128)(2,1)}, u32[]{:S(2)}, u32[]{:S(2)}) %collective-permute-start.7) | collective-permute-done | bytes 2097184 | tf_op jit(solution)/shard_map/ppermute | solution.py:237
  136.4 1.0 copy-done.12
  137.4 1.0 copy-done.13
  138.3 13.9 %shard_map.69 = bf16[512,1024]{1,0:T(8,128)(2,1)} custom-call(bf16[512,4096]{1,0:T(8,128)(2,1)} %refs_0_.3, bf16[512,1024]{1,0:T(8,128)(2,1)} %copy-done.8, bf16[512,1024]{1,0:T(8,128)(2,1)} %copy-done.9, bf16[512,2048]{1,0:T(8,128)(2,1)} %collective-permute-done.7.refs_3_, bf16[1024,1024]{1,0:T(8,128)(2,1)} %copy-done.2, ...), custom_call_target="tpu_custom_call" | custom-call | flops 4294967296 | bytes 16777216 | tf_op jit(solution)/shard_map/pallas_call | solution.py:208
  152.3 1.6 fusion.10
  153.9 1.7 convolution_convert_fusion.1
  155.7 1.5 collective-permute-start.27
  157.3 0.5 convolution_convert_fusion.2
  157.8 0.9 collective-permute-done.27
  158.9 4.3 %collective-permute-start.29 = (bf16[128,1024]{1,0:T(8,128)(2,1)S(1)}, bf16[128,1024]{1,0:T(8,128)(2,1)S(1)}, u32[]{:S(2)}, u32[]{:S(2)}) collective-permute-start(bf16[128,1024]{1,0:T(8,128)(2,1)S(1)} %bitcast.70), channel_id=1, source_target_pairs={{0,8},{4,12},{8,0},{12,4},{1,9},{5,13},{9,1},{13,5},{2,10},{6,14},... | collective-permute-start | bytes 786440 | tf_op jit(solution)/shard_map/ppermute | solution.py:337
  163.2 1.5 collective-permute-start.19
  164.7 15.5 %collective-permute-done.19.refs_1_ = f32[136,128]{1,0:T(8,128)S(1)} collective-permute-done((f32[136,128]{1,0:T(8,128)S(1)}, f32[136,128]{1,0:T(8,128)S(1)}, u32[]{:S(2)}, u32[]{:S(2)}) %collective-permute-start.19) | collective-permute-done | bytes 69664 | tf_op jit(solution)/shard_map/ppermute | solution.py:327
  180.3 2.1 collective-permute-start.21
  182.3 0.8 copy.26.refs_4_
  183.1 2.0 collective-permute-done.20.refs_2_
  185.1 3.8 %collective-permute-done.21.refs_3_ = f32[136,128]{1,0:T(8,128)S(1)} collective-permute-done((f32[136,128]{1,0:T(8,128)S(1)}, f32[136,128]{1,0:T(8,128)S(1)}, u32[]{:S(2)}, u32[]{:S(2)}) %collective-permute-start.21) | collective-permute-done | bytes 69664 | tf_op jit(solution)/shard_map/ppermute | solution.py:327
  189.0 0.6 copy-done.21
  189.6 13.0 %shard_map.70 = f32[2,128,64]{2,1,0:T(8,128)} custom-call(f32[136,128]{1,0:T(8,128)} %copy-done.17, f32[136,128]{1,0:T(8,128)} %copy-done.19, f32[136,128]{1,0:T(8,128)} %copy-done.20, f32[136,128]{1,0:T(8,128)} %copy-done.21, f32[2,128,64]{2,1,0:T(8,128)} %copy.26.refs_4_), custom_call_target="tpu_custom_call" | custom-call | flops 4194304 | bytes 131072 | tf_op jit(solution)/shard_map/pallas_call | solution.py:93
  202.6 1.5 collective-permute-start.22
  204.1 0.8 convolution_convert_fusion
  204.9 0.9 fusion.36
  205.8 0.7 convolution_convert_fusion.3
  206.5 0.8 copy.22
  (81 shorter events, 1.0 us)
Async XLA Ops:
  0.6 181.7 %copy-start = (f32[4,128,64]{1,2,0:T(8,128)S(1)}, f32[4,128,64]{1,2,0:T(8,128)}, u32[]{:S(2)}) copy-start(f32[4,128,64]{1,2,0:T(8,128)} %param.8) | copy-start | bytes 393220
  0.6 1.6 copy-start.14
  2.4 54.8 %copy-start.2 = (bf16[1024,1024]{1,0:T(8,128)(2,1)}, bf16[1024,1024]{1,0:T(8,128)(2,1)S(1)}, u32[]{:S(2)}) copy-start(bf16[1024,1024]{1,0:T(8,128)(2,1)S(1)} %constant_dynamic-update-slice_fusion.refs_3_.refs_4_) | copy-start | bytes 6291460
  2.5 8.0 %copy-start.1 = (bf16[512,4096]{1,0:T(8,128)(2,1)S(1)}, bf16[512,4096]{1,0:T(8,128)(2,1)}, u32[]{:S(2)}) copy-start(bf16[512,4096]{1,0:T(8,128)(2,1)} %refs_0_.3) | copy-start | bytes 12582916
  2.5 24.1 %collective-permute-start = (bf16[512,1024]{1,0:T(8,128)(2,1)S(1)}, bf16[512,1024]{1,0:T(8,128)(2,1)S(1)}, u32[]{:S(2)}, u32[]{:S(2)}) collective-permute-start(bf16[512,1024]{1,0:T(8,128)(2,1)S(1)} %constant_dynamic-slice_fusion.1), channel_id=1, source_target_pairs={{0,4},{4,0},{8,12},{12,8},{1,5},{5,1},{9,13},{13,9},{2,6},{6,2},{1... | collective-permute-start | bytes 3145736 | tf_op jit(solution)/shard_map/ppermute | solution.py:234
  2.7 27.0 %collective-permute-start.1 = (bf16[512,1024]{1,0:T(8,128)(2,1)S(1)}, bf16[512,1024]{1,0:T(8,128)(2,1)S(1)}, u32[]{:S(2)}, u32[]{:S(2)}) collective-permute-start(bf16[512,1024]{1,0:T(8,128)(2,1)S(1)} %constant_dynamic-slice_fusion.1), channel_id=1, source_target_pairs={{4,8},{8,4},{5,9},{9,5},{6,10},{10,6},{7,11},{11,7},{20,24},{24,20... | collective-permute-start | bytes 3145736 | tf_op jit(solution)/shard_map/ppermute | solution.py:234
  8.9 23.5 %collective-permute-start.2 = (bf16[512,1024]{1,0:T(8,128)(2,1)S(1)}, bf16[512,1024]{1,0:T(8,128)(2,1)S(1)}, u32[]{:S(2)}, u32[]{:S(2)}) collective-permute-start(bf16[512,1024]{1,0:T(8,128)(2,1)S(1)} %get-tuple-element.39), channel_id=1, source_target_pairs={{0,2},{2,0},{1,3},{3,1},{4,6},{6,4},{5,7},{7,5},{8,10},{10,8},{9,1... | collective-permute-start | bytes 3145736 | tf_op jit(solution)/shard_map/ppermute | solution.py:237
  9.2 45.7 %collective-permute-start.5 = (bf16[512,1024]{1,0:T(8,128)(2,1)S(1)}, bf16[512,1024]{1,0:T(8,128)(2,1)S(1)}, u32[]{:S(2)}, u32[]{:S(2)}) collective-permute-start(bf16[512,1024]{1,0:T(8,128)(2,1)S(1)} %get-tuple-element.38), channel_id=1, source_target_pairs={{0,2},{2,0},{1,3},{3,1},{4,6},{6,4},{5,7},{7,5},{8,10},{10,8},{9,1... | collective-permute-start | bytes 3145736 | tf_op jit(solution)/shard_map/ppermute | solution.py:237
  11.9 55.3 %copy-start.22 = (s32[512]{0:T(512)S(1)}, s32[512]{0:T(512)}, u32[]{:S(2)}) copy-start(s32[512]{0:T(512)} %param.9) | copy-start | bytes 6148
  26.6 28.6 %copy-start.6 = (bf16[512,1024]{1,0:T(8,128)(2,1)}, bf16[512,1024]{1,0:T(8,128)(2,1)S(1)}, u32[]{:S(2)}) copy-start(bf16[512,1024]{1,0:T(8,128)(2,1)S(1)} %collective-permute-done.refs_5_.refs_6_) | copy-start | bytes 3145732
  29.7 27.4 %copy-start.15 = (bf16[512,1024]{1,0:T(8,128)(2,1)}, bf16[512,1024]{1,0:T(8,128)(2,1)S(1)}, u32[]{:S(2)}) copy-start(bf16[512,1024]{1,0:T(8,128)(2,1)S(1)} %collective-permute-done.1) | copy-start | bytes 3145732
  32.4 24.8 %copy-start.8 = (bf16[512,1024]{1,0:T(8,128)(2,1)}, bf16[512,1024]{1,0:T(8,128)(2,1)S(1)}, u32[]{:S(2)}) copy-start(bf16[512,1024]{1,0:T(8,128)(2,1)S(1)} %collective-permute-done.2.refs_1_) | copy-start | bytes 3145732
  32.4 22.7 %collective-permute-start.3 = (bf16[512,1024]{1,0:T(8,128)(2,1)S(1)}, bf16[512,1024]{1,0:T(8,128)(2,1)}, u32[]{:S(2)}, u32[]{:S(2)}) collective-permute-start(bf16[512,1024]{1,0:T(8,128)(2,1)S(1)} %collective-permute-done.refs_5_.refs_6_), channel_id=1, source_target_pairs={{4,8},{8,4},{5,9},{9,5},{6,10},{10,6},{7,11},{11,7},{20,24},{24,20... | collective-permute-start | bytes 3145736 | tf_op jit(solution)/shard_map/ppermute | solution.py:234
  34.6 20.5 %collective-permute-start.4 = (bf16[512,1024]{1,0:T(8,128)(2,1)S(1)}, bf16[512,1024]{1,0:T(8,128)(2,1)S(1)}, u32[]{:S(2)}, u32[]{:S(2)}) collective-permute-start(bf16[512,1024]{1,0:T(8,128)(2,1)S(1)} %collective-permute-done.1), channel_id=1, source_target_pairs={{4,0},{8,12},{5,1},{9,13},{6,2},{10,14},{7,3},{11,15},{20,16},{24,... | collective-permute-start | bytes 3145736 | tf_op jit(solution)/shard_map/ppermute | solution.py:234
  36.0 21.2 %collective-permute-start.6 = (bf16[512,1024]{1,0:T(8,128)(2,1)S(1)}, bf16[512,1024]{1,0:T(8,128)(2,1)}, u32[]{:S(2)}, u32[]{:S(2)}) collective-permute-start(bf16[512,1024]{1,0:T(8,128)(2,1)S(1)} %collective-permute-done.refs_5_.refs_6_), channel_id=1, source_target_pairs={{0,16},{16,0},{1,17},{17,1},{2,18},{18,2},{3,19},{19,3},{4,20},{20... | collective-permute-start | bytes 3145736 | tf_op jit(solution)/shard_map/ppermute | solution.py:231
  55.0 2.2 %copy-start.9 = (bf16[512,1024]{1,0:T(8,128)(2,1)}, bf16[512,1024]{1,0:T(8,128)(2,1)S(1)}, u32[]{:S(2)}) copy-start(bf16[512,1024]{1,0:T(8,128)(2,1)S(1)} %collective-permute-done.5.refs_2_) | copy-start | bytes 3145732
  55.1 2.0 copy-start.16
  57.2 30.0 %collective-permute-start.11 = (bf16[1024,1024]{1,0:T(8,128)(2,1)S(1)}, bf16[1024,1024]{1,0:T(8,128)(2,1)}, u32[]{:S(2)}, u32[]{:S(2)}) collective-permute-start(bf16[1024,1024]{1,0:T(8,128)(2,1)S(1)} %constant_dynamic-update-slice_fusion.refs_3_.refs_4_), channel_id=1, source_target_pairs={{0,1},{1,0},{2,3},{3,2},{4,5},{5,4},{6,7},{7,6},{8,9},{9,8},{10,11... | collective-permute-start | bytes 6291464 | tf_op jit(solution)/shard_map/ppermute | solution.py:228
  61.8 25.4 %collective-permute-start.8 = (bf16[512,1024]{1,0:T(8,128)(2,1)}, bf16[512,1024]{1,0:T(8,128)(2,1)}, u32[]{:S(2)}, u32[]{:S(2)}) collective-permute-start(bf16[512,1024]{1,0:T(8,128)(2,1)} %collective-permute-done.3), channel_id=1, source_target_pairs={{4,0},{8,12},{5,1},{9,13},{6,2},{10,14},{7,3},{11,15},{20,16},{24,... | collective-permute-start | bytes 3145736 | tf_op jit(solution)/shard_map/ppermute | solution.py:234
  66.6 49.5 %copy-start.3 = (bf16[512,1024]{1,0:T(8,128)(2,1)}, bf16[512,1024]{1,0:T(8,128)(2,1)S(1)}, u32[]{:S(2)}) copy-start(bf16[512,1024]{1,0:T(8,128)(2,1)S(1)} %broadcast_select_fusion.1.refs_9_.refs_10_) | copy-start | bytes 3145732
  66.6 20.6 %collective-permute-start.9 = (bf16[512,1024]{1,0:T(8,128)(2,1)S(1)}, bf16[512,1024]{1,0:T(8,128)(2,1)}, u32[]{:S(2)}, u32[]{:S(2)}) collective-permute-start(bf16[512,1024]{1,0:T(8,128)(2,1)S(1)} %broadcast_select_fusion.1.refs_9_.refs_10_), channel_id=1, source_target_pairs={{0,1},{1,0},{2,3},{3,2},{4,5},{5,4},{6,7},{7,6},{8,9},{9,8},{10,11... | collective-permute-start | bytes 3145736 | tf_op jit(solution)/shard_map/ppermute | solution.py:228
  67.0 20.2 %collective-permute-start.10 = (bf16[512,1024]{1,0:T(8,128)(2,1)}, bf16[512,1024]{1,0:T(8,128)(2,1)}, u32[]{:S(2)}, u32[]{:S(2)}) collective-permute-start(bf16[512,1024]{1,0:T(8,128)(2,1)} %collective-permute-done.6.refs_6_.refs_7_), channel_id=1, source_target_pairs={{0,1},{1,0},{2,3},{3,2},{4,5},{5,4},{6,7},{7,6},{8,9},{9,8},{10,11... | collective-permute-start | bytes 3145736 | tf_op jit(solution)/shard_map/ppermute | solution.py:228
  67.7 33.3 %collective-permute-start.13 = (bf16[512,1024]{1,0:T(8,128)(2,1)S(1)}, bf16[512,1024]{1,0:T(8,128)(2,1)}, u32[]{:S(2)}, u32[]{:S(2)}) collective-permute-start(bf16[512,1024]{1,0:T(8,128)(2,1)S(1)} %broadcast_select_fusion.1.refs_9_.refs_10_), channel_id=1, source_target_pairs={{0,16},{16,0},{1,17},{17,1},{2,18},{18,2},{3,19},{19,3},{4,20},{20... | collective-permute-start | bytes 3145736 | tf_op jit(solution)/shard_map/ppermute | solution.py:231
  87.2 9.5 %copy-start.7 = (bf16[512,1024]{1,0:T(8,128)(2,1)S(1)}, bf16[512,1024]{1,0:T(8,128)(2,1)}, u32[]{:S(2)}) copy-start(bf16[512,1024]{1,0:T(8,128)(2,1)} %copy-done.6) | copy-start | bytes 3145732
  88.7 27.5 %copy-start.4 = (bf16[512,1024]{1,0:T(8,128)(2,1)}, bf16[512,1024]{1,0:T(8,128)(2,1)S(1)}, u32[]{:S(2)}) copy-start(bf16[512,1024]{1,0:T(8,128)(2,1)S(1)} %broadcast_select_fusion.refs_11_.refs_14_) | copy-start | bytes 3145732
  88.7 26.1 %collective-permute-start.15 = (bf16[512,1024]{1,0:T(8,128)(2,1)S(1)}, bf16[512,1024]{1,0:T(8,128)(2,1)}, u32[]{:S(2)}, u32[]{:S(2)}) collective-permute-start(bf16[512,1024]{1,0:T(8,128)(2,1)S(1)} %broadcast_select_fusion.refs_11_.refs_14_), channel_id=1, source_target_pairs={{0,16},{16,0},{1,17},{17,1},{2,18},{18,2},{3,19},{19,3},{4,20},{20... | collective-permute-start | bytes 3145736 | tf_op jit(solution)/shard_map/ppermute | solution.py:231
  90.0 46.4 %collective-permute-start.7 = (bf16[512,2048]{1,0:T(8,128)(2,1)}, bf16[512,2048]{1,0:T(8,128)(2,1)}, u32[]{:S(2)}, u32[]{:S(2)}) collective-permute-start(bf16[512,2048]{1,0:T(8,128)(2,1)} %slice.65), channel_id=1, source_target_pairs={{0,2},{2,0},{1,3},{3,1},{4,6},{6,4},{5,7},{7,5},{8,10},{10,8},{9,1... | collective-permute-start | bytes 6291464 | tf_op jit(solution)/shard_map/ppermute | solution.py:237
  90.2 4.4 %collective-permute-start.25 = (s32[512]{0:T(512)S(1)}, s32[512]{0:T(512)S(1)}, u32[]{:S(2)}, u32[]{:S(2)}) collective-permute-start(s32[512]{0:T(512)S(1)} %select_reduce_fusion), channel_id=1, source_target_pairs={{0,12},{4,8},{8,4},{12,0},{1,13},{5,9},{9,5},{13,1},{2,14},{6,10},... | collective-permute-start | bytes 6152 | tf_op jit(solution)/shard_map/ppermute | solution.py:260
  91.4 5.2 %collective-permute-start.24 = (s32[512]{0:T(512)S(1)}, s32[512]{0:T(512)S(1)}, u32[]{:S(2)}, u32[]{:S(2)}) collective-permute-start(s32[512]{0:T(512)S(1)} %select_reduce_fusion), channel_id=1, source_target_pairs={{0,8},{4,12},{8,0},{12,4},{1,9},{5,13},{9,1},{13,5},{2,10},{6,14},... | collective-permute-start | bytes 6152 | tf_op jit(solution)/shard_map/ppermute | solution.py:260
  94.6 4.9 %collective-permute-start.23 = (s32[512]{0:T(512)S(1)}, s32[512]{0:T(512)S(1)}, u32[]{:S(2)}, u32[]{:S(2)}) collective-permute-start(s32[512]{0:T(512)S(1)} %select_reduce_fusion), channel_id=1, source_target_pairs={{0,4},{4,0},{8,12},{12,8},{1,5},{5,1},{9,13},{13,9},{2,6},{6,2},{1... | collective-permute-start | bytes 6152 | tf_op jit(solution)/shard_map/ppermute | solution.py:260
  96.7 19.5 %collective-permute-start.12 = (bf16[512,1024]{1,0:T(8,128)(2,1)S(1)}, bf16[512,1024]{1,0:T(8,128)(2,1)S(1)}, u32[]{:S(2)}, u32[]{:S(2)}) collective-permute-start(bf16[512,1024]{1,0:T(8,128)(2,1)S(1)} %copy-done.7), channel_id=1, source_target_pairs={{0,1},{1,0},{2,3},{3,2},{4,5},{5,4},{6,7},{7,6},{8,9},{9,8},{10,11... | collective-permute-start | bytes 3145736 | tf_op jit(solution)/shard_map/ppermute | solution.py:228
  99.5 16.6 %collective-permute-start.16 = (bf16[512,1024]{1,0:T(8,128)(2,1)S(1)}, bf16[512,1024]{1,0:T(8,128)(2,1)S(1)}, u32[]{:S(2)}, u32[]{:S(2)}) collective-permute-start(bf16[512,1024]{1,0:T(8,128)(2,1)S(1)} %broadcast_select_fusion.refs_11_.refs_14_), channel_id=1, source_target_pairs={{0,1},{1,0},{2,3},{3,2},{4,5},{5,4},{6,7},{7,6},{8,9},{9,8},{10,11... | collective-permute-start | bytes 3145736 | tf_op jit(solution)/shard_map/ppermute | solution.py:228
  101.0 2.3 %collective-permute-start.26 = (s32[4,512]{1,0:T(4,128)S(1)}, s32[4,512]{1,0:T(4,128)S(1)}, u32[]{:S(2)}, u32[]{:S(2)}) collective-permute-start(s32[4,512]{1,0:T(4,128)S(1)} %pad_add_fusion), channel_id=1, source_target_pairs={{0,1},{1,0},{2,3},{3,2},{4,5},{5,4},{6,7},{7,6},{8,9},{9,8},{10,11... | collective-permute-start | bytes 24584 | tf_op jit(solution)/shard_map/ppermute | solution.py:228
  103.3 33.0 %collective-permute-start.14 = (bf16[512,1024]{1,0:T(8,128)(2,1)}, bf16[512,1024]{1,0:T(8,128)(2,1)S(1)}, u32[]{:S(2)}, u32[]{:S(2)}) collective-permute-start(bf16[512,1024]{1,0:T(8,128)(2,1)} %collective-permute-done.13.refs_11_), channel_id=1, source_target_pairs={{0,1},{1,0},{2,3},{3,2},{4,5},{5,4},{6,7},{7,6},{8,9},{9,8},{10,11... | collective-permute-start | bytes 3145736 | tf_op jit(solution)/shard_map/ppermute | solution.py:228
  114.8 21.6 %collective-permute-start.17 = (bf16[512,1024]{1,0:T(8,128)(2,1)}, bf16[512,1024]{1,0:T(8,128)(2,1)S(1)}, u32[]{:S(2)}, u32[]{:S(2)}) collective-permute-start(bf16[512,1024]{1,0:T(8,128)(2,1)} %collective-permute-done.15.refs_15_), channel_id=1, source_target_pairs={{0,1},{1,0},{2,3},{3,2},{4,5},{5,4},{6,7},{7,6},{8,9},{9,8},{10,11... | collective-permute-start | bytes 3145736 | tf_op jit(solution)/shard_map/ppermute | solution.py:228
  116.2 1.0 copy-start.10
  117.1 1.0 copy-start.11
  136.4 1.0 copy-start.12
  137.4 1.0 copy-start.13
  152.3 5.1 %copy-start.5 = (bf16[512,1024]{1,0:T(8,128)(2,1)S(1)}, bf16[512,1024]{1,0:T(8,128)(2,1)}, u32[]{:S(2)}) copy-start(bf16[512,1024]{1,0:T(8,128)(2,1)} %shard_map.69) | copy-start | bytes 3145732
  155.7 3.1 %collective-permute-start.27 = (bf16[256,1024]{1,0:T(8,128)(2,1)S(1)}, bf16[256,1024]{1,0:T(8,128)(2,1)S(1)}, u32[]{:S(2)}, u32[]{:S(2)}) collective-permute-start(bf16[256,1024]{1,0:T(8,128)(2,1)S(1)} %convolution_convert_fusion.1), channel_id=1, source_target_pairs={{0,1},{1,0},{2,3},{3,2},{4,5},{5,4},{6,7},{7,6},{8,9},{9,8},{10,11... | collective-permute-start | bytes 1572872 | tf_op jit(solution)/shard_map/ppermute | solution.py:332
  157.3 5.9 %collective-permute-start.18 = (f32[136,128]{1,0:T(8,128)S(1)}, f32[136,128]{1,0:T(8,128)S(1)}, u32[]{:S(2)}, u32[]{:S(2)}) collective-permute-start(f32[136,128]{1,0:T(8,128)S(1)} %fusion.27), channel_id=1, source_target_pairs={{0,1},{1,0},{2,3},{3,2},{4,5},{5,4},{6,7},{7,6},{8,9},{9,8},{10,11... | collective-permute-start | bytes 208904 | tf_op jit(solution)/shard_map/ppermute | solution.py:307
  158.8 45.3 %collective-permute-start.30 = (bf16[128,1024]{1,0:T(8,128)(2,1)S(1)}, bf16[128,1024]{1,0:T(8,128)(2,1)S(1)}, u32[]{:S(2)}, u32[]{:S(2)}) collective-permute-start(bf16[128,1024]{1,0:T(8,128)(2,1)S(1)} %bitcast.71), channel_id=1, source_target_pairs={{0,12},{4,8},{8,4},{12,0},{1,13},{5,9},{9,5},{13,1},{2,14},{6,10},... | collective-permute-start | bytes 786440 | tf_op jit(solution)/shard_map/ppermute | solution.py:337
  158.9 45.2 %collective-permute-start.29 = (bf16[128,1024]{1,0:T(8,128)(2,1)S(1)}, bf16[128,1024]{1,0:T(8,128)(2,1)S(1)}, u32[]{:S(2)}, u32[]{:S(2)}) collective-permute-start(bf16[128,1024]{1,0:T(8,128)(2,1)S(1)} %bitcast.70), channel_id=1, source_target_pairs={{0,8},{4,12},{8,0},{12,4},{1,9},{5,13},{9,1},{13,5},{2,10},{6,14},... | collective-permute-start | bytes 786440 | tf_op jit(solution)/shard_map/ppermute | solution.py:337
  163.2 40.9 %collective-permute-start.28 = (bf16[128,1024]{1,0:T(8,128)(2,1)S(1)}, bf16[128,1024]{1,0:T(8,128)(2,1)S(1)}, u32[]{:S(2)}, u32[]{:S(2)}) collective-permute-start(bf16[128,1024]{1,0:T(8,128)(2,1)S(1)} %bitcast.69), channel_id=1, source_target_pairs={{0,4},{4,0},{8,12},{12,8},{1,5},{5,1},{9,13},{13,9},{2,6},{6,2},{1... | collective-permute-start | bytes 786440 | tf_op jit(solution)/shard_map/ppermute | solution.py:337
  163.2 25.7 %copy-start.17 = (f32[136,128]{1,0:T(8,128)}, f32[136,128]{1,0:T(8,128)S(1)}, u32[]{:S(2)}) copy-start(f32[136,128]{1,0:T(8,128)S(1)} %fusion.30.refs_0_) | copy-start | bytes 208900
  163.2 17.0 %collective-permute-start.19 = (f32[136,128]{1,0:T(8,128)S(1)}, f32[136,128]{1,0:T(8,128)S(1)}, u32[]{:S(2)}, u32[]{:S(2)}) collective-permute-start(f32[136,128]{1,0:T(8,128)S(1)} %fusion.30.refs_0_), channel_id=1, source_target_pairs={{0,4},{4,0},{8,12},{12,8},{1,5},{5,1},{9,13},{13,9},{2,6},{6,2},{1... | collective-permute-start | bytes 208904 | tf_op jit(solution)/shard_map/ppermute | solution.py:327
  164.7 20.4 %collective-permute-start.20 = (f32[136,128]{1,0:T(8,128)S(1)}, f32[136,128]{1,0:T(8,128)S(1)}, u32[]{:S(2)}, u32[]{:S(2)}) collective-permute-start(f32[136,128]{1,0:T(8,128)S(1)} %fusion.30.refs_0_), channel_id=1, source_target_pairs={{0,8},{4,12},{8,0},{12,4},{1,9},{5,13},{9,1},{13,5},{2,10},{6,14},... | collective-permute-start | bytes 208904 | tf_op jit(solution)/shard_map/ppermute | solution.py:327
  180.3 8.7 %copy-start.19 = (f32[136,128]{1,0:T(8,128)}, f32[136,128]{1,0:T(8,128)S(1)}, u32[]{:S(2)}) copy-start(f32[136,128]{1,0:T(8,128)S(1)} %collective-permute-done.19.refs_1_) | copy-start | bytes 208900
  180.3 8.7 %collective-permute-start.21 = (f32[136,128]{1,0:T(8,128)S(1)}, f32[136,128]{1,0:T(8,128)S(1)}, u32[]{:S(2)}, u32[]{:S(2)}) collective-permute-start(f32[136,128]{1,0:T(8,128)S(1)} %fusion.30.refs_0_), channel_id=1, source_target_pairs={{0,12},{4,8},{8,4},{12,0},{1,13},{5,9},{9,5},{13,1},{2,14},{6,10},... | collective-permute-start | bytes 208904 | tf_op jit(solution)/shard_map/ppermute | solution.py:327
  185.1 3.8 %copy-start.20 = (f32[136,128]{1,0:T(8,128)}, f32[136,128]{1,0:T(8,128)S(1)}, u32[]{:S(2)}) copy-start(f32[136,128]{1,0:T(8,128)S(1)} %collective-permute-done.20.refs_2_) | copy-start | bytes 208900
  189.0 0.6 copy-start.21
  202.6 3.2 %collective-permute-start.22 = (f32[2,128,64]{2,1,0:T(8,128)}, f32[2,128,64]{2,1,0:T(8,128)S(1)}, u32[]{:S(2)}, u32[]{:S(2)}) collective-permute-start(f32[2,128,64]{2,1,0:T(8,128)} %shard_map.70), channel_id=1, source_target_pairs={{0,1},{1,0},{2,3},{3,2},{4,5},{5,4},{6,7},{7,6},{8,9},{9,8},{10,11... | collective-permute-start | bytes 196616 | tf_op jit(solution)/shard_map/ppermute | solution.py:350
  204.9 0.9 copy-start.18

commit v3 on v2

--- a/solution.py
+++ b/solution.py
@@ -100,7 +100,7 @@
 
 
 ALL_PIECES = [(d, k) for d in (1, 2, 3) for k in range(4)]
-EARLY_PIECES = [(1, 0), (1, 1), (1, 2), (1, 3), (2, 0), (2, 2), (3, 0), (3, 2)]
+EARLY_PIECES = [(1, 0), (1, 1), (1, 2), (1, 3), (2, 0), (2, 2), (3, 0)]
 
 
 def project_kernel(near, widths, last, *refs):
@@ -115,74 +115,69 @@
     g, s, h, c = (lax.axis_index(a) for a in ("groups", "seq", "head", "sub"))
     block = own.shape[0]
     half = block // 2
-    blocks = 2 * near
+    count = 2 * near
     far_early = sum(widths) - (widths[-1] if last else 0)
 
-    def x_copy(src, at):
-        lanes = pl.ds(pl.multiple_of(at * block, block), block)
-        return pltpu.make_async_copy(src, xbuf.at[:, lanes], xsem.at[at])
-
-    def w_copy(src, at, part):
-        row = pl.multiple_of(at * block + part * half, half)
-        return pltpu.make_async_copy(src, wbuf.at[pl.ds(row, half)], wsem.at[at * 2 + part])
-
-    def needed(at, part):
-        dist = (at // 2) ^ s
-        kind = jnp.where(at % 2 == c, 0, 2) + jnp.where(part == g, 0, 1)
+    def x_copy(src, n):
+        lanes = pl.ds(pl.multiple_of(n * half, half), half)
+        return pltpu.make_async_copy(src, xbuf.at[:, lanes], xsem.at[n])
+
+    def w_copy(src, n):
+        return pltpu.make_async_copy(src, wbuf.at[pl.ds(pl.multiple_of(n * half, half), half)], wsem.at[n])
+
+    def needed(n):
+        dist = (n // 4) ^ s
+        kind = jnp.where((n // 2) % 2 == c, 0, 2) + jnp.where(n % 2 == g, 0, 1)
         have = dist == 0
         for d, k in EARLY_PIECES:
             have = have | ((dist == d) & (kind == k))
-        fresh = (at // near == h) | (at - (1 - h) * near < far_early)
+        fresh = (n // near == h) | (n - (1 - h) * near < far_early)
         return (have & fresh) != last
 
     if last:
         pltpu.make_async_copy(acc_in, acc, asem).start()
     else:
         acc[...] = jnp.zeros_like(acc)
+    for i in range(near):
+        x_copy(x_own.at[:, i * half : (i + 1) * half], h * near + i).start()
     for part in range(2):
         for core, src in ((c, own), (1 - c, sib)):
-
-            @pl.when(needed(s * 2 + core, part))
+            n = s * 4 + core * 2 + part
+
+            @pl.when(needed(n))
             def _():
-                w_copy(src.at[pl.ds(part * half, half)], s * 2 + core, part).start()
-
-    for i in range(near):
-        x_copy(x_own.at[:, i * block : (i + 1) * block], h * near + i).start()
-    at = (1 - h) * near
+                w_copy(src.at[pl.ds(part * half, half)], n).start()
+
+    for (d, k), src in pieces.items():
+        core = c if k < 2 else 1 - c
+        n = (s ^ d) * 4 + core * 2 + (g if k % 2 == 0 else 1 - g)
+
+        @pl.when(needed(n))
+        def _():
+            w_copy(src, n).start()
+
+    n = (1 - h) * near
     for x_far, width in zip(xs, widths):
         for i in range(width):
-            x_copy(x_far.at[:, i * block : (i + 1) * block], at).start()
-            at = at + 1
-    for (d, k), src in pieces.items():
-        core = c if k < 2 else 1 - c
-        part = g if k % 2 == 0 else 1 - g
-
-        @pl.when(needed((s ^ d) * 2 + core, part))
+            x_copy(x_far.at[:, i * half : (i + 1) * half], n).start()
+            n = n + 1
+    if last:
+        pltpu.make_async_copy(acc_in, acc, asem).wait()
+
+    @pl.loop(0, near + sum(widths))
+    def _(i):
+        n = lax.rem(i + h * near, count)
+        x_copy(x_own.at[:, :half], n).wait()
+
+        @pl.when(needed(n))
         def _():
-            w_copy(src, (s ^ d) * 2 + core, part).start()
-
-    if last:
-        pltpu.make_async_copy(acc_in, acc, asem).wait()
-
-    @pl.loop(0, blocks)
-    def _(n):
-        at = lax.rem(n + h * near, blocks)
-
-        @pl.when((n < near) | (n - near < sum(widths)))
-        def _():
-            x_copy(x_own.at[:, :block], at).wait()
-
-        @pl.loop(0, 2)
-        def _(part):
-            @pl.when(needed(at, part))
-            def _():
-                w_copy(own.at[pl.ds(0, half)], at, part).wait()
-                off = pl.multiple_of(at * block + part * half, half)
-                acc[...] += jnp.dot(
-                    xbuf[:, pl.ds(off, half)],
-                    wbuf[pl.ds(off, half), :],
-                    preferred_element_type=jnp.float32,
-                )
+            w_copy(own.at[pl.ds(0, half)], n).wait()
+            off = pl.multiple_of(n * half, half)
+            acc[...] += jnp.dot(
+                xbuf[:, pl.ds(off, half)],
+                wbuf[pl.ds(off, half), :],
+                preferred_element_type=jnp.float32,
+            )
 
     if last:
         out_ref[...] = acc[...].astype(out_ref.dtype)
@@ -192,8 +187,8 @@
     last = acc is not None
     tokens, feats = x.shape
     block, width = own.shape
-    near = feats // block
-    widths = [v.shape[1] // block for v in xs]
+    near = 2 * feats // block
+    widths = [2 * v.shape[1] // block for v in xs]
     given = [pieces[name] for name in (ALL_PIECES if last else EARLY_PIECES)]
     anywhere = pl.BlockSpec(memory_space=pl.ANY)
     args = [x, *xs, own, sib, *given] + ([acc] if last else [])
@@ -201,7 +196,7 @@
         pltpu.VMEM((tokens, 2 * feats), x.dtype),
         pltpu.VMEM((2 * feats, width), x.dtype),
         pltpu.SemaphoreType.DMA((2 * near,)),
-        pltpu.SemaphoreType.DMA((4 * near,)),
+        pltpu.SemaphoreType.DMA((2 * near,)),
     ]
     if last:
         scratch += [pltpu.VMEM((tokens, width), jnp.float32), pltpu.SemaphoreType.DMA]
@@ -211,7 +206,7 @@
         in_specs=[anywhere] * len(args),
         out_specs=pl.BlockSpec(memory_space=pltpu.VMEM),
         scratch_shapes=scratch,
-        compiler_params=pltpu.CompilerParams(vmem_limit_bytes=56 << 20),
+        compiler_params=pltpu.CompilerParams(vmem_limit_bytes=36 << 20),
         cost_estimate=pl.CostEstimate(
             flops=2 * tokens * feats * width, bytes_accessed=16 << 20, transcendentals=0
         ),
@@ -221,7 +216,7 @@
 def gathered_projection(x, own, wanted):
     g, s = lax.axis_index("groups"), lax.axis_index("seq")
     inner = (s == 1) | (s == 2)
-    block = own.shape[0]
+    block, feats = own.shape[0], x.shape[1]
     tie = lax.optimization_barrier
 
     def sub(value):
@@ -237,31 +232,48 @@
         return lax.ppermute(value, "head", SWAP)
 
     unit = lax.dynamic_slice_in_dim(own, g * (block // 2), block // 2, axis=0)
-    x0, x1 = far(x[:, :block]), far(x[:, block : 2 * block])
+    bounds = [0, 2, 4, 6, 8]
+
+    def part(value, i):
+        return value[:, bounds[i] * feats // 8 : bounds[i + 1] * feats // 8]
+
+    x0 = far(part(x, 0))
     one = along(unit, (0, 1), (1, 0), (2, 3), (3, 2))
     mid = along(unit, (1, 2), (2, 1))
-    one, mid, x0, x_rest, own_later = tie((one, mid, x0, x[:, 2 * block :], own))
+    x1 = far(part(tie(x), 1))
+    one, mid, x_a = tie((one, mid, x))
+    third = part(x_a, 2)
     mid_two = along(one, (1, 2), (2, 1))
     out_two = along(mid, (1, 0), (2, 3))
-    moved = {(1, 0): one, (1, 1): across(one), (1, 2): sub(one)}
-    x2 = far(x_rest)
-    mid_two, out_two, x1, moved[1, 1], own_later = tie(
-        (mid_two, out_two, x1, moved[1, 1], own_later)
+    one_twin = across(one)
+    mid_two, out_two, x0, x1, one_twin, third, one_b, x_b = tie(
+        (mid_two, out_two, x0, x1, one_twin, third, one, x)
     )
     two = jnp.where(inner, mid_two, out_two)
+    two, mid_two = tie((two, mid_two))
     out_three = along(mid_two, (1, 0), (2, 3))
-    moved.update({(2, 0): two, (2, 1): across(two), (2, 2): sub(two), (1, 3): sub(moved[1, 1])})
-    sib = sub(own_later)
-    out_three, moved[2, 2], moved[1, 3], sib, wanted = tie(
-        (out_three, moved[2, 2], moved[1, 3], sib, wanted)
+    x2 = far(third)
+    two_twin = across(two)
+    fourth = part(x_b, 3)
+    one_sib, one_twin_sib = sub(one_b), sub(one_twin)
+    one_sib, one_twin_sib, own_b, two_b = tie((one_sib, one_twin_sib, own, two))
+    sib, two_sib = sub(own_b), sub(two_b)
+    out_three, x2, two_twin, sib, two_sib, fourth = tie(
+        (out_three, x2, two_twin, sib, two_sib, fourth)
     )
     three = jnp.where(inner, mid, out_three)
-    moved.update({(3, 0): three, (3, 1): across(three), (3, 2): sub(three), (2, 3): sub(moved[2, 1])})
+    twin = across(three)
+    x3 = far(fourth)
+    moved = {(1, 0): one, (1, 1): one_twin, (1, 2): one_sib, (1, 3): one_twin_sib}
+    moved.update({(2, 0): two, (2, 2): two_sib, (3, 0): three})
+    acc = project(x, [x0, x1, x2], own, sib, moved)
+    moved.update({(2, 1): two_twin, (2, 3): sub(two_twin), (3, 2): sub(three)})
+    acc, wanted = tie((acc, wanted))
     lists = jnp.stack([wanted] + [lax.ppermute(wanted, "seq", xor(4, d)) for d in (1, 2, 3)])
     twin_lists = sub(lists)
-    acc = project(x, [x0, x1], own, sib, moved)
-    moved[3, 3] = sub(moved[3, 1])
-    return project(x, [x0, x1, x2], own, sib, moved, acc), lists, twin_lists
+    twin, x3 = tie((twin, x3))
+    moved.update({(3, 1): twin, (3, 3): sub(twin)})
+    return project(x, [x0, x1, x2, x3], own, sib, moved, acc), lists, twin_lists
 
 
 def plain_projection(x, own):
@@ -324,12 +336,13 @@
         both, lists, twin_lists = gathered_projection(hidden_states, own, wanted)
         packed = pack(local_moments(both, heads, dim).reshape(cores, mine, dim, dim))
         chip = core_split(packed, c)
-        parts = [chip] + [lax.ppermute(chip, "seq", xor(seq, d)) for d in (1, 2, 3)]
         near = [lists[d, 2 * d * share : (2 * d + 1) * share] for d in range(seq)]
         twin = [twin_lists[d, (2 * d + 1) * share : (2 * d + 2) * share] for d in range(seq)]
         give = selected(jnp.concatenate(twin), both)
         keep = selected(jnp.concatenate(near), both)
         taken = lax.ppermute(give, "sub", SWAP)
+        parts = [chip] + [lax.ppermute(chip, "seq", xor(seq, d)) for d in (1, 2, 3)]
+        keep, taken, *parts = lax.optimization_barrier((keep, taken, *parts))
         pairs = jnp.stack(
             [v.reshape(seq, share, 2 * width) for v in (keep, taken)], axis=1
         ).reshape(seq, cores * share, 2 * width)

time: 209 us -> 175 us (0.84)
  waiting for transfers between devices: 99.2 us -> 84.3 us
  starting transfers between devices: 45.9 us -> 38.5 us
  Pallas kernels: 40.1 us -> 33.5 us
  matrix products: 5.27 us -> 2.76 us
    ppermute x3, waiting for transfers between devices: 21.4 us -> 6.02 us  [per_device(): parts = [chip] + [lax.ppermute(chip, 'seq', xor(seq, d)) for d in (1, 2, 3)]]
    ppermute x3 -> x4, waiting for transfers between devices: 25.5 us -> 18.8 us  [far(): return lax.ppermute(value, 'head', SWAP)]
    pallas_call x2, Pallas kernels: 27.1 us -> 20.4 us  [project(): pl.pallas_call(functools.partial(project_kernel, near, widths, last), out...]
    ppermute x3, waiting for transfers between devices: 13.1 us -> 6.93 us  [across(): return lax.ppermute(value, 'groups', SWAP)]
    ppermute x3, waiting for transfers between devices: 0.01 us -> 6.16 us  [per_device(): lax.ppermute(pairs[d], 'seq', xor(seq, d))]
    ppermute x8, waiting for transfers between devices: 2.2 us -> 6.28 us  [sub(): return lax.ppermute(value, 'sub', SWAP)]
    ppermute x5, waiting for transfers between devices: 36.1 us -> 40 us  [along(): return lax.ppermute(value, 'seq', pairs)]
    ppermute x3, starting transfers between devices: 6.41 us -> 2.65 us  [gathered_projection(): lax.ppermute(wanted, 'seq', xor(4, d))]
  transfers between devices with their start and end apart: 31 -> 32, of which waited for: 14 -> 15; matrix products, arithmetic and copies ran while one was open for 5% -> 5% of each run, Pallas kernels for 13% -> 14%
where the time goes in v3:
time: 175 us; the launch traced here: 174 us
  waiting for transfers between devices  84.3 us (48%)
  starting transfers between devices  38.5 us (22%)
  Pallas kernels  33.5 us (19%)
  local copies, waits for them, and re-layouts  11.3 us (6%)
  matrix products  2.76 us (2%)
  other arithmetic  2.29 us (1%)
    ppermute x5, waiting for transfers between devices, along(): return lax.ppermute(value, 'seq', pairs)  40 us
    pallas_call x2, Pallas kernels, project(): pl.pallas_call(functools.partial(project_kernel, near, widths, last), out...  20.4 us
    ppermute x4, waiting for transfers between devices, far(): return lax.ppermute(value, 'head', SWAP)  18.8 us
    ppermute x5, starting transfers between devices, along(): return lax.ppermute(value, 'seq', pairs)  13.1 us
    pallas_call x1, Pallas kernels, solve(): pl.pallas_call(functools.partial(solve_kernel, 1.0 / token_total, len(par...  13 us
    ppermute x8, starting transfers between devices, sub(): return lax.ppermute(value, 'sub', SWAP)  8.74 us
    unnamed x39, local copies, waits for them, and re-layouts  7.5 us
    ppermute x3, waiting for transfers between devices, across(): return lax.ppermute(value, 'groups', SWAP)  6.93 us
  transfers between devices with their start and end apart: 32, of which 15 were waited for; matrix products, arithmetic and copies ran while one was open for 5% of the time, Pallas kernels for 14%

profile of v3, /device:TPU:11, one launch (start us, length us, event | category | flops | bytes accessed | tf_op | source)
XLA Modules:
  0.0 173.5 jit_solution(100866787534376107)
XLA Ops:
  0.7 1.5 constant_dynamic-update-slice_fusion.1
  2.2 0.1 constant_dynamic-update-slice_fusion.refs_4_.refs_5_
  2.5 0.2 collective-permute-start
  2.7 4.5 %collective-permute-start.1 = (bf16[512,1024]{1,0:T(8,128)(2,1)S(1)}, bf16[512,1024]{1,0:T(8,128)(2,1)S(1)}, u32[]{:S(2)}, u32[]{:S(2)}) collective-permute-start(bf16[512,1024]{1,0:T(8,128)(2,1)S(1)} %constant_dynamic-slice_fusion.1), channel_id=1, source_target_pairs={{4,8},{8,4},{5,9},{9,5},{6,10},{10,6},{7,11},{11,7},{20,24},{24,20... | collective-permute-start | bytes 3145736 | tf_op jit(solution)/shard_map/ppermute | solution.py:229
  7.3 0.3 collective-permute-start.4
  7.7 1.3 collective-permute-start.5
  9.0 17.7 %collective-permute-done.refs_6_.refs_7_ = bf16[512,1024]{1,0:T(8,128)(2,1)} collective-permute-done((bf16[512,1024]{1,0:T(8,128)(2,1)S(1)}, bf16[512,1024]{1,0:T(8,128)(2,1)}, u32[]{:S(2)}, u32[]{:S(2)}) %collective-permute-start) | collective-permute-done | bytes 1048608 | tf_op jit(solution)/shard_map/ppermute | solution.py:229
  26.7 3.0 %collective-permute-done.1 = bf16[512,1024]{1,0:T(8,128)(2,1)S(1)} collective-permute-done((bf16[512,1024]{1,0:T(8,128)(2,1)S(1)}, bf16[512,1024]{1,0:T(8,128)(2,1)S(1)}, u32[]{:S(2)}, u32[]{:S(2)}) %collective-permute-start.1) | collective-permute-done | bytes 1048608 | tf_op jit(solution)/shard_map/ppermute | solution.py:229
  29.7 3.0 %collective-permute-start.2 = (bf16[512,1024]{1,0:T(8,128)(2,1)}, bf16[512,1024]{1,0:T(8,128)(2,1)}, u32[]{:S(2)}, u32[]{:S(2)}) collective-permute-start(bf16[512,1024]{1,0:T(8,128)(2,1)} %collective-permute-done.refs_6_.refs_7_), channel_id=1, source_target_pairs={{4,8},{8,4},{5,9},{9,5},{6,10},{10,6},{7,11},{11,7},{20,24},{24,20... | collective-permute-start | bytes 3145736 | tf_op jit(solution)/shard_map/ppermute | solution.py:229
  32.8 1.3 collective-permute-start.6
  34.1 1.3 collective-permute-start.3
  35.4 1.1 slice.69
  36.5 1.0 copy-done.3
  37.5 15.9 %collective-permute-done.5.refs_2_ = bf16[512,1024]{1,0:T(8,128)(2,1)S(1)} collective-permute-done((bf16[512,1024]{1,0:T(8,128)(2,1)S(1)}, bf16[512,1024]{1,0:T(8,128)(2,1)S(1)}, u32[]{:S(2)}, u32[]{:S(2)}) %collective-permute-start.5) | collective-permute-done | bytes 1048608 | tf_op jit(solution)/shard_map/ppermute | solution.py:232
  53.3 1.0 copy-done.5
  54.3 0.7 collective-permute-done.2
  55.0 0.6 collective-permute-done.6.refs_7_.refs_8_
  55.7 1.0 copy-done.11
  56.6 3.1 %collective-permute-start.11 = (bf16[512,1024]{1,0:T(8,128)(2,1)}, bf16[512,1024]{1,0:T(8,128)(2,1)}, u32[]{:S(2)}, u32[]{:S(2)}) collective-permute-start(bf16[512,1024]{1,0:T(8,128)(2,1)} %collective-permute-done.6.refs_7_.refs_8_), channel_id=1, source_target_pairs={{0,1},{1,0},{2,3},{3,2},{4,5},{5,4},{6,7},{7,6},{8,9},{9,8},{10,11... | collective-permute-start | bytes 3145736 | tf_op jit(solution)/shard_map/ppermute | solution.py:223
  59.7 1.3 broadcast_select_fusion.1.refs_10_.refs_11_
  61.0 1.3 collective-permute-done.11.refs_9_.refs_10_
  62.3 1.5 collective-permute-done.10.refs_8_.refs_9_
  63.8 0.4 collective-permute-start.12
  64.2 1.2 collective-permute-start.9
  65.4 4.1 %collective-permute-start.7 = (bf16[512,1024]{1,0:T(8,128)(2,1)}, bf16[512,1024]{1,0:T(8,128)(2,1)}, u32[]{:S(2)}, u32[]{:S(2)}) collective-permute-start(bf16[512,1024]{1,0:T(8,128)(2,1)} %collective-permute-done.2), channel_id=1, source_target_pairs={{4,0},{8,12},{5,1},{9,13},{6,2},{10,14},{7,3},{11,15},{20,16},{24,... | collective-permute-start | bytes 3145736 | tf_op jit(solution)/shard_map/ppermute | solution.py:229
  69.5 0.3 collective-permute-start.8
  69.8 1.0 collective-permute-start.13
  70.8 0.2 convert_reduce_fusion
  71.0 1.3 slice.70
  72.4 18.5 %collective-permute-done.7 = bf16[512,1024]{1,0:T(8,128)(2,1)} collective-permute-done((bf16[512,1024]{1,0:T(8,128)(2,1)}, bf16[512,1024]{1,0:T(8,128)(2,1)}, u32[]{:S(2)}, u32[]{:S(2)}) %collective-permute-start.7) | collective-permute-done | bytes 1048608 | tf_op jit(solution)/shard_map/ppermute | solution.py:229
  90.9 2.9 %collective-permute-done.8.refs_3_ = bf16[512,1024]{1,0:T(8,128)(2,1)} collective-permute-done((bf16[512,1024]{1,0:T(8,128)(2,1)}, bf16[512,1024]{1,0:T(8,128)(2,1)}, u32[]{:S(2)}, u32[]{:S(2)}) %collective-permute-start.8) | collective-permute-done | bytes 1048608 | tf_op jit(solution)/shard_map/ppermute | solution.py:232
  94.0 1.3 collective-permute-start.17
  95.3 0.3 collective-permute-start.18
  95.6 0.2 select_reduce_fusion
  95.8 11.0 %shard_map.68.refs_19_ = f32[512,1024]{1,0:T(8,128)S(1)} custom-call(bf16[512,4096]{1,0:T(8,128)(2,1)} %refs_0_.3, bf16[512,1024]{1,0:T(8,128)(2,1)S(1)} %copy-done.4, bf16[512,1024]{1,0:T(8,128)(2,1)S(1)} %copy-done.6, bf16[512,1024]{1,0:T(8,128)(2,1)} %collective-permute-done.8.refs_3_, ...), custom_call_target="tpu_custom_call" | custom-call | flops 4294967296 | bytes 16777216 | tf_op jit(solution)/shard_map/pallas_call | solution.py:203
  106.8 1.4 copy-done.2
  108.1 0.9 collective-permute-start.14
  109.0 0.7 collective-permute-start.15
  109.7 1.1 collective-permute-start.16
  110.8 6.3 %collective-permute-done.17.refs_16_ = bf16[512,1024]{1,0:T(8,128)(2,1)S(1)} collective-permute-done((bf16[512,1024]{1,0:T(8,128)(2,1)S(1)}, bf16[512,1024]{1,0:T(8,128)(2,1)S(1)}, u32[]{:S(2)}, u32[]{:S(2)}) %collective-permute-start.17) | collective-permute-done | bytes 1048608 | tf_op jit(solution)/shard_map/ppermute | solution.py:226
  117.1 2.5 %collective-permute-start.20 = (bf16[512,1024]{1,0:T(8,128)(2,1)S(1)}, bf16[512,1024]{1,0:T(8,128)(2,1)S(1)}, u32[]{:S(2)}, u32[]{:S(2)}) collective-permute-start(bf16[512,1024]{1,0:T(8,128)(2,1)S(1)} %broadcast_select_fusion.refs_12_.refs_15_), channel_id=1, source_target_pairs={{0,1},{1,0},{2,3},{3,2},{4,5},{5,4},{6,7},{7,6},{8,9},{9,8},{10,11... | collective-permute-start | bytes 3145736 | tf_op jit(solution)/shard_map/ppermute | solution.py:223
  119.6 1.2 collective-permute-start.19
  120.9 0.6 collective-permute-start.22
  121.4 3.4 %collective-permute-done.22 = s32[4,512]{1,0:T(4,128)S(1)} collective-permute-done((s32[4,512]{1,0:T(4,128)S(1)}, s32[4,512]{1,0:T(4,128)S(1)}, u32[]{:S(2)}, u32[]{:S(2)}) %collective-permute-start.22) | collective-permute-done | bytes 8224 | tf_op jit(solution)/shard_map/ppermute | solution.py:223
  125.1 9.5 %shard_map.69 = bf16[512,1024]{1,0:T(8,128)(2,1)S(1)} custom-call(bf16[512,4096]{1,0:T(8,128)(2,1)} %refs_0_.3, bf16[512,1024]{1,0:T(8,128)(2,1)S(1)} %copy-done.4, bf16[512,1024]{1,0:T(8,128)(2,1)S(1)} %copy-done.6, bf16[512,1024]{1,0:T(8,128)(2,1)} %collective-permute-done.8.refs_3_, bf16[512,1024]{1,0:T(8,128)(2,1)S(1)} %collective-permute-done.18.refs_4_, ...), custom_call_target="tpu_custom_call" | custom-call | flops 4294967296 | bytes 16777216 | tf_op jit(solution)/shard_map/pallas_call | solution.py:203
  134.6 0.3 fusion.10
  135.0 0.4 collective-permute-start.24
  135.4 0.5 convolution_convert_fusion.1
  135.9 0.2 collective-permute-start.23
  136.3 0.9 collective-permute-start.25
  137.3 1.8 %collective-permute-start.27 = (f32[136,128]{1,0:T(8,128)S(1)}, f32[136,128]{1,0:T(8,128)S(1)}, u32[]{:S(2)}, u32[]{:S(2)}) collective-permute-start(f32[136,128]{1,0:T(8,128)S(1)} %fusion.30.refs_0_), channel_id=1, source_target_pairs={{0,12},{4,8},{8,4},{12,0},{1,13},{5,9},{9,5},{13,1},{2,14},{6,10},... | collective-permute-start | bytes 208904 | tf_op jit(solution)/shard_map/ppermute | solution.py:344
  139.1 0.5 convolution_convert_fusion.2
  139.6 1.9 %collective-permute-done.26.refs_2_ = f32[136,128]{1,0:T(8,128)S(1)} collective-permute-done((f32[136,128]{1,0:T(8,128)S(1)}, f32[136,128]{1,0:T(8,128)S(1)}, u32[]{:S(2)}, u32[]{:S(2)}) %collective-permute-start.26) | collective-permute-done | bytes 69664 | tf_op jit(solution)/shard_map/ppermute | solution.py:344
  141.5 4.1 %collective-permute-done.27.refs_3_ = f32[136,128]{1,0:T(8,128)S(1)} collective-permute-done((f32[136,128]{1,0:T(8,128)S(1)}, f32[136,128]{1,0:T(8,128)S(1)}, u32[]{:S(2)}, u32[]{:S(2)}) %collective-permute-start.27) | collective-permute-done | bytes 69664 | tf_op jit(solution)/shard_map/ppermute | solution.py:344
  145.8 1.3 collective-permute-start.30
  147.1 1.3 collective-permute-start.31
  148.4 0.8 copy.26.refs_4_
  149.2 13.0 %shard_map.70 = f32[2,128,64]{2,1,0:T(8,128)} custom-call(f32[136,128]{1,0:T(8,128)} %copy-done.12, f32[136,128]{1,0:T(8,128)} %copy-done.14, f32[136,128]{1,0:T(8,128)} %copy-done.15, f32[136,128]{1,0:T(8,128)} %copy-done.16, f32[2,128,64]{2,1,0:T(8,128)} %copy.26.refs_4_), custom_call_target="tpu_custom_call" | custom-call | flops 4194304 | bytes 131072 | tf_op jit(solution)/shard_map/pallas_call | solution.py:93
  162.2 1.9 %collective-permute-start.28 = (f32[2,128,64]{2,1,0:T(8,128)}, f32[2,128,64]{2,1,0:T(8,128)S(1)}, u32[]{:S(2)}, u32[]{:S(2)}) collective-permute-start(f32[2,128,64]{2,1,0:T(8,128)} %shard_map.70), channel_id=1, source_target_pairs={{0,1},{1,0},{2,3},{3,2},{4,5},{5,4},{6,7},{7,6},{8,9},{9,8},{10,11... | collective-permute-start | bytes 196616 | tf_op jit(solution)/shard_map/ppermute | solution.py:363
  164.1 6.2 %collective-permute-done.31 = bf16[128,1024]{1,0:T(8,128)(2,1)S(1)} collective-permute-done((bf16[128,1024]{1,0:T(8,128)(2,1)S(1)}, bf16[128,1024]{1,0:T(8,128)(2,1)S(1)}, u32[]{:S(2)}, u32[]{:S(2)}) %collective-permute-start.31) | collective-permute-done | bytes 262176 | tf_op jit(solution)/shard_map/ppermute | solution.py:350
  170.3 0.8 convolution_convert_fusion
  171.1 0.9 fusion.35
  172.0 0.7 convolution_convert_fusion.3
  172.7 0.8 copy.22
  (75 shorter events, 1.3 us)
Async XLA Ops:
  0.6 147.8 %copy-start = (f32[4,128,64]{1,2,0:T(8,128)S(1)}, f32[4,128,64]{1,2,0:T(8,128)}, u32[]{:S(2)}) copy-start(f32[4,128,64]{1,2,0:T(8,128)} %param.8) | copy-start | bytes 393220
  0.6 1.6 copy-start.8
  2.2 4.9 %copy-start.7 = (bf16[512,4096]{1,0:T(8,128)(2,1)S(1)}, bf16[512,4096]{1,0:T(8,128)(2,1)}, u32[]{:S(2)}) copy-start(bf16[512,4096]{1,0:T(8,128)(2,1)} %refs_0_.3) | copy-start | bytes 12582916
  2.4 93.4 %copy-start.1 = (bf16[1024,1024]{1,0:T(8,128)(2,1)}, bf16[1024,1024]{1,0:T(8,128)(2,1)S(1)}, u32[]{:S(2)}) copy-start(bf16[1024,1024]{1,0:T(8,128)(2,1)S(1)} %constant_dynamic-update-slice_fusion.refs_4_.refs_5_) | copy-start | bytes 6291460
  2.5 24.2 %collective-permute-start = (bf16[512,1024]{1,0:T(8,128)(2,1)S(1)}, bf16[512,1024]{1,0:T(8,128)(2,1)}, u32[]{:S(2)}, u32[]{:S(2)}) collective-permute-start(bf16[512,1024]{1,0:T(8,128)(2,1)S(1)} %constant_dynamic-slice_fusion.1), channel_id=1, source_target_pairs={{0,4},{4,0},{8,12},{12,8},{1,5},{5,1},{9,13},{13,9},{2,6},{6,2},{1... | collective-permute-start | bytes 3145736 | tf_op jit(solution)/shard_map/ppermute | solution.py:229
  2.7 27.0 %collective-permute-start.1 = (bf16[512,1024]{1,0:T(8,128)(2,1)S(1)}, bf16[512,1024]{1,0:T(8,128)(2,1)S(1)}, u32[]{:S(2)}, u32[]{:S(2)}) collective-permute-start(bf16[512,1024]{1,0:T(8,128)(2,1)S(1)} %constant_dynamic-slice_fusion.1), channel_id=1, source_target_pairs={{4,8},{8,4},{5,9},{9,5},{6,10},{10,6},{7,11},{11,7},{20,24},{24,20... | collective-permute-start | bytes 3145736 | tf_op jit(solution)/shard_map/ppermute | solution.py:229
  7.3 29.2 %collective-permute-start.4 = (bf16[512,1024]{1,0:T(8,128)(2,1)S(1)}, bf16[512,1024]{1,0:T(8,128)(2,1)S(1)}, u32[]{:S(2)}, u32[]{:S(2)}) collective-permute-start(bf16[512,1024]{1,0:T(8,128)(2,1)S(1)} %slice.67), channel_id=1, source_target_pairs={{0,2},{2,0},{1,3},{3,1},{4,6},{6,4},{5,7},{7,5},{8,10},{10,8},{9,1... | collective-permute-start | bytes 3145736 | tf_op jit(solution)/shard_map/ppermute | solution.py:232
  7.7 45.6 %collective-permute-start.5 = (bf16[512,1024]{1,0:T(8,128)(2,1)S(1)}, bf16[512,1024]{1,0:T(8,128)(2,1)S(1)}, u32[]{:S(2)}, u32[]{:S(2)}) collective-permute-start(bf16[512,1024]{1,0:T(8,128)(2,1)S(1)} %slice.88), channel_id=1, source_target_pairs={{0,2},{2,0},{1,3},{3,1},{4,6},{6,4},{5,7},{7,5},{8,10},{10,8},{9,1... | collective-permute-start | bytes 3145736 | tf_op jit(solution)/shard_map/ppermute | solution.py:232
  29.7 23.6 %copy-start.9 = (bf16[512,1024]{1,0:T(8,128)(2,1)}, bf16[512,1024]{1,0:T(8,128)(2,1)S(1)}, u32[]{:S(2)}) copy-start(bf16[512,1024]{1,0:T(8,128)(2,1)S(1)} %collective-permute-done.1) | copy-start | bytes 3145732
  29.7 25.3 %collective-permute-start.2 = (bf16[512,1024]{1,0:T(8,128)(2,1)}, bf16[512,1024]{1,0:T(8,128)(2,1)}, u32[]{:S(2)}, u32[]{:S(2)}) collective-permute-start(bf16[512,1024]{1,0:T(8,128)(2,1)} %collective-permute-done.refs_6_.refs_7_), channel_id=1, source_target_pairs={{4,8},{8,4},{5,9},{9,5},{6,10},{10,6},{7,11},{11,7},{20,24},{24,20... | collective-permute-start | bytes 3145736 | tf_op jit(solution)/shard_map/ppermute | solution.py:229
  32.8 22.9 %collective-permute-start.6 = (bf16[512,1024]{1,0:T(8,128)(2,1)}, bf16[512,1024]{1,0:T(8,128)(2,1)}, u32[]{:S(2)}, u32[]{:S(2)}) collective-permute-start(bf16[512,1024]{1,0:T(8,128)(2,1)} %collective-permute-done.refs_6_.refs_7_), channel_id=1, source_target_pairs={{0,16},{16,0},{1,17},{17,1},{2,18},{18,2},{3,19},{19,3},{4,20},{20... | collective-permute-start | bytes 3145736 | tf_op jit(solution)/shard_map/ppermute | solution.py:226
  34.1 21.6 %collective-permute-start.3 = (bf16[512,1024]{1,0:T(8,128)(2,1)S(1)}, bf16[512,1024]{1,0:T(8,128)(2,1)S(1)}, u32[]{:S(2)}, u32[]{:S(2)}) collective-permute-start(bf16[512,1024]{1,0:T(8,128)(2,1)S(1)} %collective-permute-done.1), channel_id=1, source_target_pairs={{4,0},{8,12},{5,1},{9,13},{6,2},{10,14},{7,3},{11,15},{20,16},{24,... | collective-permute-start | bytes 3145736 | tf_op jit(solution)/shard_map/ppermute | solution.py:229
  36.5 34.3 %copy-start.17 = (s32[512]{0:T(512)S(1)}, s32[512]{0:T(512)}, u32[]{:S(2)}) copy-start(s32[512]{0:T(512)} %param.9) | copy-start | bytes 6148
  36.5 1.0 copy-start.3
  53.3 1.0 copy-start.5
  55.7 1.0 copy-start.11
  56.6 5.7 %collective-permute-start.11 = (bf16[512,1024]{1,0:T(8,128)(2,1)}, bf16[512,1024]{1,0:T(8,128)(2,1)}, u32[]{:S(2)}, u32[]{:S(2)}) collective-permute-start(bf16[512,1024]{1,0:T(8,128)(2,1)} %collective-permute-done.6.refs_7_.refs_8_), channel_id=1, source_target_pairs={{0,1},{1,0},{2,3},{3,2},{4,5},{5,4},{6,7},{7,6},{8,9},{9,8},{10,11... | collective-permute-start | bytes 3145736 | tf_op jit(solution)/shard_map/ppermute | solution.py:223
  59.7 4.1 %collective-permute-start.10 = (bf16[512,1024]{1,0:T(8,128)(2,1)}, bf16[512,1024]{1,0:T(8,128)(2,1)}, u32[]{:S(2)}, u32[]{:S(2)}) collective-permute-start(bf16[512,1024]{1,0:T(8,128)(2,1)} %collective-permute-done.refs_6_.refs_7_), channel_id=1, source_target_pairs={{0,1},{1,0},{2,3},{3,2},{4,5},{5,4},{6,7},{7,6},{8,9},{9,8},{10,11... | collective-permute-start | bytes 3145736 | tf_op jit(solution)/shard_map/ppermute | solution.py:223
  63.8 30.0 %collective-permute-start.12 = (bf16[1024,1024]{1,0:T(8,128)(2,1)S(1)}, bf16[1024,1024]{1,0:T(8,128)(2,1)}, u32[]{:S(2)}, u32[]{:S(2)}) collective-permute-start(bf16[1024,1024]{1,0:T(8,128)(2,1)S(1)} %constant_dynamic-update-slice_fusion.refs_4_.refs_5_), channel_id=1, source_target_pairs={{0,1},{1,0},{2,3},{3,2},{4,5},{5,4},{6,7},{7,6},{8,9},{9,8},{10,11... | collective-permute-start | bytes 6291464 | tf_op jit(solution)/shard_map/ppermute | solution.py:223
  64.2 26.7 %collective-permute-start.9 = (bf16[512,1024]{1,0:T(8,128)(2,1)S(1)}, bf16[512,1024]{1,0:T(8,128)(2,1)}, u32[]{:S(2)}, u32[]{:S(2)}) collective-permute-start(bf16[512,1024]{1,0:T(8,128)(2,1)S(1)} %broadcast_select_fusion.1.refs_10_.refs_11_), channel_id=1, source_target_pairs={{0,16},{16,0},{1,17},{17,1},{2,18},{18,2},{3,19},{19,3},{4,20},{20... | collective-permute-start | bytes 3145736 | tf_op jit(solution)/shard_map/ppermute | solution.py:226
  65.4 25.5 %collective-permute-start.7 = (bf16[512,1024]{1,0:T(8,128)(2,1)}, bf16[512,1024]{1,0:T(8,128)(2,1)}, u32[]{:S(2)}, u32[]{:S(2)}) collective-permute-start(bf16[512,1024]{1,0:T(8,128)(2,1)} %collective-permute-done.2), channel_id=1, source_target_pairs={{4,0},{8,12},{5,1},{9,13},{6,2},{10,14},{7,3},{11,15},{20,16},{24,... | collective-permute-start | bytes 3145736 | tf_op jit(solution)/shard_map/ppermute | solution.py:229
  69.5 24.3 %collective-permute-start.8 = (bf16[512,1024]{1,0:T(8,128)(2,1)}, bf16[512,1024]{1,0:T(8,128)(2,1)}, u32[]{:S(2)}, u32[]{:S(2)}) collective-permute-start(bf16[512,1024]{1,0:T(8,128)(2,1)} %slice.69), channel_id=1, source_target_pairs={{0,2},{2,0},{1,3},{3,1},{4,6},{6,4},{5,7},{7,5},{8,10},{10,8},{9,1... | collective-permute-start | bytes 3145736 | tf_op jit(solution)/shard_map/ppermute | solution.py:232
  69.8 24.0 %collective-permute-start.13 = (bf16[512,1024]{1,0:T(8,128)(2,1)S(1)}, bf16[512,1024]{1,0:T(8,128)(2,1)}, u32[]{:S(2)}, u32[]{:S(2)}) collective-permute-start(bf16[512,1024]{1,0:T(8,128)(2,1)S(1)} %broadcast_select_fusion.1.refs_10_.refs_11_), channel_id=1, source_target_pairs={{0,1},{1,0},{2,3},{3,2},{4,5},{5,4},{6,7},{7,6},{8,9},{9,8},{10,11... | collective-permute-start | bytes 3145736 | tf_op jit(solution)/shard_map/ppermute | solution.py:223
  70.8 23.1 %copy-start.10 = (bf16[512,1024]{1,0:T(8,128)(2,1)S(1)}, bf16[512,1024]{1,0:T(8,128)(2,1)}, u32[]{:S(2)}) copy-start(bf16[512,1024]{1,0:T(8,128)(2,1)} %copy-done.9) | copy-start | bytes 3145732
  72.4 23.4 %copy-start.4 = (bf16[512,1024]{1,0:T(8,128)(2,1)S(1)}, bf16[512,1024]{1,0:T(8,128)(2,1)}, u32[]{:S(2)}) copy-start(bf16[512,1024]{1,0:T(8,128)(2,1)} %copy-done.3) | copy-start | bytes 3145732
  72.4 23.4 %copy-start.6 = (bf16[512,1024]{1,0:T(8,128)(2,1)S(1)}, bf16[512,1024]{1,0:T(8,128)(2,1)}, u32[]{:S(2)}) copy-start(bf16[512,1024]{1,0:T(8,128)(2,1)} %copy-done.5) | copy-start | bytes 3145732
  94.0 23.1 %collective-permute-start.17 = (bf16[512,1024]{1,0:T(8,128)(2,1)S(1)}, bf16[512,1024]{1,0:T(8,128)(2,1)S(1)}, u32[]{:S(2)}, u32[]{:S(2)}) collective-permute-start(bf16[512,1024]{1,0:T(8,128)(2,1)S(1)} %broadcast_select_fusion.refs_12_.refs_15_), channel_id=1, source_target_pairs={{0,16},{16,0},{1,17},{17,1},{2,18},{18,2},{3,19},{19,3},{4,20},{20... | collective-permute-start | bytes 3145736 | tf_op jit(solution)/shard_map/ppermute | solution.py:226
  95.3 24.3 %collective-permute-start.18 = (bf16[512,1024]{1,0:T(8,128)(2,1)S(1)}, bf16[512,1024]{1,0:T(8,128)(2,1)S(1)}, u32[]{:S(2)}, u32[]{:S(2)}) collective-permute-start(bf16[512,1024]{1,0:T(8,128)(2,1)S(1)} %slice.70), channel_id=1, source_target_pairs={{0,2},{2,0},{1,3},{3,1},{4,6},{6,4},{5,7},{7,5},{8,10},{10,8},{9,1... | collective-permute-start | bytes 3145736 | tf_op jit(solution)/shard_map/ppermute | solution.py:232
  106.8 1.4 copy-start.2
  108.1 12.7 %collective-permute-start.14 = (s32[512]{0:T(512)S(1)}, s32[512]{0:T(512)S(1)}, u32[]{:S(2)}, u32[]{:S(2)}) collective-permute-start(s32[512]{0:T(512)S(1)} %select_reduce_fusion), channel_id=1, source_target_pairs={{0,4},{4,0},{8,12},{12,8},{1,5},{5,1},{9,13},{13,9},{2,6},{6,2},{1... | collective-permute-start | bytes 6152 | tf_op jit(solution)/shard_map/ppermute | solution.py:272
  109.0 11.9 %collective-permute-start.15 = (s32[512]{0:T(512)S(1)}, s32[512]{0:T(512)S(1)}, u32[]{:S(2)}, u32[]{:S(2)}) collective-permute-start(s32[512]{0:T(512)S(1)} %select_reduce_fusion), channel_id=1, source_target_pairs={{0,8},{4,12},{8,0},{12,4},{1,9},{5,13},{9,1},{13,5},{2,10},{6,14},... | collective-permute-start | bytes 6152 | tf_op jit(solution)/shard_map/ppermute | solution.py:272
  109.7 11.1 %collective-permute-start.16 = (s32[512]{0:T(512)S(1)}, s32[512]{0:T(512)S(1)}, u32[]{:S(2)}, u32[]{:S(2)}) collective-permute-start(s32[512]{0:T(512)S(1)} %select_reduce_fusion), channel_id=1, source_target_pairs={{0,12},{4,8},{8,4},{12,0},{1,13},{5,9},{9,5},{13,1},{2,14},{6,10},... | collective-permute-start | bytes 6152 | tf_op jit(solution)/shard_map/ppermute | solution.py:272
  117.1 8.0 %collective-permute-start.20 = (bf16[512,1024]{1,0:T(8,128)(2,1)S(1)}, bf16[512,1024]{1,0:T(8,128)(2,1)S(1)}, u32[]{:S(2)}, u32[]{:S(2)}) collective-permute-start(bf16[512,1024]{1,0:T(8,128)(2,1)S(1)} %broadcast_select_fusion.refs_12_.refs_15_), channel_id=1, source_target_pairs={{0,1},{1,0},{2,3},{3,2},{4,5},{5,4},{6,7},{7,6},{8,9},{9,8},{10,11... | collective-permute-start | bytes 3145736 | tf_op jit(solution)/shard_map/ppermute | solution.py:223
  119.6 5.5 %collective-permute-start.19 = (bf16[512,1024]{1,0:T(8,128)(2,1)}, bf16[512,1024]{1,0:T(8,128)(2,1)S(1)}, u32[]{:S(2)}, u32[]{:S(2)}) collective-permute-start(bf16[512,1024]{1,0:T(8,128)(2,1)} %collective-permute-done.9.refs_12_), channel_id=1, source_target_pairs={{0,1},{1,0},{2,3},{3,2},{4,5},{5,4},{6,7},{7,6},{8,9},{9,8},{10,11... | collective-permute-start | bytes 3145736 | tf_op jit(solution)/shard_map/ppermute | solution.py:223
  120.8 4.3 %collective-permute-start.21 = (bf16[512,1024]{1,0:T(8,128)(2,1)S(1)}, bf16[512,1024]{1,0:T(8,128)(2,1)S(1)}, u32[]{:S(2)}, u32[]{:S(2)}) collective-permute-start(bf16[512,1024]{1,0:T(8,128)(2,1)S(1)} %collective-permute-done.17.refs_16_), channel_id=1, source_target_pairs={{0,1},{1,0},{2,3},{3,2},{4,5},{5,4},{6,7},{7,6},{8,9},{9,8},{10,11... | collective-permute-start | bytes 3145736 | tf_op jit(solution)/shard_map/ppermute | solution.py:223
  120.9 4.0 %collective-permute-start.22 = (s32[4,512]{1,0:T(4,128)S(1)}, s32[4,512]{1,0:T(4,128)S(1)}, u32[]{:S(2)}, u32[]{:S(2)}) collective-permute-start(s32[4,512]{1,0:T(4,128)S(1)} %pad_add_fusion), channel_id=1, source_target_pairs={{0,1},{1,0},{2,3},{3,2},{4,5},{5,4},{6,7},{7,6},{8,9},{9,8},{10,11... | collective-permute-start | bytes 24584 | tf_op jit(solution)/shard_map/ppermute | solution.py:223
  135.0 1.3 collective-permute-start.24
  135.9 9.7 %collective-permute-start.23 = (bf16[256,1024]{1,0:T(8,128)(2,1)S(1)}, bf16[256,1024]{1,0:T(8,128)(2,1)S(1)}, u32[]{:S(2)}, u32[]{:S(2)}) collective-permute-start(bf16[256,1024]{1,0:T(8,128)(2,1)S(1)} %convolution_convert_fusion.1), channel_id=1, source_target_pairs={{0,1},{1,0},{2,3},{3,2},{4,5},{5,4},{6,7},{7,6},{8,9},{9,8},{10,11... | collective-permute-start | bytes 1572872 | tf_op jit(solution)/shard_map/ppermute | solution.py:343
  136.3 12.8 %copy-start.12 = (f32[136,128]{1,0:T(8,128)}, f32[136,128]{1,0:T(8,128)S(1)}, u32[]{:S(2)}) copy-start(f32[136,128]{1,0:T(8,128)S(1)} %fusion.30.refs_0_) | copy-start | bytes 208900
  136.3 3.2 %collective-permute-start.25 = (f32[136,128]{1,0:T(8,128)S(1)}, f32[136,128]{1,0:T(8,128)S(1)}, u32[]{:S(2)}, u32[]{:S(2)}) collective-permute-start(f32[136,128]{1,0:T(8,128)S(1)} %fusion.30.refs_0_), channel_id=1, source_target_pairs={{0,4},{4,0},{8,12},{12,8},{1,5},{5,1},{9,13},{13,9},{2,6},{6,2},{1... | collective-permute-start | bytes 208904 | tf_op jit(solution)/shard_map/ppermute | solution.py:344
  137.3 4.2 %collective-permute-start.26 = (f32[136,128]{1,0:T(8,128)S(1)}, f32[136,128]{1,0:T(8,128)S(1)}, u32[]{:S(2)}, u32[]{:S(2)}) collective-permute-start(f32[136,128]{1,0:T(8,128)S(1)} %fusion.30.refs_0_), channel_id=1, source_target_pairs={{0,8},{4,12},{8,0},{12,4},{1,9},{5,13},{9,1},{13,5},{2,10},{6,14},... | collective-permute-start | bytes 208904 | tf_op jit(solution)/shard_map/ppermute | solution.py:344
  137.3 8.3 %collective-permute-start.27 = (f32[136,128]{1,0:T(8,128)S(1)}, f32[136,128]{1,0:T(8,128)S(1)}, u32[]{:S(2)}, u32[]{:S(2)}) collective-permute-start(f32[136,128]{1,0:T(8,128)S(1)} %fusion.30.refs_0_), channel_id=1, source_target_pairs={{0,12},{4,8},{8,4},{12,0},{1,13},{5,9},{9,5},{13,1},{2,14},{6,10},... | collective-permute-start | bytes 208904 | tf_op jit(solution)/shard_map/ppermute | solution.py:344
  139.6 9.6 %copy-start.14 = (f32[136,128]{1,0:T(8,128)}, f32[136,128]{1,0:T(8,128)S(1)}, u32[]{:S(2)}) copy-start(f32[136,128]{1,0:T(8,128)S(1)} %collective-permute-done.25.refs_1_) | copy-start | bytes 208900
  141.4 7.7 %copy-start.15 = (f32[136,128]{1,0:T(8,128)}, f32[136,128]{1,0:T(8,128)S(1)}, u32[]{:S(2)}) copy-start(f32[136,128]{1,0:T(8,128)S(1)} %collective-permute-done.26.refs_2_) | copy-start | bytes 208900
  145.6 3.6 %copy-start.16 = (f32[136,128]{1,0:T(8,128)}, f32[136,128]{1,0:T(8,128)S(1)}, u32[]{:S(2)}) copy-start(f32[136,128]{1,0:T(8,128)S(1)} %collective-permute-done.27.refs_3_) | copy-start | bytes 208900
  145.7 18.5 %collective-permute-start.29 = (bf16[128,1024]{1,0:T(8,128)(2,1)S(1)}, bf16[128,1024]{1,0:T(8,128)(2,1)S(1)}, u32[]{:S(2)}, u32[]{:S(2)}) collective-permute-start(bf16[128,1024]{1,0:T(8,128)(2,1)S(1)} %bitcast.71), channel_id=1, source_target_pairs={{0,4},{4,0},{8,12},{12,8},{1,5},{5,1},{9,13},{13,9},{2,6},{6,2},{1... | collective-permute-start | bytes 786440 | tf_op jit(solution)/shard_map/ppermute | solution.py:350
  145.8 18.4 %collective-permute-start.30 = (bf16[128,1024]{1,0:T(8,128)(2,1)S(1)}, bf16[128,1024]{1,0:T(8,128)(2,1)S(1)}, u32[]{:S(2)}, u32[]{:S(2)}) collective-permute-start(bf16[128,1024]{1,0:T(8,128)(2,1)S(1)} %bitcast.70), channel_id=1, source_target_pairs={{0,8},{4,12},{8,0},{12,4},{1,9},{5,13},{9,1},{13,5},{2,10},{6,14},... | collective-permute-start | bytes 786440 | tf_op jit(solution)/shard_map/ppermute | solution.py:350
  147.1 23.2 %collective-permute-start.31 = (bf16[128,1024]{1,0:T(8,128)(2,1)S(1)}, bf16[128,1024]{1,0:T(8,128)(2,1)S(1)}, u32[]{:S(2)}, u32[]{:S(2)}) collective-permute-start(bf16[128,1024]{1,0:T(8,128)(2,1)S(1)} %bitcast.69), channel_id=1, source_target_pairs={{0,12},{4,8},{8,4},{12,0},{1,13},{5,9},{9,5},{13,1},{2,14},{6,10},... | collective-permute-start | bytes 786440 | tf_op jit(solution)/shard_map/ppermute | solution.py:350
  162.2 9.7 %collective-permute-start.28 = (f32[2,128,64]{2,1,0:T(8,128)}, f32[2,128,64]{2,1,0:T(8,128)S(1)}, u32[]{:S(2)}, u32[]{:S(2)}) collective-permute-start(f32[2,128,64]{2,1,0:T(8,128)} %shard_map.70), channel_id=1, source_target_pairs={{0,1},{1,0},{2,3},{3,2},{4,5},{5,4},{6,7},{7,6},{8,9},{9,8},{10,11... | collective-permute-start | bytes 196616 | tf_op jit(solution)/shard_map/ppermute | solution.py:363
  171.1 0.9 copy-start.13

commit v4 on v3

--- a/solution.py
+++ b/solution.py
@@ -95,12 +95,12 @@
         out_shape=jax.ShapeDtypeStruct((heads, dim, rank), jnp.float32),
         in_specs=[vmem] * (len(parts) + 1),
         out_specs=vmem,
-        cost_estimate=pl.CostEstimate(flops=heads * dim**3, bytes_accessed=4 * heads * dim * dim, transcendentals=0),
+        cost_estimate=pl.CostEstimate(flops=6000 * heads * dim**3 // 2, bytes_accessed=4 * heads * dim * dim, transcendentals=0),
     )(*parts, basis)
 
 
 ALL_PIECES = [(d, k) for d in (1, 2, 3) for k in range(4)]
-EARLY_PIECES = [(1, 0), (1, 1), (1, 2), (1, 3), (2, 0), (2, 2), (3, 0)]
+EARLY_PIECES = [(1, 0), (1, 1), (1, 2), (1, 3), (2, 0), (2, 1), (2, 2), (2, 3), (3, 0), (3, 2)]
 
 
 def project_kernel(near, widths, last, *refs):
@@ -109,7 +109,7 @@
     own, sib = refs.pop(0), refs.pop(0)
     pieces = {name: refs.pop(0) for name in (ALL_PIECES if last else EARLY_PIECES)}
     if last:
-        acc_in, out_ref, xbuf, wbuf, xsem, wsem, acc, asem = refs
+        acc_in, out_ref, xbuf, wbuf, xsem, wsem, acc = refs
     else:
         acc, xbuf, wbuf, xsem, wsem = refs
     g, s, h, c = (lax.axis_index(a) for a in ("groups", "seq", "head", "sub"))
@@ -134,10 +134,6 @@
         fresh = (n // near == h) | (n - (1 - h) * near < far_early)
         return (have & fresh) != last
 
-    if last:
-        pltpu.make_async_copy(acc_in, acc, asem).start()
-    else:
-        acc[...] = jnp.zeros_like(acc)
     for i in range(near):
         x_copy(x_own.at[:, i * half : (i + 1) * half], h * near + i).start()
     for part in range(2):
@@ -161,8 +157,7 @@
         for i in range(width):
             x_copy(x_far.at[:, i * half : (i + 1) * half], n).start()
             n = n + 1
-    if last:
-        pltpu.make_async_copy(acc_in, acc, asem).wait()
+    acc[...] = acc_in[...] if last else jnp.zeros_like(acc)
 
     @pl.loop(0, near + sum(widths))
     def _(i):
@@ -190,8 +185,9 @@
     near = 2 * feats // block
     widths = [2 * v.shape[1] // block for v in xs]
     given = [pieces[name] for name in (ALL_PIECES if last else EARLY_PIECES)]
-    anywhere = pl.BlockSpec(memory_space=pl.ANY)
-    args = [x, *xs, own, sib, *given] + ([acc] if last else [])
+    hbm, vmem = pl.BlockSpec(memory_space=pltpu.HBM), pl.BlockSpec(memory_space=pltpu.VMEM)
+    args = [pltpu.with_memory_space_constraint(v, pltpu.HBM) for v in (x, *xs, own, sib, *given)]
+    specs = [hbm] * len(args)
     scratch = [
         pltpu.VMEM((tokens, 2 * feats), x.dtype),
         pltpu.VMEM((2 * feats, width), x.dtype),
@@ -199,12 +195,14 @@
         pltpu.SemaphoreType.DMA((2 * near,)),
     ]
     if last:
-        scratch += [pltpu.VMEM((tokens, width), jnp.float32), pltpu.SemaphoreType.DMA]
+        args.append(acc)
+        specs.append(vmem)
+        scratch.append(pltpu.VMEM((tokens, width), jnp.float32))
     return pl.pallas_call(
         functools.partial(project_kernel, near, widths, last),
         out_shape=jax.ShapeDtypeStruct((tokens, width), jnp.bfloat16 if last else jnp.float32),
-        in_specs=[anywhere] * len(args),
-        out_specs=pl.BlockSpec(memory_space=pltpu.VMEM),
+        in_specs=specs,
+        out_specs=vmem,
         scratch_shapes=scratch,
         compiler_params=pltpu.CompilerParams(vmem_limit_bytes=36 << 20),
         cost_estimate=pl.CostEstimate(
@@ -241,7 +239,7 @@
     one = along(unit, (0, 1), (1, 0), (2, 3), (3, 2))
     mid = along(unit, (1, 2), (2, 1))
     x1 = far(part(tie(x), 1))
-    one, mid, x_a = tie((one, mid, x))
+    one, mid, x_a, sib = tie((one, mid, x, sub(own)))
     third = part(x_a, 2)
     mid_two = along(one, (1, 2), (2, 1))
     out_two = along(mid, (1, 0), (2, 3))
@@ -256,22 +254,20 @@
     two_twin = across(two)
     fourth = part(x_b, 3)
     one_sib, one_twin_sib = sub(one_b), sub(one_twin)
-    one_sib, one_twin_sib, own_b, two_b = tie((one_sib, one_twin_sib, own, two))
-    sib, two_sib = sub(own_b), sub(two_b)
-    out_three, x2, two_twin, sib, two_sib, fourth = tie(
-        (out_three, x2, two_twin, sib, two_sib, fourth)
+    out_three, x2, two_twin, one_sib, one_twin_sib, fourth, two_c = tie(
+        (out_three, x2, two_twin, one_sib, one_twin_sib, fourth, two)
     )
     three = jnp.where(inner, mid, out_three)
     twin = across(three)
     x3 = far(fourth)
     moved = {(1, 0): one, (1, 1): one_twin, (1, 2): one_sib, (1, 3): one_twin_sib}
-    moved.update({(2, 0): two, (2, 2): two_sib, (3, 0): three})
+    moved.update({(2, 0): two, (2, 1): two_twin, (3, 0): three})
+    moved.update({(2, 2): sub(two_c), (2, 3): sub(two_twin), (3, 2): sub(three)})
     acc = project(x, [x0, x1, x2], own, sib, moved)
-    moved.update({(2, 1): two_twin, (2, 3): sub(two_twin), (3, 2): sub(three)})
     acc, wanted = tie((acc, wanted))
     lists = jnp.stack([wanted] + [lax.ppermute(wanted, "seq", xor(4, d)) for d in (1, 2, 3)])
     twin_lists = sub(lists)
-    twin, x3 = tie((twin, x3))
+    twin, x3, acc = tie((twin, x3, acc))
     moved.update({(3, 1): twin, (3, 3): sub(twin)})
     return project(x, [x0, x1, x2, x3], own, sib, moved, acc), lists, twin_lists
 
@@ -293,6 +289,47 @@
     return sums.astype(jnp.bfloat16)
 
 
+def finish_kernel(position_ref, mine_ref, other_ref, *refs):
+    got, coeff_ref, value_ref = refs[:-2], refs[-2], refs[-1]
+    rows = jnp.concatenate([r[...] for r in got])
+    tokens, width = rows.shape
+    half = width // 2
+    heads, dim, rank = mine_ref.shape
+    place = lax.broadcasted_iota(jnp.int32, (tokens, tokens), 1)
+    unpick = (position_ref[...] == place).astype(jnp.bfloat16)
+    rows = jnp.dot(unpick, rows, preferred_element_type=jnp.float32)
+    value_ref[...] = rows[:, half:].astype(value_ref.dtype)
+    first = lax.axis_index("sub") == 0
+    maps = [jnp.where(first, mine_ref[i], other_ref[i]) for i in range(heads)]
+    maps += [jnp.where(first, other_ref[i], mine_ref[i]) for i in range(heads)]
+    coeffs = [
+        jnp.dot(
+            rows[:, i * dim : (i + 1) * dim],
+            m,
+            precision=lax.Precision.HIGHEST,
+            preferred_element_type=jnp.float32,
+        )
+        for i, m in enumerate(maps)
+    ]
+    coeff_ref[...] = jnp.concatenate(coeffs, axis=1).astype(coeff_ref.dtype)
+
+
+def finish(position, got, solved, other):
+    heads, dim, rank = solved.shape
+    tokens = position.shape[0]
+    vmem = pl.BlockSpec(memory_space=pltpu.VMEM)
+    return pl.pallas_call(
+        finish_kernel,
+        out_shape=(
+            jax.ShapeDtypeStruct((tokens, 2 * heads * rank), jnp.bfloat16),
+            jax.ShapeDtypeStruct((tokens, 2 * heads * dim), jnp.bfloat16),
+        ),
+        in_specs=[vmem] * (3 + len(got)),
+        out_specs=(vmem, vmem),
+        compiler_params=pltpu.CompilerParams(vmem_limit_bytes=24 << 20),
+    )(position[:, None], solved, other, *got)
+
+
 def spread(order, tokens, share, slot):
     place = lax.iota(jnp.int32, tokens)
     block = slot // tokens
@@ -300,7 +337,7 @@
     position = order(block) * share + jnp.sum(before.astype(jnp.int32), axis=1)
     hits = position[:, None] == place[None, :]
     wanted = jnp.sum(jnp.where(hits, (slot - block * tokens)[:, None], 0), axis=0)
-    return hits.astype(jnp.bfloat16), wanted
+    return position, wanted
 
 
 def selected(asked, rows):
@@ -332,7 +369,7 @@
     basis_here = lax.dynamic_slice_in_dim(basis, c * mine, mine, axis=0)
 
     if seq == 4 and head == 2 and lax.axis_size("groups") == 2 and mine == 2:
-        unpick, wanted = spread(lambda b: b ^ (s * cores + c), tokens, share, slot)
+        position, wanted = spread(lambda b: b ^ (s * cores + c), tokens, share, slot)
         both, lists, twin_lists = gathered_projection(hidden_states, own, wanted)
         packed = pack(local_moments(both, heads, dim).reshape(cores, mine, dim, dim))
         chip = core_split(packed, c)
@@ -342,34 +379,25 @@
         keep = selected(jnp.concatenate(near), both)
         taken = lax.ppermute(give, "sub", SWAP)
         parts = [chip] + [lax.ppermute(chip, "seq", xor(seq, d)) for d in (1, 2, 3)]
-        keep, taken, *parts = lax.optimization_barrier((keep, taken, *parts))
         pairs = jnp.stack(
             [v.reshape(seq, share, 2 * width) for v in (keep, taken)], axis=1
         ).reshape(seq, cores * share, 2 * width)
-        got = jnp.concatenate(
-            [pairs[0]] + [lax.ppermute(pairs[d], "seq", xor(seq, d)) for d in (1, 2, 3)]
-        )
+        got = [pairs[0]] + [lax.ppermute(pairs[d], "seq", xor(seq, d)) for d in (1, 2, 3)]
     else:
-        unpick, wanted = spread(lambda b: b, tokens, share, slot)
+        position, wanted = spread(lambda b: b, tokens, share, slot)
         asked = lax.all_to_all(wanted, ("seq", "sub"), split_axis=0, concat_axis=0, tiled=True)
         both = plain_projection(hidden_states, own)
         chip = core_split(local_moments(both, heads, dim).reshape(cores, mine, dim, dim), c)
         parts = [lax.psum(chip, "seq")]
-        got = lax.all_to_all(
-            selected(asked, both), ("seq", "sub"), split_axis=0, concat_axis=0, tiled=True
-        )
+        got = [
+            lax.all_to_all(
+                selected(asked, both), ("seq", "sub"), split_axis=0, concat_axis=0, tiled=True
+            )
+        ]
 
     solved = solve(parts, basis_here, tokens * peers)
     other = lax.ppermute(solved, "sub", SWAP)
-    maps = jnp.where(c == 0, jnp.concatenate([solved, other]), jnp.concatenate([other, solved]))
-    rows = jnp.dot(unpick, got, preferred_element_type=jnp.float32).astype(jnp.bfloat16)
-    coeffs = jnp.einsum(
-        "thd,hdr->thr",
-        rows[:, :width].astype(jnp.float32).reshape(tokens, heads, dim),
-        maps,
-        precision=lax.Precision.HIGHEST,
-    )
-    return coeffs.reshape(tokens, heads * rank).astype(jnp.bfloat16), rows[:, width:]
+    return finish(position, got, solved, other)
 
 
 def solution(mesh):

time: 175 us -> 173 us (0.989)
  waiting for transfers between devices: 84.3 us -> 76.6 us
  Pallas kernels: 33.5 us -> 40.1 us
  local copies, waits for them, and re-layouts: 11.3 us -> 15.5 us
  starting transfers between devices: 38.5 us -> 35.1 us
    ppermute x5, waiting for transfers between devices: 40 us -> 19.9 us  [along(): return lax.ppermute(value, 'seq', pairs)]
    ppermute x3, waiting for transfers between devices: 6.93 us -> 14.8 us  [across(): return lax.ppermute(value, 'groups', SWAP)]
    ppermute x4, waiting for transfers between devices: 18.8 us -> 24.4 us  [far(): return lax.ppermute(value, 'head', SWAP)]
    slice x4, local copies, waits for them, and re-layouts: 2.6 us -> 8.15 us  [part(): return value[:, bounds[i] * feats // 8:bounds[i + 1] * feats // 8]]
    pallas_call x2, Pallas kernels: 20.4 us -> 24.7 us  [project(): pl.pallas_call(functools.partial(project_kernel, near, widths, last), out...]
    pallas_call x0 -> x1, Pallas kernels: none -> 2.37 us  [finish(): pl.pallas_call(finish_kernel, out_shape=(jax.ShapeDtypeStruct((tokens, 2...]
    ppermute x8, waiting for transfers between devices: 6.28 us -> 4.32 us  [sub(): return lax.ppermute(value, 'sub', SWAP)]
    ppermute x3, waiting for transfers between devices: 6.02 us -> 4.14 us  [per_device(): parts = [chip] + [lax.ppermute(chip, 'seq', xor(seq, d)) for d in (1, 2, 3)]]
  transfers between devices with their start and end apart: 32 -> 32, of which waited for: 15 -> 18; matrix products, arithmetic and copies ran while one was open for 5% -> 6% of each run, Pallas kernels for 14% -> 17%
where the time goes in v4:
time: 173 us
  waiting for transfers between devices  76.6 us (44%)
  Pallas kernels  40.1 us (23%)
  starting transfers between devices  35.1 us (20%)
  local copies, waits for them, and re-layouts  15.5 us (9%)
  other arithmetic  3.5 us (2%)
    pallas_call x2, Pallas kernels, project(): pl.pallas_call(functools.partial(project_kernel, near, widths, last), out...  24.7 us
    ppermute x4, waiting for transfers between devices, far(): return lax.ppermute(value, 'head', SWAP)  24.4 us
    ppermute x5, waiting for transfers between devices, along(): return lax.ppermute(value, 'seq', pairs)  19.9 us
    ppermute x3, waiting for transfers between devices, across(): return lax.ppermute(value, 'groups', SWAP)  14.8 us
    ppermute x5, starting transfers between devices, along(): return lax.ppermute(value, 'seq', pairs)  13.1 us
    pallas_call x1, Pallas kernels, solve(): pl.pallas_call(functools.partial(solve_kernel, 1.0 / token_total, len(par...  13 us
    slice x4, local copies, waits for them, and re-layouts, part(): return value[:, bounds[i] * feats // 8:bounds[i + 1] * feats // 8]  8.15 us
    ppermute x3, waiting for transfers between devices, per_device(): lax.ppermute(pairs[d], 'seq', xor(seq, d))  7.08 us
  transfers between devices with their start and end apart: 32, of which 18 were waited for; matrix products, arithmetic and copies ran while one was open for 6% of the time, Pallas kernels for 17%

profile of v4, /device:TPU:11, one launch (start us, length us, event | category | flops | bytes accessed | tf_op | source)
XLA Modules:
  0.0 173.0 jit_solution(10435074448045397965)
XLA Ops:
  0.7 1.5 constant_dynamic-update-slice_fusion.1
  2.2 0.1 constant_dynamic-update-slice_fusion.refs_4_.refs_5_
  2.4 0.7 collective-permute-start.2
  3.2 0.2 collective-permute-start
  3.4 4.3 %collective-permute-start.1 = (bf16[512,1024]{1,0:T(8,128)(2,1)S(1)}, bf16[512,1024]{1,0:T(8,128)(2,1)}, u32[]{:S(2)}, u32[]{:S(2)}) collective-permute-start(bf16[512,1024]{1,0:T(8,128)(2,1)S(1)} %constant_dynamic-slice_fusion.1), channel_id=1, source_target_pairs={{4,8},{8,4},{5,9},{9,5},{6,10},{10,6},{7,11},{11,7},{20,24},{24,20... | collective-permute-start | bytes 3145736 | tf_op jit(solution)/shard_map/ppermute | solution.py:227
  7.8 2.3 %slice.61 = bf16[512,1024]{1,0:T(8,128)(2,1)} slice(bf16[512,4096]{1,0:T(8,128)(2,1)} %refs_0_.3), slice={[0:512], [0:1024]} | slice | bytes 2097152 | tf_op jit(solution)/shard_map/slice | solution.py:236
  10.0 0.3 collective-permute-start.5
  10.3 2.3 %slice.80 = bf16[512,1024]{1,0:T(8,128)(2,1)} slice(bf16[512,4096]{1,0:T(8,128)(2,1)} %refs_0_.3), slice={[0:512], [1024:2048]} | slice | bytes 2097152 | tf_op jit(solution)/shard_map/slice | solution.py:236
  12.6 1.2 collective-permute-start.6
  13.8 14.3 %collective-permute-done.refs_6_.refs_7_ = bf16[512,1024]{1,0:T(8,128)(2,1)S(1)} collective-permute-done((bf16[512,1024]{1,0:T(8,128)(2,1)S(1)}, bf16[512,1024]{1,0:T(8,128)(2,1)S(1)}, u32[]{:S(2)}, u32[]{:S(2)}) %collective-permute-start) | collective-permute-done | bytes 1048608 | tf_op jit(solution)/shard_map/ppermute | solution.py:227
  28.1 3.0 %collective-permute-done.1 = bf16[512,1024]{1,0:T(8,128)(2,1)} collective-permute-done((bf16[512,1024]{1,0:T(8,128)(2,1)S(1)}, bf16[512,1024]{1,0:T(8,128)(2,1)}, u32[]{:S(2)}, u32[]{:S(2)}) %collective-permute-start.1) | collective-permute-done | bytes 1048608 | tf_op jit(solution)/shard_map/ppermute | solution.py:227
  31.2 3.0 %collective-permute-start.3 = (bf16[512,1024]{1,0:T(8,128)(2,1)S(1)}, bf16[512,1024]{1,0:T(8,128)(2,1)}, u32[]{:S(2)}, u32[]{:S(2)}) collective-permute-start(bf16[512,1024]{1,0:T(8,128)(2,1)S(1)} %collective-permute-done.refs_6_.refs_7_), channel_id=1, source_target_pairs={{4,8},{8,4},{5,9},{9,5},{6,10},{10,6},{7,11},{11,7},{20,24},{24,20... | collective-permute-start | bytes 3145736 | tf_op jit(solution)/shard_map/ppermute | solution.py:227
  34.2 1.3 collective-permute-start.7
  35.5 2.3 %collective-permute-start.4 = (bf16[512,1024]{1,0:T(8,128)(2,1)}, bf16[512,1024]{1,0:T(8,128)(2,1)}, u32[]{:S(2)}, u32[]{:S(2)}) collective-permute-start(bf16[512,1024]{1,0:T(8,128)(2,1)} %collective-permute-done.1), channel_id=1, source_target_pairs={{4,0},{8,12},{5,1},{9,13},{6,2},{10,14},{7,3},{11,15},{20,16},{24,... | collective-permute-start | bytes 3145736 | tf_op jit(solution)/shard_map/ppermute | solution.py:227
  37.8 1.3 slice.63
  39.1 17.9 %collective-permute-done.6.refs_2_ = bf16[512,1024]{1,0:T(8,128)(2,1)} collective-permute-done((bf16[512,1024]{1,0:T(8,128)(2,1)}, bf16[512,1024]{1,0:T(8,128)(2,1)}, u32[]{:S(2)}, u32[]{:S(2)}) %collective-permute-start.6) | collective-permute-done | bytes 1048608 | tf_op jit(solution)/shard_map/ppermute | solution.py:230
  57.0 0.6 collective-permute-done.7.refs_7_.refs_8_
  57.6 0.5 collective-permute-done.4
  58.1 1.3 broadcast_select_fusion.1.refs_10_.refs_11_
  59.5 1.2 collective-permute-start.10
  60.6 3.3 %collective-permute-start.8 = (bf16[512,1024]{1,0:T(8,128)(2,1)}, bf16[512,1024]{1,0:T(8,128)(2,1)S(1)}, u32[]{:S(2)}, u32[]{:S(2)}) collective-permute-start(bf16[512,1024]{1,0:T(8,128)(2,1)} %collective-permute-done.3), channel_id=1, source_target_pairs={{4,0},{8,12},{5,1},{9,13},{6,2},{10,14},{7,3},{11,15},{20,16},{24,... | collective-permute-start | bytes 3145736 | tf_op jit(solution)/shard_map/ppermute | solution.py:227
  63.9 3.0 %collective-permute-start.12 = (bf16[512,1024]{1,0:T(8,128)(2,1)S(1)}, bf16[512,1024]{1,0:T(8,128)(2,1)S(1)}, u32[]{:S(2)}, u32[]{:S(2)}) collective-permute-start(bf16[512,1024]{1,0:T(8,128)(2,1)S(1)} %collective-permute-done.7.refs_7_.refs_8_), channel_id=1, source_target_pairs={{0,1},{1,0},{2,3},{3,2},{4,5},{5,4},{6,7},{7,6},{8,9},{9,8},{10,11... | collective-permute-start | bytes 3145736 | tf_op jit(solution)/shard_map/ppermute | solution.py:221
  67.0 0.3 collective-permute-start.9
  67.2 2.3 %slice.64 = bf16[512,1024]{1,0:T(8,128)(2,1)} slice(bf16[512,4096]{1,0:T(8,128)(2,1)} %refs_0_.3), slice={[0:512], [3072:4096]} | slice | bytes 2097152 | tf_op jit(solution)/shard_map/slice | solution.py:236
  69.5 12.5 %collective-permute-done.10.refs_11_.refs_12_ = bf16[512,1024]{1,0:T(8,128)(2,1)} collective-permute-done((bf16[512,1024]{1,0:T(8,128)(2,1)S(1)}, bf16[512,1024]{1,0:T(8,128)(2,1)}, u32[]{:S(2)}, u32[]{:S(2)}) %collective-permute-start.10) | collective-permute-done | bytes 1048608 | tf_op jit(solution)/shard_map/ppermute | solution.py:224
  82.0 2.0 %collective-permute-done.8 = bf16[512,1024]{1,0:T(8,128)(2,1)S(1)} collective-permute-done((bf16[512,1024]{1,0:T(8,128)(2,1)}, bf16[512,1024]{1,0:T(8,128)(2,1)S(1)}, u32[]{:S(2)}, u32[]{:S(2)}) %collective-permute-start.8) | collective-permute-done | bytes 1048608 | tf_op jit(solution)/shard_map/ppermute | solution.py:227
  84.0 1.0 copy-done.7
  85.0 1.0 copy-done.8
  86.0 5.4 %collective-permute-done.9.refs_3_ = bf16[512,1024]{1,0:T(8,128)(2,1)} collective-permute-done((bf16[512,1024]{1,0:T(8,128)(2,1)S(1)}, bf16[512,1024]{1,0:T(8,128)(2,1)}, u32[]{:S(2)}, u32[]{:S(2)}) %collective-permute-start.9) | collective-permute-done | bytes 1048608 | tf_op jit(solution)/shard_map/ppermute | solution.py:230
  91.4 1.3 broadcast_select_fusion.refs_14_.refs_15_
  92.7 1.3 collective-permute-start.17
  94.2 0.4 collective-permute-start.16
  94.6 0.8 copy.32.refs_4_
  95.4 0.2 convert_reduce_fusion
  95.6 1.3 collective-permute-start.13
  96.9 0.3 collective-permute-start.14
  97.2 0.2 select_reduce_fusion
  97.5 1.9 %collective-permute-done.15.refs_12_.refs_13_ = bf16[512,1024]{1,0:T(8,128)(2,1)} collective-permute-done((bf16[512,1024]{1,0:T(8,128)(2,1)S(1)}, bf16[512,1024]{1,0:T(8,128)(2,1)}, u32[]{:S(2)}, u32[]{:S(2)}) %collective-permute-start.15) | collective-permute-done | bytes 1048608 | tf_op jit(solution)/shard_map/ppermute | solution.py:221
  99.4 0.3 collective-permute-done.16.refs_13_.refs_14_
  99.7 16.3 %shard_map.68.refs_19_ = f32[512,1024]{1,0:T(8,128)S(1)} custom-call(bf16[512,4096]{1,0:T(8,128)(2,1)} %refs_0_.3, bf16[512,1024]{1,0:T(8,128)(2,1)} %collective-permute-done.5.refs_1_, bf16[512,1024]{1,0:T(8,128)(2,1)} %collective-permute-done.6.refs_2_, bf16[512,1024]{1,0:T(8,128)(2,1)} %collective-permute-done.9.refs_3_, bf16[1024,1024]{1,0:T(8,128)(2,1)} %copy-done.2, ...), custom_call_target="tpu_custom_call" | custom-call | flops 4294967296 | bytes 16777216 | tf_op jit(solution)/shard_map/pallas_call | solution.py:201
  116.2 2.6 %collective-permute-start.24 = (s32[512]{0:T(512)S(1)}, s32[512]{0:T(512)S(1)}, u32[]{:S(2)}, u32[]{:S(2)}) collective-permute-start(s32[512]{0:T(512)S(1)} %select_reduce_fusion), channel_id=1, source_target_pairs={{0,4},{4,0},{8,12},{12,8},{1,5},{5,1},{9,13},{13,9},{2,6},{6,2},{1... | collective-permute-start | bytes 6152 | tf_op jit(solution)/shard_map/ppermute | solution.py:268
  118.7 1.7 collective-permute-done.13.refs_16_
  120.4 1.1 collective-permute-done.14.refs_4_
  121.6 1.2 collective-permute-start.18
  123.0 2.1 %collective-permute-done.27 = s32[4,512]{1,0:T(4,128)S(1)} collective-permute-done((s32[4,512]{1,0:T(4,128)S(1)}, s32[4,512]{1,0:T(4,128)S(1)}, u32[]{:S(2)}, u32[]{:S(2)}) %collective-permute-start.27) | collective-permute-done | bytes 8224 | tf_op jit(solution)/shard_map/ppermute | solution.py:221
  125.2 1.0 copy-done.12
  126.2 8.4 %shard_map.69 = bf16[512,1024]{1,0:T(8,128)(2,1)S(1)} custom-call(bf16[512,4096]{1,0:T(8,128)(2,1)} %refs_0_.3, bf16[512,1024]{1,0:T(8,128)(2,1)} %collective-permute-done.5.refs_1_, bf16[512,1024]{1,0:T(8,128)(2,1)} %collective-permute-done.6.refs_2_, bf16[512,1024]{1,0:T(8,128)(2,1)} %collective-permute-done.9.refs_3_, bf16[512,1024]{1,0:T(8,128)(2,1)} %copy-done.11, ...), custom_call_target="tpu_custom_call" | custom-call | flops 4294967296 | bytes 16777216 | tf_op jit(solution)/shard_map/pallas_call | solution.py:201
  134.6 0.3 fusion.1
  135.0 0.5 convolution_convert_fusion
  135.6 0.6 collective-permute-start.19
  136.2 0.5 convolution_convert_fusion.1
  136.7 0.9 collective-permute-done.19
  137.7 2.6 %collective-permute-start.22 = (f32[136,128]{1,0:T(8,128)S(1)}, f32[136,128]{1,0:T(8,128)S(1)}, u32[]{:S(2)}, u32[]{:S(2)}) collective-permute-start(f32[136,128]{1,0:T(8,128)S(1)} %fusion.14.refs_0_), channel_id=1, source_target_pairs={{0,12},{4,8},{8,4},{12,0},{1,13},{5,9},{9,5},{13,1},{2,14},{6,10},... | collective-permute-start | bytes 208904 | tf_op jit(solution)/shard_map/ppermute | solution.py:381
  140.4 1.0 collective-permute-start.29
  141.4 0.2 collective-permute-start.30
  141.6 1.5 collective-permute-start.31
  143.1 4.1 %collective-permute-done.22.refs_3_ = f32[136,128]{1,0:T(8,128)S(1)} collective-permute-done((f32[136,128]{1,0:T(8,128)S(1)}, f32[136,128]{1,0:T(8,128)S(1)}, u32[]{:S(2)}, u32[]{:S(2)}) %collective-permute-start.22) | collective-permute-done | bytes 69664 | tf_op jit(solution)/shard_map/ppermute | solution.py:381
  147.3 0.6 copy-done.18
  147.9 13.0 %shard_map.70.mine_ref = f32[2,128,64]{2,1,0:T(8,128)} custom-call(f32[136,128]{1,0:T(8,128)} %copy-done.14, f32[136,128]{1,0:T(8,128)} %copy-done.16, f32[136,128]{1,0:T(8,128)} %copy-done.17, f32[136,128]{1,0:T(8,128)} %copy-done.18, f32[2,128,64]{2,1,0:T(8,128)} %copy.32.refs_4_), custom_call_target="tpu_custom_call" | custom-call | flops 12582912000 | bytes 131072 | tf_op jit(solution)/shard_map/pallas_call | solution.py:93
  160.9 0.6 collective-permute-start.23
  161.6 1.0 collective-permute-done.23.other_ref
  162.7 7.1 %collective-permute-done.31.refs_3_ = bf16[128,1024]{1,0:T(8,128)(2,1)S(1)} collective-permute-done((bf16[128,1024]{1,0:T(8,128)(2,1)S(1)}, bf16[128,1024]{1,0:T(8,128)(2,1)S(1)}, u32[]{:S(2)}, u32[]{:S(2)}) %collective-permute-start.31) | collective-permute-done | bytes 262176 | tf_op jit(solution)/shard_map/ppermute | solution.py:385
  169.7 0.9 copy-done.1
  170.7 2.4 %shard_map.71 = (bf16[512,256]{1,0:T(8,128)(2,1)}, bf16[512,512]{1,0:T(8,128)(2,1)}) custom-call(s32[512,1]{1,0:T(8,128)S(1)} %copy.29.position_ref, f32[2,128,64]{2,1,0:T(8,128)S(1)} %copy-done.1, f32[2,128,64]{2,1,0:T(8,128)S(1)} %collective-permute-done.23.other_ref, bf16[128,1024]{1,0:T(8,128)(2,1)S(1)} %bitcast.61, ...), custom_call_target="tpu_custom_call" | custom-call | tf_op jit(solution)/shard_map/pallas_call | solution.py:321
  (75 shorter events, 1.5 us)
Async XLA Ops:
  0.6 94.0 %copy-start = (f32[4,128,64]{1,2,0:T(8,128)S(1)}, f32[4,128,64]{1,2,0:T(8,128)}, u32[]{:S(2)}) copy-start(f32[4,128,64]{1,2,0:T(8,128)} %param.8) | copy-start | bytes 393220
  0.6 1.6 copy-start.13
  2.4 7.7 %copy-start.2 = (bf16[1024,1024]{1,0:T(8,128)(2,1)}, bf16[1024,1024]{1,0:T(8,128)(2,1)S(1)}, u32[]{:S(2)}) copy-start(bf16[1024,1024]{1,0:T(8,128)(2,1)S(1)} %constant_dynamic-update-slice_fusion.refs_4_.refs_5_) | copy-start | bytes 6291460
  2.4 28.8 %collective-permute-start.2 = (bf16[1024,1024]{1,0:T(8,128)(2,1)S(1)}, bf16[1024,1024]{1,0:T(8,128)(2,1)}, u32[]{:S(2)}, u32[]{:S(2)}) collective-permute-start(bf16[1024,1024]{1,0:T(8,128)(2,1)S(1)} %constant_dynamic-update-slice_fusion.refs_4_.refs_5_), channel_id=1, source_target_pairs={{0,1},{1,0},{2,3},{3,2},{4,5},{5,4},{6,7},{7,6},{8,9},{9,8},{10,11... | collective-permute-start | bytes 6291464 | tf_op jit(solution)/shard_map/ppermute | solution.py:221
  3.2 24.9 %collective-permute-start = (bf16[512,1024]{1,0:T(8,128)(2,1)S(1)}, bf16[512,1024]{1,0:T(8,128)(2,1)S(1)}, u32[]{:S(2)}, u32[]{:S(2)}) collective-permute-start(bf16[512,1024]{1,0:T(8,128)(2,1)S(1)} %constant_dynamic-slice_fusion.1), channel_id=1, source_target_pairs={{0,4},{4,0},{8,12},{12,8},{1,5},{5,1},{9,13},{13,9},{2,6},{6,2},{1... | collective-permute-start | bytes 3145736 | tf_op jit(solution)/shard_map/ppermute | solution.py:227
  3.4 27.7 %collective-permute-start.1 = (bf16[512,1024]{1,0:T(8,128)(2,1)S(1)}, bf16[512,1024]{1,0:T(8,128)(2,1)}, u32[]{:S(2)}, u32[]{:S(2)}) collective-permute-start(bf16[512,1024]{1,0:T(8,128)(2,1)S(1)} %constant_dynamic-slice_fusion.1), channel_id=1, source_target_pairs={{4,8},{8,4},{5,9},{9,5},{6,10},{10,6},{7,11},{11,7},{20,24},{24,20... | collective-permute-start | bytes 3145736 | tf_op jit(solution)/shard_map/ppermute | solution.py:227
  10.0 29.0 %collective-permute-start.5 = (bf16[512,1024]{1,0:T(8,128)(2,1)}, bf16[512,1024]{1,0:T(8,128)(2,1)}, u32[]{:S(2)}, u32[]{:S(2)}) collective-permute-start(bf16[512,1024]{1,0:T(8,128)(2,1)} %slice.61), channel_id=1, source_target_pairs={{0,2},{2,0},{1,3},{3,1},{4,6},{6,4},{5,7},{7,5},{8,10},{10,8},{9,1... | collective-permute-start | bytes 3145736 | tf_op jit(solution)/shard_map/ppermute | solution.py:230
  12.6 44.3 %collective-permute-start.6 = (bf16[512,1024]{1,0:T(8,128)(2,1)}, bf16[512,1024]{1,0:T(8,128)(2,1)}, u32[]{:S(2)}, u32[]{:S(2)}) collective-permute-start(bf16[512,1024]{1,0:T(8,128)(2,1)} %slice.80), channel_id=1, source_target_pairs={{0,2},{2,0},{1,3},{3,1},{4,6},{6,4},{5,7},{7,5},{8,10},{10,8},{9,1... | collective-permute-start | bytes 3145736 | tf_op jit(solution)/shard_map/ppermute | solution.py:230
  28.1 38.8 %copy-start.5 = (bf16[512,1024]{1,0:T(8,128)(2,1)}, bf16[512,1024]{1,0:T(8,128)(2,1)S(1)}, u32[]{:S(2)}) copy-start(bf16[512,1024]{1,0:T(8,128)(2,1)S(1)} %collective-permute-done.refs_6_.refs_7_) | copy-start | bytes 3145732
  31.2 25.9 %collective-permute-start.3 = (bf16[512,1024]{1,0:T(8,128)(2,1)S(1)}, bf16[512,1024]{1,0:T(8,128)(2,1)}, u32[]{:S(2)}, u32[]{:S(2)}) collective-permute-start(bf16[512,1024]{1,0:T(8,128)(2,1)S(1)} %collective-permute-done.refs_6_.refs_7_), channel_id=1, source_target_pairs={{4,8},{8,4},{5,9},{9,5},{6,10},{10,6},{7,11},{11,7},{20,24},{24,20... | collective-permute-start | bytes 3145736 | tf_op jit(solution)/shard_map/ppermute | solution.py:227
  34.2 23.4 %collective-permute-start.7 = (bf16[512,1024]{1,0:T(8,128)(2,1)S(1)}, bf16[512,1024]{1,0:T(8,128)(2,1)S(1)}, u32[]{:S(2)}, u32[]{:S(2)}) collective-permute-start(bf16[512,1024]{1,0:T(8,128)(2,1)S(1)} %collective-permute-done.refs_6_.refs_7_), channel_id=1, source_target_pairs={{0,16},{16,0},{1,17},{17,1},{2,18},{18,2},{3,19},{19,3},{4,20},{20... | collective-permute-start | bytes 3145736 | tf_op jit(solution)/shard_map/ppermute | solution.py:224
  35.5 22.6 %collective-permute-start.4 = (bf16[512,1024]{1,0:T(8,128)(2,1)}, bf16[512,1024]{1,0:T(8,128)(2,1)}, u32[]{:S(2)}, u32[]{:S(2)}) collective-permute-start(bf16[512,1024]{1,0:T(8,128)(2,1)} %collective-permute-done.1), channel_id=1, source_target_pairs={{4,0},{8,12},{5,1},{9,13},{6,2},{10,14},{7,3},{11,15},{20,16},{24,... | collective-permute-start | bytes 3145736 | tf_op jit(solution)/shard_map/ppermute | solution.py:227
  57.6 11.9 %copy-start.6 = (bf16[512,1024]{1,0:T(8,128)(2,1)}, bf16[512,1024]{1,0:T(8,128)(2,1)S(1)}, u32[]{:S(2)}) copy-start(bf16[512,1024]{1,0:T(8,128)(2,1)S(1)} %collective-permute-done.7.refs_7_.refs_8_) | copy-start | bytes 3145732
  59.5 34.6 %copy-start.3 = (bf16[512,1024]{1,0:T(8,128)(2,1)}, bf16[512,1024]{1,0:T(8,128)(2,1)S(1)}, u32[]{:S(2)}) copy-start(bf16[512,1024]{1,0:T(8,128)(2,1)S(1)} %broadcast_select_fusion.1.refs_10_.refs_11_) | copy-start | bytes 3145732
  59.5 22.5 %collective-permute-start.10 = (bf16[512,1024]{1,0:T(8,128)(2,1)S(1)}, bf16[512,1024]{1,0:T(8,128)(2,1)}, u32[]{:S(2)}, u32[]{:S(2)}) collective-permute-start(bf16[512,1024]{1,0:T(8,128)(2,1)S(1)} %broadcast_select_fusion.1.refs_10_.refs_11_), channel_id=1, source_target_pairs={{0,16},{16,0},{1,17},{17,1},{2,18},{18,2},{3,19},{19,3},{4,20},{20... | collective-permute-start | bytes 3145736 | tf_op jit(solution)/shard_map/ppermute | solution.py:224
  60.6 23.4 %collective-permute-start.8 = (bf16[512,1024]{1,0:T(8,128)(2,1)}, bf16[512,1024]{1,0:T(8,128)(2,1)S(1)}, u32[]{:S(2)}, u32[]{:S(2)}) collective-permute-start(bf16[512,1024]{1,0:T(8,128)(2,1)} %collective-permute-done.3), channel_id=1, source_target_pairs={{4,0},{8,12},{5,1},{9,13},{6,2},{10,14},{7,3},{11,15},{20,16},{24,... | collective-permute-start | bytes 3145736 | tf_op jit(solution)/shard_map/ppermute | solution.py:227
  63.9 20.1 %collective-permute-start.12 = (bf16[512,1024]{1,0:T(8,128)(2,1)S(1)}, bf16[512,1024]{1,0:T(8,128)(2,1)S(1)}, u32[]{:S(2)}, u32[]{:S(2)}) collective-permute-start(bf16[512,1024]{1,0:T(8,128)(2,1)S(1)} %collective-permute-done.7.refs_7_.refs_8_), channel_id=1, source_target_pairs={{0,1},{1,0},{2,3},{3,2},{4,5},{5,4},{6,7},{7,6},{8,9},{9,8},{10,11... | collective-permute-start | bytes 3145736 | tf_op jit(solution)/shard_map/ppermute | solution.py:221
  66.9 17.1 %collective-permute-start.11 = (bf16[512,1024]{1,0:T(8,128)(2,1)S(1)}, bf16[512,1024]{1,0:T(8,128)(2,1)S(1)}, u32[]{:S(2)}, u32[]{:S(2)}) collective-permute-start(bf16[512,1024]{1,0:T(8,128)(2,1)S(1)} %collective-permute-done.refs_6_.refs_7_), channel_id=1, source_target_pairs={{0,1},{1,0},{2,3},{3,2},{4,5},{5,4},{6,7},{7,6},{8,9},{9,8},{10,11... | collective-permute-start | bytes 3145736 | tf_op jit(solution)/shard_map/ppermute | solution.py:221
  67.0 24.4 %collective-permute-start.9 = (bf16[512,1024]{1,0:T(8,128)(2,1)S(1)}, bf16[512,1024]{1,0:T(8,128)(2,1)}, u32[]{:S(2)}, u32[]{:S(2)}) collective-permute-start(bf16[512,1024]{1,0:T(8,128)(2,1)S(1)} %slice.63), channel_id=1, source_target_pairs={{0,2},{2,0},{1,3},{3,1},{4,6},{6,4},{5,7},{7,5},{8,10},{10,8},{9,1... | collective-permute-start | bytes 3145736 | tf_op jit(solution)/shard_map/ppermute | solution.py:230
  69.5 25.9 %copy-start.15 = (s32[512]{0:T(512)S(1)}, s32[512]{0:T(512)}, u32[]{:S(2)}) copy-start(s32[512]{0:T(512)} %param.9) | copy-start | bytes 6148
  84.0 1.0 copy-start.7
  85.0 1.0 copy-start.8
  92.7 7.0 %copy-start.4 = (bf16[512,1024]{1,0:T(8,128)(2,1)}, bf16[512,1024]{1,0:T(8,128)(2,1)S(1)}, u32[]{:S(2)}) copy-start(bf16[512,1024]{1,0:T(8,128)(2,1)S(1)} %broadcast_select_fusion.refs_14_.refs_15_) | copy-start | bytes 3145732
  92.7 4.7 %collective-permute-start.17 = (bf16[512,1024]{1,0:T(8,128)(2,1)S(1)}, bf16[512,1024]{1,0:T(8,128)(2,1)S(1)}, u32[]{:S(2)}, u32[]{:S(2)}) collective-permute-start(bf16[512,1024]{1,0:T(8,128)(2,1)S(1)} %broadcast_select_fusion.refs_14_.refs_15_), channel_id=1, source_target_pairs={{0,1},{1,0},{2,3},{3,2},{4,5},{5,4},{6,7},{7,6},{8,9},{9,8},{10,11... | collective-permute-start | bytes 3145736 | tf_op jit(solution)/shard_map/ppermute | solution.py:221
  94.1 5.3 %collective-permute-start.15 = (bf16[512,1024]{1,0:T(8,128)(2,1)S(1)}, bf16[512,1024]{1,0:T(8,128)(2,1)}, u32[]{:S(2)}, u32[]{:S(2)}) collective-permute-start(bf16[512,1024]{1,0:T(8,128)(2,1)S(1)} %broadcast_select_fusion.1.refs_10_.refs_11_), channel_id=1, source_target_pairs={{0,1},{1,0},{2,3},{3,2},{4,5},{5,4},{6,7},{7,6},{8,9},{9,8},{10,11... | collective-permute-start | bytes 3145736 | tf_op jit(solution)/shard_map/ppermute | solution.py:221
  94.2 5.5 %collective-permute-start.16 = (bf16[512,1024]{1,0:T(8,128)(2,1)}, bf16[512,1024]{1,0:T(8,128)(2,1)}, u32[]{:S(2)}, u32[]{:S(2)}) collective-permute-start(bf16[512,1024]{1,0:T(8,128)(2,1)} %collective-permute-done.10.refs_11_.refs_12_), channel_id=1, source_target_pairs={{0,1},{1,0},{2,3},{3,2},{4,5},{5,4},{6,7},{7,6},{8,9},{9,8},{10,11... | collective-permute-start | bytes 3145736 | tf_op jit(solution)/shard_map/ppermute | solution.py:221
  95.6 24.8 %collective-permute-start.13 = (bf16[512,1024]{1,0:T(8,128)(2,1)S(1)}, bf16[512,1024]{1,0:T(8,128)(2,1)S(1)}, u32[]{:S(2)}, u32[]{:S(2)}) collective-permute-start(bf16[512,1024]{1,0:T(8,128)(2,1)S(1)} %broadcast_select_fusion.refs_14_.refs_15_), channel_id=1, source_target_pairs={{0,16},{16,0},{1,17},{17,1},{2,18},{18,2},{3,19},{19,3},{4,20},{20... | collective-permute-start | bytes 3145736 | tf_op jit(solution)/shard_map/ppermute | solution.py:224
  96.9 24.6 %collective-permute-start.14 = (bf16[512,1024]{1,0:T(8,128)(2,1)}, bf16[512,1024]{1,0:T(8,128)(2,1)S(1)}, u32[]{:S(2)}, u32[]{:S(2)}) collective-permute-start(bf16[512,1024]{1,0:T(8,128)(2,1)} %slice.64), channel_id=1, source_target_pairs={{0,2},{2,0},{1,3},{3,1},{4,6},{6,4},{5,7},{7,5},{8,10},{10,8},{9,1... | collective-permute-start | bytes 3145736 | tf_op jit(solution)/shard_map/ppermute | solution.py:230
  97.5 2.2 %copy-start.9 = (bf16[512,1024]{1,0:T(8,128)(2,1)}, bf16[512,1024]{1,0:T(8,128)(2,1)S(1)}, u32[]{:S(2)}) copy-start(bf16[512,1024]{1,0:T(8,128)(2,1)S(1)} %collective-permute-done.17.refs_15_.refs_17_) | copy-start | bytes 3145732
  116.0 6.7 %collective-permute-start.26 = (s32[512]{0:T(512)S(1)}, s32[512]{0:T(512)S(1)}, u32[]{:S(2)}, u32[]{:S(2)}) collective-permute-start(s32[512]{0:T(512)S(1)} %select_reduce_fusion), channel_id=1, source_target_pairs={{0,12},{4,8},{8,4},{12,0},{1,13},{5,9},{9,5},{13,1},{2,14},{6,10},... | collective-permute-start | bytes 6152 | tf_op jit(solution)/shard_map/ppermute | solution.py:268
  116.1 6.7 %collective-permute-start.25 = (s32[512]{0:T(512)S(1)}, s32[512]{0:T(512)S(1)}, u32[]{:S(2)}, u32[]{:S(2)}) collective-permute-start(s32[512]{0:T(512)S(1)} %select_reduce_fusion), channel_id=1, source_target_pairs={{0,8},{4,12},{8,0},{12,4},{1,9},{5,13},{9,1},{13,5},{2,10},{6,14},... | collective-permute-start | bytes 6152 | tf_op jit(solution)/shard_map/ppermute | solution.py:268
  116.2 6.6 %collective-permute-start.24 = (s32[512]{0:T(512)S(1)}, s32[512]{0:T(512)S(1)}, u32[]{:S(2)}, u32[]{:S(2)}) collective-permute-start(s32[512]{0:T(512)S(1)} %select_reduce_fusion), channel_id=1, source_target_pairs={{0,4},{4,0},{8,12},{12,8},{1,5},{5,1},{9,13},{13,9},{2,6},{6,2},{1... | collective-permute-start | bytes 6152 | tf_op jit(solution)/shard_map/ppermute | solution.py:268
  120.4 4.8 %copy-start.10 = (bf16[512,1024]{1,0:T(8,128)(2,1)}, bf16[512,1024]{1,0:T(8,128)(2,1)S(1)}, u32[]{:S(2)}) copy-start(bf16[512,1024]{1,0:T(8,128)(2,1)S(1)} %collective-permute-done.13.refs_16_) | copy-start | bytes 3145732
  121.5 3.6 %copy-start.11 = (bf16[512,1024]{1,0:T(8,128)(2,1)}, bf16[512,1024]{1,0:T(8,128)(2,1)S(1)}, u32[]{:S(2)}) copy-start(bf16[512,1024]{1,0:T(8,128)(2,1)S(1)} %collective-permute-done.14.refs_4_) | copy-start | bytes 3145732
  121.6 3.6 %collective-permute-start.18 = (bf16[512,1024]{1,0:T(8,128)(2,1)S(1)}, bf16[512,1024]{1,0:T(8,128)(2,1)S(1)}, u32[]{:S(2)}, u32[]{:S(2)}) collective-permute-start(bf16[512,1024]{1,0:T(8,128)(2,1)S(1)} %collective-permute-done.13.refs_16_), channel_id=1, source_target_pairs={{0,1},{1,0},{2,3},{3,2},{4,5},{5,4},{6,7},{7,6},{8,9},{9,8},{10,11... | collective-permute-start | bytes 3145736 | tf_op jit(solution)/shard_map/ppermute | solution.py:221
  122.8 2.3 %collective-permute-start.27 = (s32[4,512]{1,0:T(4,128)S(1)}, s32[4,512]{1,0:T(4,128)S(1)}, u32[]{:S(2)}, u32[]{:S(2)}) collective-permute-start(s32[4,512]{1,0:T(4,128)S(1)} %pad_add_fusion), channel_id=1, source_target_pairs={{0,1},{1,0},{2,3},{3,2},{4,5},{5,4},{6,7},{7,6},{8,9},{9,8},{10,11... | collective-permute-start | bytes 24584 | tf_op jit(solution)/shard_map/ppermute | solution.py:221
  125.2 1.0 copy-start.12
  135.5 4.8 %collective-permute-start.28 = (bf16[256,1024]{1,0:T(8,128)(2,1)S(1)}, bf16[256,1024]{1,0:T(8,128)(2,1)S(1)}, u32[]{:S(2)}, u32[]{:S(2)}) collective-permute-start(bf16[256,1024]{1,0:T(8,128)(2,1)S(1)} %convolution_convert_fusion), channel_id=1, source_target_pairs={{0,1},{1,0},{2,3},{3,2},{4,5},{5,4},{6,7},{7,6},{8,9},{9,8},{10,11... | collective-permute-start | bytes 1572872 | tf_op jit(solution)/shard_map/ppermute | solution.py:380
  135.6 1.9 %collective-permute-start.19 = (f32[136,128]{1,0:T(8,128)S(1)}, f32[136,128]{1,0:T(8,128)S(1)}, u32[]{:S(2)}, u32[]{:S(2)}) collective-permute-start(f32[136,128]{1,0:T(8,128)S(1)} %fusion.11), channel_id=1, source_target_pairs={{0,1},{1,0},{2,3},{3,2},{4,5},{5,4},{6,7},{7,6},{8,9},{9,8},{10,11... | collective-permute-start | bytes 208904 | tf_op jit(solution)/shard_map/ppermute | solution.py:356
  137.5 9.7 %copy-start.14 = (f32[136,128]{1,0:T(8,128)}, f32[136,128]{1,0:T(8,128)S(1)}, u32[]{:S(2)}) copy-start(f32[136,128]{1,0:T(8,128)S(1)} %fusion.14.refs_0_) | copy-start | bytes 208900
  137.6 4.1 %collective-permute-start.20 = (f32[136,128]{1,0:T(8,128)S(1)}, f32[136,128]{1,0:T(8,128)S(1)}, u32[]{:S(2)}, u32[]{:S(2)}) collective-permute-start(f32[136,128]{1,0:T(8,128)S(1)} %fusion.14.refs_0_), channel_id=1, source_target_pairs={{0,4},{4,0},{8,12},{12,8},{1,5},{5,1},{9,13},{13,9},{2,6},{6,2},{1... | collective-permute-start | bytes 208904 | tf_op jit(solution)/shard_map/ppermute | solution.py:381
  137.6 5.5 %collective-permute-start.21 = (f32[136,128]{1,0:T(8,128)S(1)}, f32[136,128]{1,0:T(8,128)S(1)}, u32[]{:S(2)}, u32[]{:S(2)}) collective-permute-start(f32[136,128]{1,0:T(8,128)S(1)} %fusion.14.refs_0_), channel_id=1, source_target_pairs={{0,8},{4,12},{8,0},{12,4},{1,9},{5,13},{9,1},{13,5},{2,10},{6,14},... | collective-permute-start | bytes 208904 | tf_op jit(solution)/shard_map/ppermute | solution.py:381
  137.7 9.5 %collective-permute-start.22 = (f32[136,128]{1,0:T(8,128)S(1)}, f32[136,128]{1,0:T(8,128)S(1)}, u32[]{:S(2)}, u32[]{:S(2)}) collective-permute-start(f32[136,128]{1,0:T(8,128)S(1)} %fusion.14.refs_0_), channel_id=1, source_target_pairs={{0,12},{4,8},{8,4},{12,0},{1,13},{5,9},{9,5},{13,1},{2,14},{6,10},... | collective-permute-start | bytes 208904 | tf_op jit(solution)/shard_map/ppermute | solution.py:381
  140.4 22.3 %collective-permute-start.29 = (bf16[128,1024]{1,0:T(8,128)(2,1)S(1)}, bf16[128,1024]{1,0:T(8,128)(2,1)S(1)}, u32[]{:S(2)}, u32[]{:S(2)}) collective-permute-start(bf16[128,1024]{1,0:T(8,128)(2,1)S(1)} %bitcast.67), channel_id=1, source_target_pairs={{0,4},{4,0},{8,12},{12,8},{1,5},{5,1},{9,13},{13,9},{2,6},{6,2},{1... | collective-permute-start | bytes 786440 | tf_op jit(solution)/shard_map/ppermute | solution.py:385
  141.4 21.3 %collective-permute-start.30 = (bf16[128,1024]{1,0:T(8,128)(2,1)S(1)}, bf16[128,1024]{1,0:T(8,128)(2,1)S(1)}, u32[]{:S(2)}, u32[]{:S(2)}) collective-permute-start(bf16[128,1024]{1,0:T(8,128)(2,1)S(1)} %bitcast.66), channel_id=1, source_target_pairs={{0,8},{4,12},{8,0},{12,4},{1,9},{5,13},{9,1},{13,5},{2,10},{6,14},... | collective-permute-start | bytes 786440 | tf_op jit(solution)/shard_map/ppermute | solution.py:385
  141.6 5.6 %copy-start.16 = (f32[136,128]{1,0:T(8,128)}, f32[136,128]{1,0:T(8,128)S(1)}, u32[]{:S(2)}) copy-start(f32[136,128]{1,0:T(8,128)S(1)} %collective-permute-done.20.refs_1_) | copy-start | bytes 208900
  141.6 28.1 %collective-permute-start.31 = (bf16[128,1024]{1,0:T(8,128)(2,1)S(1)}, bf16[128,1024]{1,0:T(8,128)(2,1)S(1)}, u32[]{:S(2)}, u32[]{:S(2)}) collective-permute-start(bf16[128,1024]{1,0:T(8,128)(2,1)S(1)} %bitcast.65), channel_id=1, source_target_pairs={{0,12},{4,8},{8,4},{12,0},{1,13},{5,9},{9,5},{13,1},{2,14},{6,10},... | collective-permute-start | bytes 786440 | tf_op jit(solution)/shard_map/ppermute | solution.py:385
  143.1 4.1 %copy-start.17 = (f32[136,128]{1,0:T(8,128)}, f32[136,128]{1,0:T(8,128)S(1)}, u32[]{:S(2)}) copy-start(f32[136,128]{1,0:T(8,128)S(1)} %collective-permute-done.21.refs_2_) | copy-start | bytes 208900
  147.2 0.6 copy-start.18
  160.9 1.8 %collective-permute-start.23 = (f32[2,128,64]{2,1,0:T(8,128)}, f32[2,128,64]{2,1,0:T(8,128)S(1)}, u32[]{:S(2)}, u32[]{:S(2)}) collective-permute-start(f32[2,128,64]{2,1,0:T(8,128)} %shard_map.70.mine_ref), channel_id=1, source_target_pairs={{0,1},{1,0},{2,3},{3,2},{4,5},{5,4},{6,7},{7,6},{8,9},{9,8},{10,11... | collective-permute-start | bytes 196616 | tf_op jit(solution)/shard_map/ppermute | solution.py:399
  169.7 0.9 copy-start.1

commit v5 on v4

--- a/solution.py
+++ b/solution.py
@@ -135,7 +135,11 @@
         return (have & fresh) != last
 
     for i in range(near):
-        x_copy(x_own.at[:, i * half : (i + 1) * half], h * near + i).start()
+
+        @pl.when(needed(h * near + i))
+        def _():
+            x_copy(x_own.at[:, i * half : (i + 1) * half], h * near + i).start()
+
     for part in range(2):
         for core, src in ((c, own), (1 - c, sib)):
             n = s * 4 + core * 2 + part
@@ -155,17 +159,21 @@
     n = (1 - h) * near
     for x_far, width in zip(xs, widths):
         for i in range(width):
-            x_copy(x_far.at[:, i * half : (i + 1) * half], n).start()
+
+            @pl.when(needed(n))
+            def _():
+                x_copy(x_far.at[:, i * half : (i + 1) * half], n).start()
+
             n = n + 1
     acc[...] = acc_in[...] if last else jnp.zeros_like(acc)
 
     @pl.loop(0, near + sum(widths))
     def _(i):
         n = lax.rem(i + h * near, count)
-        x_copy(x_own.at[:, :half], n).wait()
 
         @pl.when(needed(n))
         def _():
+            x_copy(x_own.at[:, :half], n).wait()
             w_copy(own.at[pl.ds(0, half)], n).wait()
             off = pl.multiple_of(n * half, half)
             acc[...] += jnp.dot(
@@ -186,7 +194,10 @@
     widths = [2 * v.shape[1] // block for v in xs]
     given = [pieces[name] for name in (ALL_PIECES if last else EARLY_PIECES)]
     hbm, vmem = pl.BlockSpec(memory_space=pltpu.HBM), pl.BlockSpec(memory_space=pltpu.VMEM)
-    args = [pltpu.with_memory_space_constraint(v, pltpu.HBM) for v in (x, *xs, own, sib, *given)]
+    free = 1 if last else 0
+    args = [x, *xs, own, sib, *given]
+    pinned = len(args) - free
+    args = [pltpu.with_memory_space_constraint(v, pltpu.HBM) for v in args[:pinned]] + args[pinned:]
     specs = [hbm] * len(args)
     scratch = [
         pltpu.VMEM((tokens, 2 * feats), x.dtype),
@@ -254,9 +265,7 @@
     two_twin = across(two)
     fourth = part(x_b, 3)
     one_sib, one_twin_sib = sub(one_b), sub(one_twin)
-    out_three, x2, two_twin, one_sib, one_twin_sib, fourth, two_c = tie(
-        (out_three, x2, two_twin, one_sib, one_twin_sib, fourth, two)
-    )
+    out_three, x2, two_twin, fourth, two_c = tie((out_three, x2, two_twin, fourth, two))
     three = jnp.where(inner, mid, out_three)
     twin = across(three)
     x3 = far(fourth)

time: 173 us -> 167 us (0.965)
  starting transfers between devices: 35.1 us -> 39.6 us
  waiting for transfers between devices: 76.6 us -> 73.4 us
  Pallas kernels: 40.1 us -> 37 us
  local copies, waits for them, and re-layouts: 15.5 us -> 12.5 us
    ppermute x4, waiting for transfers between devices: 24.4 us -> 21.2 us  [far(): return lax.ppermute(value, 'head', SWAP)]
    pallas_call x2, Pallas kernels: 24.7 us -> 21.6 us  [project(): pl.pallas_call(functools.partial(project_kernel, near, widths, last), out...]
    unnamed x40 -> x30, local copies, waits for them, and re-layouts: 6.85 us -> 3.9 us
    ppermute x8, starting transfers between devices: 6.89 us -> 9.58 us  [sub(): return lax.ppermute(value, 'sub', SWAP)]
  transfers between devices with their start and end apart: 32 -> 32, of which waited for: 18 -> 18; matrix products, arithmetic and copies ran while one was open for 6% -> 7% of each run, Pallas kernels for 17% -> 17%
where the time goes in v5:
time: 167 us
  waiting for transfers between devices  73.4 us (44%)
  starting transfers between devices  39.6 us (24%)
  Pallas kernels  37 us (22%)
  local copies, waits for them, and re-layouts  12.5 us (7%)
  other arithmetic  2.28 us (1%)
    pallas_call x2, Pallas kernels, project(): pl.pallas_call(functools.partial(project_kernel, near, widths, last), out...  21.6 us
    ppermute x4, waiting for transfers between devices, far(): return lax.ppermute(value, 'head', SWAP)  21.2 us
    ppermute x5, waiting for transfers between devices, along(): return lax.ppermute(value, 'seq', pairs)  20.9 us
    ppermute x5, starting transfers between devices, along(): return lax.ppermute(value, 'seq', pairs)  14.7 us
    ppermute x3, waiting for transfers between devices, across(): return lax.ppermute(value, 'groups', SWAP)  13.7 us
    pallas_call x1, Pallas kernels, solve(): pl.pallas_call(functools.partial(solve_kernel, 1.0 / token_total, len(par...  13 us
    ppermute x8, starting transfers between devices, sub(): return lax.ppermute(value, 'sub', SWAP)  9.58 us
    slice x4, local copies, waits for them, and re-layouts, part(): return value[:, bounds[i] * feats // 8:bounds[i + 1] * feats // 8]  8.13 us
  transfers between devices with their start and end apart: 32, of which 18 were waited for; matrix products, arithmetic and copies ran while one was open for 7% of the time, Pallas kernels for 17%

profile of v5, /device:TPU:11, one launch (start us, length us, event | category | flops | bytes accessed | tf_op | source)
XLA Modules:
  0.0 167.0 jit_solution(1240318553237283760)
XLA Ops:
  0.7 1.5 constant_dynamic-update-slice_fusion.1
  2.1 0.1 copy-done.8
  2.2 0.1 constant_dynamic-update-slice_fusion.refs_4_.refs_5_
  2.4 0.7 collective-permute-start.2
  3.2 0.2 collective-permute-start
  3.4 4.3 %collective-permute-start.1 = (bf16[512,1024]{1,0:T(8,128)(2,1)S(1)}, bf16[512,1024]{1,0:T(8,128)(2,1)}, u32[]{:S(2)}, u32[]{:S(2)}) collective-permute-start(bf16[512,1024]{1,0:T(8,128)(2,1)S(1)} %constant_dynamic-slice_fusion.1), channel_id=1, source_target_pairs={{4,8},{8,4},{5,9},{9,5},{6,10},{10,6},{7,11},{11,7},{20,24},{24,20... | collective-permute-start | bytes 3145736 | tf_op jit(solution)/shard_map/ppermute | solution.py:238
  7.8 2.3 %slice.61 = bf16[512,1024]{1,0:T(8,128)(2,1)} slice(bf16[512,4096]{1,0:T(8,128)(2,1)} %refs_0_.3), slice={[0:512], [0:1024]} | slice | bytes 2097152 | tf_op jit(solution)/shard_map/slice | solution.py:247
  10.0 0.3 collective-permute-start.5
  10.3 2.3 %slice.80 = bf16[512,1024]{1,0:T(8,128)(2,1)} slice(bf16[512,4096]{1,0:T(8,128)(2,1)} %refs_0_.3), slice={[0:512], [1024:2048]} | slice | bytes 2097152 | tf_op jit(solution)/shard_map/slice | solution.py:247
  12.6 1.2 collective-permute-start.6
  13.8 14.3 %collective-permute-done.refs_6_.refs_7_ = bf16[512,1024]{1,0:T(8,128)(2,1)S(1)} collective-permute-done((bf16[512,1024]{1,0:T(8,128)(2,1)S(1)}, bf16[512,1024]{1,0:T(8,128)(2,1)S(1)}, u32[]{:S(2)}, u32[]{:S(2)}) %collective-permute-start) | collective-permute-done | bytes 1048608 | tf_op jit(solution)/shard_map/ppermute | solution.py:238
  28.1 3.0 %collective-permute-done.1 = bf16[512,1024]{1,0:T(8,128)(2,1)} collective-permute-done((bf16[512,1024]{1,0:T(8,128)(2,1)S(1)}, bf16[512,1024]{1,0:T(8,128)(2,1)}, u32[]{:S(2)}, u32[]{:S(2)}) %collective-permute-start.1) | collective-permute-done | bytes 1048608 | tf_op jit(solution)/shard_map/ppermute | solution.py:238
  31.2 3.0 %collective-permute-start.3 = (bf16[512,1024]{1,0:T(8,128)(2,1)S(1)}, bf16[512,1024]{1,0:T(8,128)(2,1)S(1)}, u32[]{:S(2)}, u32[]{:S(2)}) collective-permute-start(bf16[512,1024]{1,0:T(8,128)(2,1)S(1)} %collective-permute-done.refs_6_.refs_7_), channel_id=1, source_target_pairs={{4,8},{8,4},{5,9},{9,5},{6,10},{10,6},{7,11},{11,7},{20,24},{24,20... | collective-permute-start | bytes 3145736 | tf_op jit(solution)/shard_map/ppermute | solution.py:238
  34.2 1.3 collective-permute-start.7
  35.5 2.3 %collective-permute-start.4 = (bf16[512,1024]{1,0:T(8,128)(2,1)}, bf16[512,1024]{1,0:T(8,128)(2,1)}, u32[]{:S(2)}, u32[]{:S(2)}) collective-permute-start(bf16[512,1024]{1,0:T(8,128)(2,1)} %collective-permute-done.1), channel_id=1, source_target_pairs={{4,0},{8,12},{5,1},{9,13},{6,2},{10,14},{7,3},{11,15},{20,16},{24,... | collective-permute-start | bytes 3145736 | tf_op jit(solution)/shard_map/ppermute | solution.py:238
  37.8 1.3 slice.63
  39.1 17.9 %collective-permute-done.6.refs_2_ = bf16[512,1024]{1,0:T(8,128)(2,1)} collective-permute-done((bf16[512,1024]{1,0:T(8,128)(2,1)}, bf16[512,1024]{1,0:T(8,128)(2,1)}, u32[]{:S(2)}, u32[]{:S(2)}) %collective-permute-start.6) | collective-permute-done | bytes 1048608 | tf_op jit(solution)/shard_map/ppermute | solution.py:241
  57.0 0.6 collective-permute-done.7.refs_7_.refs_8_
  57.6 0.5 collective-permute-done.4
  58.1 0.1 broadcast_select_fusion.1.refs_10_.refs_11_
  58.2 0.8 collective-permute-start.10
  59.0 4.9 %collective-permute-start.8 = (bf16[512,1024]{1,0:T(8,128)(2,1)S(1)}, bf16[512,1024]{1,0:T(8,128)(2,1)S(1)}, u32[]{:S(2)}, u32[]{:S(2)}) collective-permute-start(bf16[512,1024]{1,0:T(8,128)(2,1)S(1)} %collective-permute-done.3), channel_id=1, source_target_pairs={{4,0},{8,12},{5,1},{9,13},{6,2},{10,14},{7,3},{11,15},{20,16},{24,... | collective-permute-start | bytes 3145736 | tf_op jit(solution)/shard_map/ppermute | solution.py:238
  63.9 0.3 collective-permute-start.9
  64.3 3.2 %collective-permute-start.13 = (bf16[512,1024]{1,0:T(8,128)(2,1)S(1)}, bf16[512,1024]{1,0:T(8,128)(2,1)}, u32[]{:S(2)}, u32[]{:S(2)}) collective-permute-start(bf16[512,1024]{1,0:T(8,128)(2,1)S(1)} %collective-permute-done.refs_6_.refs_7_), channel_id=1, source_target_pairs={{0,1},{1,0},{2,3},{3,2},{4,5},{5,4},{6,7},{7,6},{8,9},{9,8},{10,11... | collective-permute-start | bytes 3145736 | tf_op jit(solution)/shard_map/ppermute | solution.py:232
  67.4 2.3 %slice.64 = bf16[512,1024]{1,0:T(8,128)(2,1)} slice(bf16[512,4096]{1,0:T(8,128)(2,1)} %refs_0_.3), slice={[0:512], [3072:4096]} | slice | bytes 2097152 | tf_op jit(solution)/shard_map/slice | solution.py:247
  69.7 11.0 %collective-permute-done.10.refs_11_.refs_12_ = bf16[512,1024]{1,0:T(8,128)(2,1)} collective-permute-done((bf16[512,1024]{1,0:T(8,128)(2,1)S(1)}, bf16[512,1024]{1,0:T(8,128)(2,1)}, u32[]{:S(2)}, u32[]{:S(2)}) %collective-permute-start.10) | collective-permute-done | bytes 1048608 | tf_op jit(solution)/shard_map/ppermute | solution.py:235
  80.7 2.9 %collective-permute-done.8 = bf16[512,1024]{1,0:T(8,128)(2,1)S(1)} collective-permute-done((bf16[512,1024]{1,0:T(8,128)(2,1)S(1)}, bf16[512,1024]{1,0:T(8,128)(2,1)S(1)}, u32[]{:S(2)}, u32[]{:S(2)}) %collective-permute-start.8) | collective-permute-done | bytes 1048608 | tf_op jit(solution)/shard_map/ppermute | solution.py:238
  83.7 2.2 %collective-permute-done.9.refs_3_ = bf16[512,1024]{1,0:T(8,128)(2,1)} collective-permute-done((bf16[512,1024]{1,0:T(8,128)(2,1)S(1)}, bf16[512,1024]{1,0:T(8,128)(2,1)}, u32[]{:S(2)}, u32[]{:S(2)}) %collective-permute-start.9) | collective-permute-done | bytes 1048608 | tf_op jit(solution)/shard_map/ppermute | solution.py:241
  85.9 1.3 broadcast_select_fusion.refs_14_.refs_15_
  87.2 3.9 %collective-permute-start.17 = (bf16[512,1024]{1,0:T(8,128)(2,1)S(1)}, bf16[512,1024]{1,0:T(8,128)(2,1)}, u32[]{:S(2)}, u32[]{:S(2)}) collective-permute-start(bf16[512,1024]{1,0:T(8,128)(2,1)S(1)} %broadcast_select_fusion.refs_14_.refs_15_), channel_id=1, source_target_pairs={{0,1},{1,0},{2,3},{3,2},{4,5},{5,4},{6,7},{7,6},{8,9},{9,8},{10,11... | collective-permute-start | bytes 3145736 | tf_op jit(solution)/shard_map/ppermute | solution.py:232
  91.2 0.4 collective-permute-start.16
  91.6 0.8 copy.32.refs_4_
  92.4 0.2 convert_reduce_fusion
  92.6 1.3 collective-permute-start.11
  94.0 0.3 collective-permute-start.12
  94.3 0.2 select_reduce_fusion
  94.5 2.0 %collective-permute-done.15.refs_12_.refs_13_ = bf16[512,1024]{1,0:T(8,128)(2,1)} collective-permute-done((bf16[512,1024]{1,0:T(8,128)(2,1)S(1)}, bf16[512,1024]{1,0:T(8,128)(2,1)}, u32[]{:S(2)}, u32[]{:S(2)}) %collective-permute-start.15) | collective-permute-done | bytes 1048608 | tf_op jit(solution)/shard_map/ppermute | solution.py:232
  96.5 0.2 collective-permute-done.16.refs_13_.refs_14_
  96.7 15.9 %shard_map.68.refs_19_ = f32[512,1024]{1,0:T(8,128)S(1)} custom-call(bf16[512,4096]{1,0:T(8,128)(2,1)} %refs_0_.3, bf16[512,1024]{1,0:T(8,128)(2,1)} %collective-permute-done.5.refs_1_, bf16[512,1024]{1,0:T(8,128)(2,1)} %collective-permute-done.6.refs_2_, bf16[512,1024]{1,0:T(8,128)(2,1)} %collective-permute-done.9.refs_3_, bf16[1024,1024]{1,0:T(8,128)(2,1)} %copy-done.2, ...), custom_call_target="tpu_custom_call" | custom-call | flops 4294967296 | bytes 16777216 | tf_op jit(solution)/shard_map/pallas_call | solution.py:212
  112.8 2.6 %collective-permute-start.24 = (s32[512]{0:T(512)S(1)}, s32[512]{0:T(512)S(1)}, u32[]{:S(2)}, u32[]{:S(2)}) collective-permute-start(s32[512]{0:T(512)S(1)} %select_reduce_fusion), channel_id=1, source_target_pairs={{0,4},{4,0},{8,12},{12,8},{1,5},{5,1},{9,13},{13,9},{2,6},{6,2},{1... | collective-permute-start | bytes 6152 | tf_op jit(solution)/shard_map/ppermute | solution.py:277
  115.3 2.1 %collective-permute-done.11.refs_16_ = bf16[512,1024]{1,0:T(8,128)(2,1)S(1)} collective-permute-done((bf16[512,1024]{1,0:T(8,128)(2,1)S(1)}, bf16[512,1024]{1,0:T(8,128)(2,1)S(1)}, u32[]{:S(2)}, u32[]{:S(2)}) %collective-permute-start.11) | collective-permute-done | bytes 1048608 | tf_op jit(solution)/shard_map/ppermute | solution.py:235
  117.4 1.1 collective-permute-done.12.refs_4_
  118.6 1.2 collective-permute-start.18
  120.0 2.1 %collective-permute-done.27 = s32[4,512]{1,0:T(4,128)S(1)} collective-permute-done((s32[4,512]{1,0:T(4,128)S(1)}, s32[4,512]{1,0:T(4,128)S(1)}, u32[]{:S(2)}, u32[]{:S(2)}) %collective-permute-start.27) | collective-permute-done | bytes 8224 | tf_op jit(solution)/shard_map/ppermute | solution.py:232
  122.2 5.7 %shard_map.69 = bf16[512,1024]{1,0:T(8,128)(2,1)S(1)} custom-call(bf16[512,4096]{1,0:T(8,128)(2,1)} %refs_0_.3, bf16[512,1024]{1,0:T(8,128)(2,1)} %collective-permute-done.5.refs_1_, bf16[512,1024]{1,0:T(8,128)(2,1)} %collective-permute-done.6.refs_2_, bf16[512,1024]{1,0:T(8,128)(2,1)} %collective-permute-done.9.refs_3_, bf16[512,1024]{1,0:T(8,128)(2,1)} %copy-done.7, ...), custom_call_target="tpu_custom_call" | custom-call | flops 4294967296 | bytes 16777216 | tf_op jit(solution)/shard_map/pallas_call | solution.py:212
  127.9 0.3 fusion.1
  128.3 0.5 convolution_convert_fusion
  128.8 1.1 collective-permute-start.28
  130.0 0.5 convolution_convert_fusion.1
  130.5 1.0 collective-permute-done.19
  131.6 0.7 collective-permute-start.21
  132.3 1.9 %collective-permute-start.22 = (f32[136,128]{1,0:T(8,128)S(1)}, f32[136,128]{1,0:T(8,128)S(1)}, u32[]{:S(2)}, u32[]{:S(2)}) collective-permute-start(f32[136,128]{1,0:T(8,128)S(1)} %fusion.14.refs_0_), channel_id=1, source_target_pairs={{0,12},{4,8},{8,4},{12,0},{1,13},{5,9},{9,5},{13,1},{2,14},{6,10},... | collective-permute-start | bytes 208904 | tf_op jit(solution)/shard_map/ppermute | solution.py:390
  134.3 1.0 collective-permute-start.29
  135.4 0.2 collective-permute-start.30
  135.6 1.5 collective-permute-start.31
  137.0 4.1 %collective-permute-done.22.refs_3_ = f32[136,128]{1,0:T(8,128)S(1)} collective-permute-done((f32[136,128]{1,0:T(8,128)S(1)}, f32[136,128]{1,0:T(8,128)S(1)}, u32[]{:S(2)}, u32[]{:S(2)}) %collective-permute-start.22) | collective-permute-done | bytes 69664 | tf_op jit(solution)/shard_map/ppermute | solution.py:390
  141.2 0.6 copy-done.13
  141.8 13.0 %shard_map.70.mine_ref = f32[2,128,64]{2,1,0:T(8,128)} custom-call(f32[136,128]{1,0:T(8,128)} %copy-done.9, f32[136,128]{1,0:T(8,128)} %copy-done.11, f32[136,128]{1,0:T(8,128)} %copy-done.12, f32[136,128]{1,0:T(8,128)} %copy-done.13, f32[2,128,64]{2,1,0:T(8,128)} %copy.32.refs_4_), custom_call_target="tpu_custom_call" | custom-call | flops 12582912000 | bytes 131072 | tf_op jit(solution)/shard_map/pallas_call | solution.py:93
  154.8 0.6 collective-permute-start.23
  155.4 0.1 copy.29.position_ref
  155.6 1.0 collective-permute-done.23.other_ref
  156.6 7.0 %collective-permute-done.31.refs_3_ = bf16[128,1024]{1,0:T(8,128)(2,1)S(1)} collective-permute-done((bf16[128,1024]{1,0:T(8,128)(2,1)S(1)}, bf16[128,1024]{1,0:T(8,128)(2,1)S(1)}, u32[]{:S(2)}, u32[]{:S(2)}) %collective-permute-start.31) | collective-permute-done | bytes 262176 | tf_op jit(solution)/shard_map/ppermute | solution.py:394
  163.7 0.9 copy-done.1
  164.6 2.4 %shard_map.71 = (bf16[512,256]{1,0:T(8,128)(2,1)}, bf16[512,512]{1,0:T(8,128)(2,1)}) custom-call(s32[512,1]{1,0:T(8,128)S(1)} %copy.29.position_ref, f32[2,128,64]{2,1,0:T(8,128)S(1)} %copy-done.1, f32[2,128,64]{2,1,0:T(8,128)S(1)} %collective-permute-done.23.other_ref, bf16[128,1024]{1,0:T(8,128)(2,1)S(1)} %bitcast.61, ...), custom_call_target="tpu_custom_call" | custom-call | tf_op jit(solution)/shard_map/pallas_call | solution.py:330
  (65 shorter events, 1.1 us)
Async XLA Ops:
  0.6 91.0 %copy-start = (f32[4,128,64]{1,2,0:T(8,128)S(1)}, f32[4,128,64]{1,2,0:T(8,128)}, u32[]{:S(2)}) copy-start(f32[4,128,64]{1,2,0:T(8,128)} %param.8) | copy-start | bytes 393220
  0.6 1.6 copy-start.8
  2.4 7.7 %copy-start.2 = (bf16[1024,1024]{1,0:T(8,128)(2,1)}, bf16[1024,1024]{1,0:T(8,128)(2,1)S(1)}, u32[]{:S(2)}) copy-start(bf16[1024,1024]{1,0:T(8,128)(2,1)S(1)} %constant_dynamic-update-slice_fusion.refs_4_.refs_5_) | copy-start | bytes 6291460
  2.4 28.8 %collective-permute-start.2 = (bf16[1024,1024]{1,0:T(8,128)(2,1)S(1)}, bf16[1024,1024]{1,0:T(8,128)(2,1)}, u32[]{:S(2)}, u32[]{:S(2)}) collective-permute-start(bf16[1024,1024]{1,0:T(8,128)(2,1)S(1)} %constant_dynamic-update-slice_fusion.refs_4_.refs_5_), channel_id=1, source_target_pairs={{0,1},{1,0},{2,3},{3,2},{4,5},{5,4},{6,7},{7,6},{8,9},{9,8},{10,11... | collective-permute-start | bytes 6291464 | tf_op jit(solution)/shard_map/ppermute | solution.py:232
  3.2 24.9 %collective-permute-start = (bf16[512,1024]{1,0:T(8,128)(2,1)S(1)}, bf16[512,1024]{1,0:T(8,128)(2,1)S(1)}, u32[]{:S(2)}, u32[]{:S(2)}) collective-permute-start(bf16[512,1024]{1,0:T(8,128)(2,1)S(1)} %constant_dynamic-slice_fusion.1), channel_id=1, source_target_pairs={{0,4},{4,0},{8,12},{12,8},{1,5},{5,1},{9,13},{13,9},{2,6},{6,2},{1... | collective-permute-start | bytes 3145736 | tf_op jit(solution)/shard_map/ppermute | solution.py:238
  3.4 27.7 %collective-permute-start.1 = (bf16[512,1024]{1,0:T(8,128)(2,1)S(1)}, bf16[512,1024]{1,0:T(8,128)(2,1)}, u32[]{:S(2)}, u32[]{:S(2)}) collective-permute-start(bf16[512,1024]{1,0:T(8,128)(2,1)S(1)} %constant_dynamic-slice_fusion.1), channel_id=1, source_target_pairs={{4,8},{8,4},{5,9},{9,5},{6,10},{10,6},{7,11},{11,7},{20,24},{24,20... | collective-permute-start | bytes 3145736 | tf_op jit(solution)/shard_map/ppermute | solution.py:238
  10.0 29.0 %collective-permute-start.5 = (bf16[512,1024]{1,0:T(8,128)(2,1)}, bf16[512,1024]{1,0:T(8,128)(2,1)}, u32[]{:S(2)}, u32[]{:S(2)}) collective-permute-start(bf16[512,1024]{1,0:T(8,128)(2,1)} %slice.61), channel_id=1, source_target_pairs={{0,2},{2,0},{1,3},{3,1},{4,6},{6,4},{5,7},{7,5},{8,10},{10,8},{9,1... | collective-permute-start | bytes 3145736 | tf_op jit(solution)/shard_map/ppermute | solution.py:241
  12.6 44.4 %collective-permute-start.6 = (bf16[512,1024]{1,0:T(8,128)(2,1)}, bf16[512,1024]{1,0:T(8,128)(2,1)}, u32[]{:S(2)}, u32[]{:S(2)}) collective-permute-start(bf16[512,1024]{1,0:T(8,128)(2,1)} %slice.80), channel_id=1, source_target_pairs={{0,2},{2,0},{1,3},{3,1},{4,6},{6,4},{5,7},{7,5},{8,10},{10,8},{9,1... | collective-permute-start | bytes 3145736 | tf_op jit(solution)/shard_map/ppermute | solution.py:241
  28.1 36.1 %copy-start.5 = (bf16[512,1024]{1,0:T(8,128)(2,1)}, bf16[512,1024]{1,0:T(8,128)(2,1)S(1)}, u32[]{:S(2)}) copy-start(bf16[512,1024]{1,0:T(8,128)(2,1)S(1)} %collective-permute-done.refs_6_.refs_7_) | copy-start | bytes 3145732
  31.2 25.9 %collective-permute-start.3 = (bf16[512,1024]{1,0:T(8,128)(2,1)S(1)}, bf16[512,1024]{1,0:T(8,128)(2,1)S(1)}, u32[]{:S(2)}, u32[]{:S(2)}) collective-permute-start(bf16[512,1024]{1,0:T(8,128)(2,1)S(1)} %collective-permute-done.refs_6_.refs_7_), channel_id=1, source_target_pairs={{4,8},{8,4},{5,9},{9,5},{6,10},{10,6},{7,11},{11,7},{20,24},{24,20... | collective-permute-start | bytes 3145736 | tf_op jit(solution)/shard_map/ppermute | solution.py:238
  34.2 23.4 %collective-permute-start.7 = (bf16[512,1024]{1,0:T(8,128)(2,1)S(1)}, bf16[512,1024]{1,0:T(8,128)(2,1)}, u32[]{:S(2)}, u32[]{:S(2)}) collective-permute-start(bf16[512,1024]{1,0:T(8,128)(2,1)S(1)} %collective-permute-done.refs_6_.refs_7_), channel_id=1, source_target_pairs={{0,16},{16,0},{1,17},{17,1},{2,18},{18,2},{3,19},{19,3},{4,20},{20... | collective-permute-start | bytes 3145736 | tf_op jit(solution)/shard_map/ppermute | solution.py:235
  35.5 22.6 %collective-permute-start.4 = (bf16[512,1024]{1,0:T(8,128)(2,1)}, bf16[512,1024]{1,0:T(8,128)(2,1)}, u32[]{:S(2)}, u32[]{:S(2)}) collective-permute-start(bf16[512,1024]{1,0:T(8,128)(2,1)} %collective-permute-done.1), channel_id=1, source_target_pairs={{4,0},{8,12},{5,1},{9,13},{6,2},{10,14},{7,3},{11,15},{20,16},{24,... | collective-permute-start | bytes 3145736 | tf_op jit(solution)/shard_map/ppermute | solution.py:238
  58.2 32.9 %copy-start.3 = (bf16[512,1024]{1,0:T(8,128)(2,1)}, bf16[512,1024]{1,0:T(8,128)(2,1)S(1)}, u32[]{:S(2)}) copy-start(bf16[512,1024]{1,0:T(8,128)(2,1)S(1)} %broadcast_select_fusion.1.refs_10_.refs_11_) | copy-start | bytes 3145732
  58.2 22.5 %collective-permute-start.10 = (bf16[512,1024]{1,0:T(8,128)(2,1)S(1)}, bf16[512,1024]{1,0:T(8,128)(2,1)}, u32[]{:S(2)}, u32[]{:S(2)}) collective-permute-start(bf16[512,1024]{1,0:T(8,128)(2,1)S(1)} %broadcast_select_fusion.1.refs_10_.refs_11_), channel_id=1, source_target_pairs={{0,16},{16,0},{1,17},{17,1},{2,18},{18,2},{3,19},{19,3},{4,20},{20... | collective-permute-start | bytes 3145736 | tf_op jit(solution)/shard_map/ppermute | solution.py:235
  59.0 24.6 %collective-permute-start.8 = (bf16[512,1024]{1,0:T(8,128)(2,1)S(1)}, bf16[512,1024]{1,0:T(8,128)(2,1)S(1)}, u32[]{:S(2)}, u32[]{:S(2)}) collective-permute-start(bf16[512,1024]{1,0:T(8,128)(2,1)S(1)} %collective-permute-done.3), channel_id=1, source_target_pairs={{4,0},{8,12},{5,1},{9,13},{6,2},{10,14},{7,3},{11,15},{20,16},{24,... | collective-permute-start | bytes 3145736 | tf_op jit(solution)/shard_map/ppermute | solution.py:238
  63.9 21.9 %collective-permute-start.9 = (bf16[512,1024]{1,0:T(8,128)(2,1)S(1)}, bf16[512,1024]{1,0:T(8,128)(2,1)}, u32[]{:S(2)}, u32[]{:S(2)}) collective-permute-start(bf16[512,1024]{1,0:T(8,128)(2,1)S(1)} %slice.63), channel_id=1, source_target_pairs={{0,2},{2,0},{1,3},{3,1},{4,6},{6,4},{5,7},{7,5},{8,10},{10,8},{9,1... | collective-permute-start | bytes 3145736 | tf_op jit(solution)/shard_map/ppermute | solution.py:241
  64.3 28.4 %collective-permute-start.13 = (bf16[512,1024]{1,0:T(8,128)(2,1)S(1)}, bf16[512,1024]{1,0:T(8,128)(2,1)}, u32[]{:S(2)}, u32[]{:S(2)}) collective-permute-start(bf16[512,1024]{1,0:T(8,128)(2,1)S(1)} %collective-permute-done.refs_6_.refs_7_), channel_id=1, source_target_pairs={{0,1},{1,0},{2,3},{3,2},{4,5},{5,4},{6,7},{7,6},{8,9},{9,8},{10,11... | collective-permute-start | bytes 3145736 | tf_op jit(solution)/shard_map/ppermute | solution.py:232
  67.4 26.5 %collective-permute-start.14 = (bf16[512,1024]{1,0:T(8,128)(2,1)}, bf16[512,1024]{1,0:T(8,128)(2,1)}, u32[]{:S(2)}, u32[]{:S(2)}) collective-permute-start(bf16[512,1024]{1,0:T(8,128)(2,1)} %collective-permute-done.7.refs_7_.refs_8_), channel_id=1, source_target_pairs={{0,1},{1,0},{2,3},{3,2},{4,5},{5,4},{6,7},{7,6},{8,9},{9,8},{10,11... | collective-permute-start | bytes 3145736 | tf_op jit(solution)/shard_map/ppermute | solution.py:232
  69.7 22.6 %copy-start.10 = (s32[512]{0:T(512)S(1)}, s32[512]{0:T(512)}, u32[]{:S(2)}) copy-start(s32[512]{0:T(512)} %param.9) | copy-start | bytes 6148
  87.2 9.5 %copy-start.4 = (bf16[512,1024]{1,0:T(8,128)(2,1)}, bf16[512,1024]{1,0:T(8,128)(2,1)S(1)}, u32[]{:S(2)}) copy-start(bf16[512,1024]{1,0:T(8,128)(2,1)S(1)} %broadcast_select_fusion.refs_14_.refs_15_) | copy-start | bytes 3145732
  87.2 7.3 %collective-permute-start.17 = (bf16[512,1024]{1,0:T(8,128)(2,1)S(1)}, bf16[512,1024]{1,0:T(8,128)(2,1)}, u32[]{:S(2)}, u32[]{:S(2)}) collective-permute-start(bf16[512,1024]{1,0:T(8,128)(2,1)S(1)} %broadcast_select_fusion.refs_14_.refs_15_), channel_id=1, source_target_pairs={{0,1},{1,0},{2,3},{3,2},{4,5},{5,4},{6,7},{7,6},{8,9},{9,8},{10,11... | collective-permute-start | bytes 3145736 | tf_op jit(solution)/shard_map/ppermute | solution.py:232
  91.1 5.4 %collective-permute-start.15 = (bf16[512,1024]{1,0:T(8,128)(2,1)S(1)}, bf16[512,1024]{1,0:T(8,128)(2,1)}, u32[]{:S(2)}, u32[]{:S(2)}) collective-permute-start(bf16[512,1024]{1,0:T(8,128)(2,1)S(1)} %broadcast_select_fusion.1.refs_10_.refs_11_), channel_id=1, source_target_pairs={{0,1},{1,0},{2,3},{3,2},{4,5},{5,4},{6,7},{7,6},{8,9},{9,8},{10,11... | collective-permute-start | bytes 3145736 | tf_op jit(solution)/shard_map/ppermute | solution.py:232
  91.2 5.5 %collective-permute-start.16 = (bf16[512,1024]{1,0:T(8,128)(2,1)}, bf16[512,1024]{1,0:T(8,128)(2,1)}, u32[]{:S(2)}, u32[]{:S(2)}) collective-permute-start(bf16[512,1024]{1,0:T(8,128)(2,1)} %collective-permute-done.10.refs_11_.refs_12_), channel_id=1, source_target_pairs={{0,1},{1,0},{2,3},{3,2},{4,5},{5,4},{6,7},{7,6},{8,9},{9,8},{10,11... | collective-permute-start | bytes 3145736 | tf_op jit(solution)/shard_map/ppermute | solution.py:232
  92.6 24.8 %collective-permute-start.11 = (bf16[512,1024]{1,0:T(8,128)(2,1)S(1)}, bf16[512,1024]{1,0:T(8,128)(2,1)S(1)}, u32[]{:S(2)}, u32[]{:S(2)}) collective-permute-start(bf16[512,1024]{1,0:T(8,128)(2,1)S(1)} %broadcast_select_fusion.refs_14_.refs_15_), channel_id=1, source_target_pairs={{0,16},{16,0},{1,17},{17,1},{2,18},{18,2},{3,19},{19,3},{4,20},{20... | collective-permute-start | bytes 3145736 | tf_op jit(solution)/shard_map/ppermute | solution.py:235
  94.0 24.6 %collective-permute-start.12 = (bf16[512,1024]{1,0:T(8,128)(2,1)}, bf16[512,1024]{1,0:T(8,128)(2,1)S(1)}, u32[]{:S(2)}, u32[]{:S(2)}) collective-permute-start(bf16[512,1024]{1,0:T(8,128)(2,1)} %slice.64), channel_id=1, source_target_pairs={{0,2},{2,0},{1,3},{3,1},{4,6},{6,4},{5,7},{7,5},{8,10},{10,8},{9,1... | collective-permute-start | bytes 3145736 | tf_op jit(solution)/shard_map/ppermute | solution.py:241
  112.6 7.2 %collective-permute-start.26 = (s32[512]{0:T(512)S(1)}, s32[512]{0:T(512)S(1)}, u32[]{:S(2)}, u32[]{:S(2)}) collective-permute-start(s32[512]{0:T(512)S(1)} %select_reduce_fusion), channel_id=1, source_target_pairs={{0,12},{4,8},{8,4},{12,0},{1,13},{5,9},{9,5},{13,1},{2,14},{6,10},... | collective-permute-start | bytes 6152 | tf_op jit(solution)/shard_map/ppermute | solution.py:277
  112.7 7.1 %collective-permute-start.25 = (s32[512]{0:T(512)S(1)}, s32[512]{0:T(512)S(1)}, u32[]{:S(2)}, u32[]{:S(2)}) collective-permute-start(s32[512]{0:T(512)S(1)} %select_reduce_fusion), channel_id=1, source_target_pairs={{0,8},{4,12},{8,0},{12,4},{1,9},{5,13},{9,1},{13,5},{2,10},{6,14},... | collective-permute-start | bytes 6152 | tf_op jit(solution)/shard_map/ppermute | solution.py:277
  112.8 7.0 %collective-permute-start.24 = (s32[512]{0:T(512)S(1)}, s32[512]{0:T(512)S(1)}, u32[]{:S(2)}, u32[]{:S(2)}) collective-permute-start(s32[512]{0:T(512)S(1)} %select_reduce_fusion), channel_id=1, source_target_pairs={{0,4},{4,0},{8,12},{12,8},{1,5},{5,1},{9,13},{13,9},{2,6},{6,2},{1... | collective-permute-start | bytes 6152 | tf_op jit(solution)/shard_map/ppermute | solution.py:277
  117.4 4.8 %copy-start.6 = (bf16[512,1024]{1,0:T(8,128)(2,1)}, bf16[512,1024]{1,0:T(8,128)(2,1)S(1)}, u32[]{:S(2)}) copy-start(bf16[512,1024]{1,0:T(8,128)(2,1)S(1)} %collective-permute-done.11.refs_16_) | copy-start | bytes 3145732
  118.6 3.6 %copy-start.7 = (bf16[512,1024]{1,0:T(8,128)(2,1)}, bf16[512,1024]{1,0:T(8,128)(2,1)S(1)}, u32[]{:S(2)}) copy-start(bf16[512,1024]{1,0:T(8,128)(2,1)S(1)} %collective-permute-done.12.refs_4_) | copy-start | bytes 3145732
  118.6 3.6 %collective-permute-start.18 = (bf16[512,1024]{1,0:T(8,128)(2,1)S(1)}, bf16[512,1024]{1,0:T(8,128)(2,1)S(1)}, u32[]{:S(2)}, u32[]{:S(2)}) collective-permute-start(bf16[512,1024]{1,0:T(8,128)(2,1)S(1)} %collective-permute-done.11.refs_16_), channel_id=1, source_target_pairs={{0,1},{1,0},{2,3},{3,2},{4,5},{5,4},{6,7},{7,6},{8,9},{9,8},{10,11... | collective-permute-start | bytes 3145736 | tf_op jit(solution)/shard_map/ppermute | solution.py:232
  119.8 2.3 %collective-permute-start.27 = (s32[4,512]{1,0:T(4,128)S(1)}, s32[4,512]{1,0:T(4,128)S(1)}, u32[]{:S(2)}, u32[]{:S(2)}) collective-permute-start(s32[4,512]{1,0:T(4,128)S(1)} %pad_add_fusion), channel_id=1, source_target_pairs={{0,1},{1,0},{2,3},{3,2},{4,5},{5,4},{6,7},{7,6},{8,9},{9,8},{10,11... | collective-permute-start | bytes 24584 | tf_op jit(solution)/shard_map/ppermute | solution.py:232
  128.8 5.4 %collective-permute-start.28 = (bf16[256,1024]{1,0:T(8,128)(2,1)S(1)}, bf16[256,1024]{1,0:T(8,128)(2,1)S(1)}, u32[]{:S(2)}, u32[]{:S(2)}) collective-permute-start(bf16[256,1024]{1,0:T(8,128)(2,1)S(1)} %convolution_convert_fusion), channel_id=1, source_target_pairs={{0,1},{1,0},{2,3},{3,2},{4,5},{5,4},{6,7},{7,6},{8,9},{9,8},{10,11... | collective-permute-start | bytes 1572872 | tf_op jit(solution)/shard_map/ppermute | solution.py:389
  129.9 1.6 collective-permute-start.19
  131.5 9.7 %copy-start.9 = (f32[136,128]{1,0:T(8,128)}, f32[136,128]{1,0:T(8,128)S(1)}, u32[]{:S(2)}) copy-start(f32[136,128]{1,0:T(8,128)S(1)} %fusion.14.refs_0_) | copy-start | bytes 208900
  131.5 4.1 %collective-permute-start.20 = (f32[136,128]{1,0:T(8,128)S(1)}, f32[136,128]{1,0:T(8,128)S(1)}, u32[]{:S(2)}, u32[]{:S(2)}) collective-permute-start(f32[136,128]{1,0:T(8,128)S(1)} %fusion.14.refs_0_), channel_id=1, source_target_pairs={{0,4},{4,0},{8,12},{12,8},{1,5},{5,1},{9,13},{13,9},{2,6},{6,2},{1... | collective-permute-start | bytes 208904 | tf_op jit(solution)/shard_map/ppermute | solution.py:390
  131.6 5.5 %collective-permute-start.21 = (f32[136,128]{1,0:T(8,128)S(1)}, f32[136,128]{1,0:T(8,128)S(1)}, u32[]{:S(2)}, u32[]{:S(2)}) collective-permute-start(f32[136,128]{1,0:T(8,128)S(1)} %fusion.14.refs_0_), channel_id=1, source_target_pairs={{0,8},{4,12},{8,0},{12,4},{1,9},{5,13},{9,1},{13,5},{2,10},{6,14},... | collective-permute-start | bytes 208904 | tf_op jit(solution)/shard_map/ppermute | solution.py:390
  132.3 8.9 %collective-permute-start.22 = (f32[136,128]{1,0:T(8,128)S(1)}, f32[136,128]{1,0:T(8,128)S(1)}, u32[]{:S(2)}, u32[]{:S(2)}) collective-permute-start(f32[136,128]{1,0:T(8,128)S(1)} %fusion.14.refs_0_), channel_id=1, source_target_pairs={{0,12},{4,8},{8,4},{12,0},{1,13},{5,9},{9,5},{13,1},{2,14},{6,10},... | collective-permute-start | bytes 208904 | tf_op jit(solution)/shard_map/ppermute | solution.py:390
  134.3 22.3 %collective-permute-start.29 = (bf16[128,1024]{1,0:T(8,128)(2,1)S(1)}, bf16[128,1024]{1,0:T(8,128)(2,1)S(1)}, u32[]{:S(2)}, u32[]{:S(2)}) collective-permute-start(bf16[128,1024]{1,0:T(8,128)(2,1)S(1)} %bitcast.67), channel_id=1, source_target_pairs={{0,4},{4,0},{8,12},{12,8},{1,5},{5,1},{9,13},{13,9},{2,6},{6,2},{1... | collective-permute-start | bytes 786440 | tf_op jit(solution)/shard_map/ppermute | solution.py:394
  135.4 21.3 %collective-permute-start.30 = (bf16[128,1024]{1,0:T(8,128)(2,1)S(1)}, bf16[128,1024]{1,0:T(8,128)(2,1)S(1)}, u32[]{:S(2)}, u32[]{:S(2)}) collective-permute-start(bf16[128,1024]{1,0:T(8,128)(2,1)S(1)} %bitcast.66), channel_id=1, source_target_pairs={{0,8},{4,12},{8,0},{12,4},{1,9},{5,13},{9,1},{13,5},{2,10},{6,14},... | collective-permute-start | bytes 786440 | tf_op jit(solution)/shard_map/ppermute | solution.py:394
  135.6 5.6 %copy-start.11 = (f32[136,128]{1,0:T(8,128)}, f32[136,128]{1,0:T(8,128)S(1)}, u32[]{:S(2)}) copy-start(f32[136,128]{1,0:T(8,128)S(1)} %collective-permute-done.20.refs_1_) | copy-start | bytes 208900
  135.6 28.1 %collective-permute-start.31 = (bf16[128,1024]{1,0:T(8,128)(2,1)S(1)}, bf16[128,1024]{1,0:T(8,128)(2,1)S(1)}, u32[]{:S(2)}, u32[]{:S(2)}) collective-permute-start(bf16[128,1024]{1,0:T(8,128)(2,1)S(1)} %bitcast.65), channel_id=1, source_target_pairs={{0,12},{4,8},{8,4},{12,0},{1,13},{5,9},{9,5},{13,1},{2,14},{6,10},... | collective-permute-start | bytes 786440 | tf_op jit(solution)/shard_map/ppermute | solution.py:394
  137.0 4.1 %copy-start.12 = (f32[136,128]{1,0:T(8,128)}, f32[136,128]{1,0:T(8,128)S(1)}, u32[]{:S(2)}) copy-start(f32[136,128]{1,0:T(8,128)S(1)} %collective-permute-done.21.refs_2_) | copy-start | bytes 208900
  141.2 0.6 copy-start.13
  154.8 1.8 %collective-permute-start.23 = (f32[2,128,64]{2,1,0:T(8,128)}, f32[2,128,64]{2,1,0:T(8,128)S(1)}, u32[]{:S(2)}, u32[]{:S(2)}) collective-permute-start(f32[2,128,64]{2,1,0:T(8,128)} %shard_map.70.mine_ref), channel_id=1, source_target_pairs={{0,1},{1,0},{2,3},{3,2},{4,5},{5,4},{6,7},{7,6},{8,9},{9,8},{10,11... | collective-permute-start | bytes 196616 | tf_op jit(solution)/shard_map/ppermute | solution.py:408
  163.7 0.9 copy-start.1

commit v6 on v5

--- a/solution.py
+++ b/solution.py
@@ -194,10 +194,12 @@
     widths = [2 * v.shape[1] // block for v in xs]
     given = [pieces[name] for name in (ALL_PIECES if last else EARLY_PIECES)]
     hbm, vmem = pl.BlockSpec(memory_space=pltpu.HBM), pl.BlockSpec(memory_space=pltpu.VMEM)
-    free = 1 if last else 0
     args = [x, *xs, own, sib, *given]
-    pinned = len(args) - free
-    args = [pltpu.with_memory_space_constraint(v, pltpu.HBM) for v in args[:pinned]] + args[pinned:]
+    free = (len(xs), len(args) - 1) if last else (len(xs),)
+    args = [
+        v if i in free else pltpu.with_memory_space_constraint(v, pltpu.HBM)
+        for i, v in enumerate(args)
+    ]
     specs = [hbm] * len(args)
     scratch = [
         pltpu.VMEM((tokens, 2 * feats), x.dtype),
@@ -265,7 +267,7 @@
     two_twin = across(two)
     fourth = part(x_b, 3)
     one_sib, one_twin_sib = sub(one_b), sub(one_twin)
-    out_three, x2, two_twin, fourth, two_c = tie((out_three, x2, two_twin, fourth, two))
+    out_three, fourth, two_c = tie((out_three, fourth, two))
     three = jnp.where(inner, mid, out_three)
     twin = across(three)
     x3 = far(fourth)
@@ -276,7 +278,7 @@
     acc, wanted = tie((acc, wanted))
     lists = jnp.stack([wanted] + [lax.ppermute(wanted, "seq", xor(4, d)) for d in (1, 2, 3)])
     twin_lists = sub(lists)
-    twin, x3, acc = tie((twin, x3, acc))
+    twin, acc = tie((twin, acc))
     moved.update({(3, 1): twin, (3, 3): sub(twin)})
     return project(x, [x0, x1, x2, x3], own, sib, moved, acc), lists, twin_lists
 

time: 167 us -> 164 us (0.982)
  waiting for transfers between devices: 73.4 us -> 69.8 us
    ppermute x5, waiting for transfers between devices: 20.9 us -> 32.2 us  [along(): return lax.ppermute(value, 'seq', pairs)]
    ppermute x3, waiting for transfers between devices: 13.7 us -> 3.14 us  [across(): return lax.ppermute(value, 'groups', SWAP)]
    ppermute x8, waiting for transfers between devices: 4.32 us -> 2.24 us  [sub(): return lax.ppermute(value, 'sub', SWAP)]
    ppermute x4, waiting for transfers between devices: 21.2 us -> 19.4 us  [far(): return lax.ppermute(value, 'head', SWAP)]
  transfers between devices with their start and end apart: 32 -> 32, of which waited for: 18 -> 15; matrix products, arithmetic and copies ran while one was open for 7% -> 8% of each run, Pallas kernels for 17% -> 18%
where the time goes in v6:
time: 164 us; the launch traced here: 163 us
  waiting for transfers between devices  69.8 us (43%)
  starting transfers between devices  39 us (24%)
  Pallas kernels  36.7 us (22%)
  local copies, waits for them, and re-layouts  13.5 us (8%)
  other arithmetic  2.28 us (1%)
    ppermute x5, waiting for transfers between devices, along(): return lax.ppermute(value, 'seq', pairs)  32.2 us
    pallas_call x2, Pallas kernels, project(): pl.pallas_call(functools.partial(project_kernel, near, widths, last), out...  21.3 us
    ppermute x4, waiting for transfers between devices, far(): return lax.ppermute(value, 'head', SWAP)  19.4 us
    ppermute x5, starting transfers between devices, along(): return lax.ppermute(value, 'seq', pairs)  15.3 us
    pallas_call x1, Pallas kernels, solve(): pl.pallas_call(functools.partial(solve_kernel, 1.0 / token_total, len(par...  13 us
    ppermute x8, starting transfers between devices, sub(): return lax.ppermute(value, 'sub', SWAP)  9.44 us
    slice x4, local copies, waits for them, and re-layouts, part(): return value[:, bounds[i] * feats // 8:bounds[i + 1] * feats // 8]  9.15 us
    ppermute x3, waiting for transfers between devices, per_device(): lax.ppermute(pairs[d], 'seq', xor(seq, d))  6.77 us
  transfers between devices with their start and end apart: 32, of which 15 were waited for; matrix products, arithmetic and copies ran while one was open for 8% of the time, Pallas kernels for 18%

profile of v6, /device:TPU:11, one launch (start us, length us, event | category | flops | bytes accessed | tf_op | source)
XLA Modules:
  0.0 163.5 jit_solution(3137555872638769535)
XLA Ops:
  0.7 1.5 constant_dynamic-update-slice_fusion.1
  2.1 0.1 copy-done.8
  2.2 0.1 constant_dynamic-update-slice_fusion.refs_4_.refs_5_
  2.4 0.7 collective-permute-start.2
  3.2 0.2 collective-permute-start
  3.4 4.3 %collective-permute-start.1 = (bf16[512,1024]{1,0:T(8,128)(2,1)S(1)}, bf16[512,1024]{1,0:T(8,128)(2,1)}, u32[]{:S(2)}, u32[]{:S(2)}) collective-permute-start(bf16[512,1024]{1,0:T(8,128)(2,1)S(1)} %constant_dynamic-slice_fusion.1), channel_id=1, source_target_pairs={{4,8},{8,4},{5,9},{9,5},{6,10},{10,6},{7,11},{11,7},{20,24},{24,20... | collective-permute-start | bytes 3145736 | tf_op jit(solution)/shard_map/ppermute | solution.py:240
  7.8 2.3 %slice.61 = bf16[512,1024]{1,0:T(8,128)(2,1)} slice(bf16[512,4096]{1,0:T(8,128)(2,1)} %refs_0_.3), slice={[0:512], [0:1024]} | slice | bytes 2097152 | tf_op jit(solution)/shard_map/slice | solution.py:249
  10.1 0.3 collective-permute-start.5
  10.3 2.3 %slice.80 = bf16[512,1024]{1,0:T(8,128)(2,1)} slice(bf16[512,4096]{1,0:T(8,128)(2,1)} %refs_0_.3), slice={[0:512], [1024:2048]} | slice | bytes 2097152 | tf_op jit(solution)/shard_map/slice | solution.py:249
  12.6 1.2 collective-permute-start.6
  13.8 14.3 %collective-permute-done.refs_6_.refs_7_ = bf16[512,1024]{1,0:T(8,128)(2,1)} collective-permute-done((bf16[512,1024]{1,0:T(8,128)(2,1)S(1)}, bf16[512,1024]{1,0:T(8,128)(2,1)}, u32[]{:S(2)}, u32[]{:S(2)}) %collective-permute-start) | collective-permute-done | bytes 1048608 | tf_op jit(solution)/shard_map/ppermute | solution.py:240
  28.1 3.0 %collective-permute-done.1 = bf16[512,1024]{1,0:T(8,128)(2,1)} collective-permute-done((bf16[512,1024]{1,0:T(8,128)(2,1)S(1)}, bf16[512,1024]{1,0:T(8,128)(2,1)}, u32[]{:S(2)}, u32[]{:S(2)}) %collective-permute-start.1) | collective-permute-done | bytes 1048608 | tf_op jit(solution)/shard_map/ppermute | solution.py:240
  31.2 3.0 %collective-permute-start.3 = (bf16[512,1024]{1,0:T(8,128)(2,1)}, bf16[512,1024]{1,0:T(8,128)(2,1)S(1)}, u32[]{:S(2)}, u32[]{:S(2)}) collective-permute-start(bf16[512,1024]{1,0:T(8,128)(2,1)} %collective-permute-done.refs_6_.refs_7_), channel_id=1, source_target_pairs={{4,8},{8,4},{5,9},{9,5},{6,10},{10,6},{7,11},{11,7},{20,24},{24,20... | collective-permute-start | bytes 3145736 | tf_op jit(solution)/shard_map/ppermute | solution.py:240
  34.2 1.3 collective-permute-start.7
  35.5 2.3 %collective-permute-start.4 = (bf16[512,1024]{1,0:T(8,128)(2,1)}, bf16[512,1024]{1,0:T(8,128)(2,1)}, u32[]{:S(2)}, u32[]{:S(2)}) collective-permute-start(bf16[512,1024]{1,0:T(8,128)(2,1)} %collective-permute-done.1), channel_id=1, source_target_pairs={{4,0},{8,12},{5,1},{9,13},{6,2},{10,14},{7,3},{11,15},{20,16},{24,... | collective-permute-start | bytes 3145736 | tf_op jit(solution)/shard_map/ppermute | solution.py:240
  37.8 2.3 %slice.63 = bf16[512,1024]{1,0:T(8,128)(2,1)} slice(bf16[512,4096]{1,0:T(8,128)(2,1)} %refs_0_.3), slice={[0:512], [2048:3072]} | slice | bytes 2097152 | tf_op jit(solution)/shard_map/slice | solution.py:249
  40.1 16.9 %collective-permute-done.6.refs_2_ = bf16[512,1024]{1,0:T(8,128)(2,1)} collective-permute-done((bf16[512,1024]{1,0:T(8,128)(2,1)}, bf16[512,1024]{1,0:T(8,128)(2,1)}, u32[]{:S(2)}, u32[]{:S(2)}) %collective-permute-start.6) | collective-permute-done | bytes 1048608 | tf_op jit(solution)/shard_map/ppermute | solution.py:243
  57.0 0.3 collective-permute-done.3
  57.2 0.6 collective-permute-done.7.refs_7_.refs_8_
  57.8 0.3 collective-permute-done.4
  58.1 0.1 broadcast_select_fusion.1.refs_10_.refs_11_
  58.2 5.4 %collective-permute-start.9 = (bf16[512,1024]{1,0:T(8,128)(2,1)S(1)}, bf16[512,1024]{1,0:T(8,128)(2,1)S(1)}, u32[]{:S(2)}, u32[]{:S(2)}) collective-permute-start(bf16[512,1024]{1,0:T(8,128)(2,1)S(1)} %collective-permute-done.3), channel_id=1, source_target_pairs={{4,0},{8,12},{5,1},{9,13},{6,2},{10,14},{7,3},{11,15},{20,16},{24,... | collective-permute-start | bytes 3145736 | tf_op jit(solution)/shard_map/ppermute | solution.py:240
  63.6 0.3 collective-permute-start.13
  63.9 2.9 %collective-permute-start.11 = (bf16[512,1024]{1,0:T(8,128)(2,1)}, bf16[512,1024]{1,0:T(8,128)(2,1)}, u32[]{:S(2)}, u32[]{:S(2)}) collective-permute-start(bf16[512,1024]{1,0:T(8,128)(2,1)} %collective-permute-done.refs_6_.refs_7_), channel_id=1, source_target_pairs={{0,1},{1,0},{2,3},{3,2},{4,5},{5,4},{6,7},{7,6},{8,9},{9,8},{10,11... | collective-permute-start | bytes 3145736 | tf_op jit(solution)/shard_map/ppermute | solution.py:234
  66.8 2.3 %slice.64 = bf16[512,1024]{1,0:T(8,128)(2,1)} slice(bf16[512,4096]{1,0:T(8,128)(2,1)} %refs_0_.3), slice={[0:512], [3072:4096]} | slice | bytes 2097152 | tf_op jit(solution)/shard_map/slice | solution.py:249
  69.1 0.3 collective-permute-start.8
  69.4 14.3 %collective-permute-done.9 = bf16[512,1024]{1,0:T(8,128)(2,1)S(1)} collective-permute-done((bf16[512,1024]{1,0:T(8,128)(2,1)S(1)}, bf16[512,1024]{1,0:T(8,128)(2,1)S(1)}, u32[]{:S(2)}, u32[]{:S(2)}) %collective-permute-start.9) | collective-permute-done | bytes 1048608 | tf_op jit(solution)/shard_map/ppermute | solution.py:240
  83.7 1.3 broadcast_select_fusion.refs_14_.refs_15_
  85.0 3.3 %collective-permute-start.17 = (bf16[512,1024]{1,0:T(8,128)(2,1)S(1)}, bf16[512,1024]{1,0:T(8,128)(2,1)}, u32[]{:S(2)}, u32[]{:S(2)}) collective-permute-start(bf16[512,1024]{1,0:T(8,128)(2,1)S(1)} %broadcast_select_fusion.refs_14_.refs_15_), channel_id=1, source_target_pairs={{0,1},{1,0},{2,3},{3,2},{4,5},{5,4},{6,7},{7,6},{8,9},{9,8},{10,11... | collective-permute-start | bytes 3145736 | tf_op jit(solution)/shard_map/ppermute | solution.py:234
  88.4 1.0 collective-permute-start.14
  89.5 0.8 copy.32.refs_4_
  90.3 0.2 convert_reduce_fusion
  90.5 0.3 collective-permute-start.16
  90.8 0.2 select_reduce_fusion
  91.1 2.5 %collective-permute-done.8.refs_3_ = bf16[512,1024]{1,0:T(8,128)(2,1)S(1)} collective-permute-done((bf16[512,1024]{1,0:T(8,128)(2,1)}, bf16[512,1024]{1,0:T(8,128)(2,1)S(1)}, u32[]{:S(2)}, u32[]{:S(2)}) %collective-permute-start.8) | collective-permute-done | bytes 1048608 | tf_op jit(solution)/shard_map/ppermute | solution.py:243
  93.6 0.3 collective-permute-start.10
  93.8 0.2 collective-permute-done.15.refs_13_.refs_14_
  94.0 15.6 %shard_map.68.refs_19_ = f32[512,1024]{1,0:T(8,128)S(1)} custom-call(bf16[512,4096]{1,0:T(8,128)(2,1)} %refs_0_.3, bf16[512,1024]{1,0:T(8,128)(2,1)} %copy-done.6, bf16[512,1024]{1,0:T(8,128)(2,1)} %collective-permute-done.6.refs_2_, bf16[512,1024]{1,0:T(8,128)(2,1)S(1)} %collective-permute-done.8.refs_3_, bf16[1024,1024]{1,0:T(8,128)(2,1)} %copy-done.3, ...), custom_call_target="tpu_custom_call" | custom-call | flops 4294967296 | bytes 16777216 | tf_op jit(solution)/shard_map/pallas_call | solution.py:214
  109.7 1.6 collective-permute-start.25
  111.3 1.0 collective-permute-start.24
  112.3 2.5 %collective-permute-done.16.refs_16_ = bf16[512,1024]{1,0:T(8,128)(2,1)S(1)} collective-permute-done((bf16[512,1024]{1,0:T(8,128)(2,1)S(1)}, bf16[512,1024]{1,0:T(8,128)(2,1)S(1)}, u32[]{:S(2)}, u32[]{:S(2)}) %collective-permute-start.16) | collective-permute-done | bytes 1048608 | tf_op jit(solution)/shard_map/ppermute | solution.py:237
  114.9 1.3 collective-permute-start.18
  116.4 2.1 %collective-permute-done.27 = s32[4,512]{1,0:T(4,128)S(1)} collective-permute-done((s32[4,512]{1,0:T(4,128)S(1)}, s32[4,512]{1,0:T(4,128)S(1)}, u32[]{:S(2)}, u32[]{:S(2)}) %collective-permute-start.27) | collective-permute-done | bytes 8224 | tf_op jit(solution)/shard_map/ppermute | solution.py:234
  118.6 5.7 %shard_map.69 = bf16[512,1024]{1,0:T(8,128)(2,1)S(1)} custom-call(bf16[512,4096]{1,0:T(8,128)(2,1)} %refs_0_.3, bf16[512,1024]{1,0:T(8,128)(2,1)} %copy-done.6, bf16[512,1024]{1,0:T(8,128)(2,1)} %collective-permute-done.6.refs_2_, bf16[512,1024]{1,0:T(8,128)(2,1)} %copy-done.1, bf16[512,1024]{1,0:T(8,128)(2,1)S(1)} %collective-permute-done.10.refs_4_, ...), custom_call_target="tpu_custom_call" | custom-call | flops 4294967296 | bytes 16777216 | tf_op jit(solution)/shard_map/pallas_call | solution.py:214
  124.3 0.3 fusion.1
  124.7 0.5 convolution_convert_fusion
  125.2 1.3 collective-permute-start.28
  126.6 0.5 convolution_convert_fusion.1
  127.1 1.0 collective-permute-done.19
  128.2 0.4 collective-permute-start.21
  128.7 2.2 %collective-permute-start.22 = (f32[136,128]{1,0:T(8,128)S(1)}, f32[136,128]{1,0:T(8,128)S(1)}, u32[]{:S(2)}, u32[]{:S(2)}) collective-permute-start(f32[136,128]{1,0:T(8,128)S(1)} %fusion.14.refs_0_), channel_id=1, source_target_pairs={{0,12},{4,8},{8,4},{12,0},{1,13},{5,9},{9,5},{13,1},{2,14},{6,10},... | collective-permute-start | bytes 208904 | tf_op jit(solution)/shard_map/ppermute | solution.py:392
  130.9 0.1 pad_maximum_fusion
  131.0 1.0 collective-permute-start.29
  132.0 0.4 collective-permute-start.30
  132.4 1.3 collective-permute-start.31
  133.7 4.0 %collective-permute-done.22.refs_3_ = f32[136,128]{1,0:T(8,128)S(1)} collective-permute-done((f32[136,128]{1,0:T(8,128)S(1)}, f32[136,128]{1,0:T(8,128)S(1)}, u32[]{:S(2)}, u32[]{:S(2)}) %collective-permute-start.22) | collective-permute-done | bytes 69664 | tf_op jit(solution)/shard_map/ppermute | solution.py:392
  137.7 0.6 copy-done.13
  138.3 13.0 %shard_map.70.mine_ref = f32[2,128,64]{2,1,0:T(8,128)} custom-call(f32[136,128]{1,0:T(8,128)} %copy-done.9, f32[136,128]{1,0:T(8,128)} %copy-done.11, f32[136,128]{1,0:T(8,128)} %copy-done.12, f32[136,128]{1,0:T(8,128)} %copy-done.13, f32[2,128,64]{2,1,0:T(8,128)} %copy.32.refs_4_), custom_call_target="tpu_custom_call" | custom-call | flops 12582912000 | bytes 131072 | tf_op jit(solution)/shard_map/pallas_call | solution.py:93
  151.4 0.9 collective-permute-start.23
  152.2 0.1 copy.29.position_ref
  152.4 1.0 collective-permute-done.23.other_ref
  153.4 6.8 %collective-permute-done.31.refs_3_ = bf16[128,1024]{1,0:T(8,128)(2,1)S(1)} collective-permute-done((bf16[128,1024]{1,0:T(8,128)(2,1)S(1)}, bf16[128,1024]{1,0:T(8,128)(2,1)S(1)}, u32[]{:S(2)}, u32[]{:S(2)}) %collective-permute-start.31) | collective-permute-done | bytes 262176 | tf_op jit(solution)/shard_map/ppermute | solution.py:396
  160.2 0.9 copy-done.2
  161.1 2.4 %shard_map.71 = (bf16[512,256]{1,0:T(8,128)(2,1)}, bf16[512,512]{1,0:T(8,128)(2,1)}) custom-call(s32[512,1]{1,0:T(8,128)S(1)} %copy.29.position_ref, f32[2,128,64]{2,1,0:T(8,128)S(1)} %copy-done.2, f32[2,128,64]{2,1,0:T(8,128)S(1)} %collective-permute-done.23.other_ref, bf16[128,1024]{1,0:T(8,128)(2,1)S(1)} %bitcast.61, ...), custom_call_target="tpu_custom_call" | custom-call | tf_op jit(solution)/shard_map/pallas_call | solution.py:332
  (65 shorter events, 0.9 us)
Async XLA Ops:
  0.6 88.8 %copy-start = (f32[4,128,64]{1,2,0:T(8,128)S(1)}, f32[4,128,64]{1,2,0:T(8,128)}, u32[]{:S(2)}) copy-start(f32[4,128,64]{1,2,0:T(8,128)} %param.8) | copy-start | bytes 393220
  0.6 1.6 copy-start.8
  2.4 7.7 %copy-start.3 = (bf16[1024,1024]{1,0:T(8,128)(2,1)}, bf16[1024,1024]{1,0:T(8,128)(2,1)S(1)}, u32[]{:S(2)}) copy-start(bf16[1024,1024]{1,0:T(8,128)(2,1)S(1)} %constant_dynamic-update-slice_fusion.refs_4_.refs_5_) | copy-start | bytes 6291460
  2.4 28.8 %collective-permute-start.2 = (bf16[1024,1024]{1,0:T(8,128)(2,1)S(1)}, bf16[1024,1024]{1,0:T(8,128)(2,1)}, u32[]{:S(2)}, u32[]{:S(2)}) collective-permute-start(bf16[1024,1024]{1,0:T(8,128)(2,1)S(1)} %constant_dynamic-update-slice_fusion.refs_4_.refs_5_), channel_id=1, source_target_pairs={{0,1},{1,0},{2,3},{3,2},{4,5},{5,4},{6,7},{7,6},{8,9},{9,8},{10,11... | collective-permute-start | bytes 6291464 | tf_op jit(solution)/shard_map/ppermute | solution.py:234
  3.2 24.9 %collective-permute-start = (bf16[512,1024]{1,0:T(8,128)(2,1)S(1)}, bf16[512,1024]{1,0:T(8,128)(2,1)}, u32[]{:S(2)}, u32[]{:S(2)}) collective-permute-start(bf16[512,1024]{1,0:T(8,128)(2,1)S(1)} %constant_dynamic-slice_fusion.1), channel_id=1, source_target_pairs={{0,4},{4,0},{8,12},{12,8},{1,5},{5,1},{9,13},{13,9},{2,6},{6,2},{1... | collective-permute-start | bytes 3145736 | tf_op jit(solution)/shard_map/ppermute | solution.py:240
  3.4 27.7 %collective-permute-start.1 = (bf16[512,1024]{1,0:T(8,128)(2,1)S(1)}, bf16[512,1024]{1,0:T(8,128)(2,1)}, u32[]{:S(2)}, u32[]{:S(2)}) collective-permute-start(bf16[512,1024]{1,0:T(8,128)(2,1)S(1)} %constant_dynamic-slice_fusion.1), channel_id=1, source_target_pairs={{4,8},{8,4},{5,9},{9,5},{6,10},{10,6},{7,11},{11,7},{20,24},{24,20... | collective-permute-start | bytes 3145736 | tf_op jit(solution)/shard_map/ppermute | solution.py:240
  10.1 30.0 %collective-permute-start.5 = (bf16[512,1024]{1,0:T(8,128)(2,1)}, bf16[512,1024]{1,0:T(8,128)(2,1)S(1)}, u32[]{:S(2)}, u32[]{:S(2)}) collective-permute-start(bf16[512,1024]{1,0:T(8,128)(2,1)} %slice.61), channel_id=1, source_target_pairs={{0,2},{2,0},{1,3},{3,1},{4,6},{6,4},{5,7},{7,5},{8,10},{10,8},{9,1... | collective-permute-start | bytes 3145736 | tf_op jit(solution)/shard_map/ppermute | solution.py:243
  12.6 44.4 %collective-permute-start.6 = (bf16[512,1024]{1,0:T(8,128)(2,1)}, bf16[512,1024]{1,0:T(8,128)(2,1)}, u32[]{:S(2)}, u32[]{:S(2)}) collective-permute-start(bf16[512,1024]{1,0:T(8,128)(2,1)} %slice.80), channel_id=1, source_target_pairs={{0,2},{2,0},{1,3},{3,1},{4,6},{6,4},{5,7},{7,5},{8,10},{10,8},{9,1... | collective-permute-start | bytes 3145736 | tf_op jit(solution)/shard_map/ppermute | solution.py:243
  31.2 26.1 %collective-permute-start.3 = (bf16[512,1024]{1,0:T(8,128)(2,1)}, bf16[512,1024]{1,0:T(8,128)(2,1)S(1)}, u32[]{:S(2)}, u32[]{:S(2)}) collective-permute-start(bf16[512,1024]{1,0:T(8,128)(2,1)} %collective-permute-done.refs_6_.refs_7_), channel_id=1, source_target_pairs={{4,8},{8,4},{5,9},{9,5},{6,10},{10,6},{7,11},{11,7},{20,24},{24,20... | collective-permute-start | bytes 3145736 | tf_op jit(solution)/shard_map/ppermute | solution.py:240
  34.2 23.6 %collective-permute-start.7 = (bf16[512,1024]{1,0:T(8,128)(2,1)}, bf16[512,1024]{1,0:T(8,128)(2,1)}, u32[]{:S(2)}, u32[]{:S(2)}) collective-permute-start(bf16[512,1024]{1,0:T(8,128)(2,1)} %collective-permute-done.refs_6_.refs_7_), channel_id=1, source_target_pairs={{0,16},{16,0},{1,17},{17,1},{2,18},{18,2},{3,19},{19,3},{4,20},{20... | collective-permute-start | bytes 3145736 | tf_op jit(solution)/shard_map/ppermute | solution.py:237
  35.5 22.6 %collective-permute-start.4 = (bf16[512,1024]{1,0:T(8,128)(2,1)}, bf16[512,1024]{1,0:T(8,128)(2,1)}, u32[]{:S(2)}, u32[]{:S(2)}) collective-permute-start(bf16[512,1024]{1,0:T(8,128)(2,1)} %collective-permute-done.1), channel_id=1, source_target_pairs={{4,0},{8,12},{5,1},{9,13},{6,2},{10,14},{7,3},{11,15},{20,16},{24,... | collective-permute-start | bytes 3145736 | tf_op jit(solution)/shard_map/ppermute | solution.py:240
  40.1 26.8 %copy-start.6 = (bf16[512,1024]{1,0:T(8,128)(2,1)}, bf16[512,1024]{1,0:T(8,128)(2,1)S(1)}, u32[]{:S(2)}) copy-start(bf16[512,1024]{1,0:T(8,128)(2,1)S(1)} %collective-permute-done.5.refs_1_) | copy-start | bytes 3145732
  58.2 30.1 %copy-start.4 = (bf16[512,1024]{1,0:T(8,128)(2,1)}, bf16[512,1024]{1,0:T(8,128)(2,1)S(1)}, u32[]{:S(2)}) copy-start(bf16[512,1024]{1,0:T(8,128)(2,1)S(1)} %broadcast_select_fusion.1.refs_10_.refs_11_) | copy-start | bytes 3145732
  58.2 25.4 %collective-permute-start.9 = (bf16[512,1024]{1,0:T(8,128)(2,1)S(1)}, bf16[512,1024]{1,0:T(8,128)(2,1)S(1)}, u32[]{:S(2)}, u32[]{:S(2)}) collective-permute-start(bf16[512,1024]{1,0:T(8,128)(2,1)S(1)} %collective-permute-done.3), channel_id=1, source_target_pairs={{4,0},{8,12},{5,1},{9,13},{6,2},{10,14},{7,3},{11,15},{20,16},{24,... | collective-permute-start | bytes 3145736 | tf_op jit(solution)/shard_map/ppermute | solution.py:240
  63.6 24.7 %collective-permute-start.13 = (bf16[512,1024]{1,0:T(8,128)(2,1)S(1)}, bf16[512,1024]{1,0:T(8,128)(2,1)}, u32[]{:S(2)}, u32[]{:S(2)}) collective-permute-start(bf16[512,1024]{1,0:T(8,128)(2,1)S(1)} %broadcast_select_fusion.1.refs_10_.refs_11_), channel_id=1, source_target_pairs={{0,16},{16,0},{1,17},{17,1},{2,18},{18,2},{3,19},{19,3},{4,20},{20... | collective-permute-start | bytes 3145736 | tf_op jit(solution)/shard_map/ppermute | solution.py:237
  63.9 25.5 %collective-permute-start.11 = (bf16[512,1024]{1,0:T(8,128)(2,1)}, bf16[512,1024]{1,0:T(8,128)(2,1)}, u32[]{:S(2)}, u32[]{:S(2)}) collective-permute-start(bf16[512,1024]{1,0:T(8,128)(2,1)} %collective-permute-done.refs_6_.refs_7_), channel_id=1, source_target_pairs={{0,1},{1,0},{2,3},{3,2},{4,5},{5,4},{6,7},{7,6},{8,9},{9,8},{10,11... | collective-permute-start | bytes 3145736 | tf_op jit(solution)/shard_map/ppermute | solution.py:234
  66.8 23.7 %collective-permute-start.12 = (bf16[512,1024]{1,0:T(8,128)(2,1)}, bf16[512,1024]{1,0:T(8,128)(2,1)}, u32[]{:S(2)}, u32[]{:S(2)}) collective-permute-start(bf16[512,1024]{1,0:T(8,128)(2,1)} %collective-permute-done.7.refs_7_.refs_8_), channel_id=1, source_target_pairs={{0,1},{1,0},{2,3},{3,2},{4,5},{5,4},{6,7},{7,6},{8,9},{9,8},{10,11... | collective-permute-start | bytes 3145736 | tf_op jit(solution)/shard_map/ppermute | solution.py:234
  69.1 21.1 %copy-start.10 = (s32[512]{0:T(512)S(1)}, s32[512]{0:T(512)}, u32[]{:S(2)}) copy-start(s32[512]{0:T(512)} %param.9) | copy-start | bytes 6148
  69.1 24.4 %collective-permute-start.8 = (bf16[512,1024]{1,0:T(8,128)(2,1)}, bf16[512,1024]{1,0:T(8,128)(2,1)S(1)}, u32[]{:S(2)}, u32[]{:S(2)}) collective-permute-start(bf16[512,1024]{1,0:T(8,128)(2,1)} %slice.63), channel_id=1, source_target_pairs={{0,2},{2,0},{1,3},{3,1},{4,6},{6,4},{5,7},{7,5},{8,10},{10,8},{9,1... | collective-permute-start | bytes 3145736 | tf_op jit(solution)/shard_map/ppermute | solution.py:243
  85.0 9.0 %copy-start.5 = (bf16[512,1024]{1,0:T(8,128)(2,1)}, bf16[512,1024]{1,0:T(8,128)(2,1)S(1)}, u32[]{:S(2)}) copy-start(bf16[512,1024]{1,0:T(8,128)(2,1)S(1)} %broadcast_select_fusion.refs_14_.refs_15_) | copy-start | bytes 3145732
  85.0 8.8 %collective-permute-start.17 = (bf16[512,1024]{1,0:T(8,128)(2,1)S(1)}, bf16[512,1024]{1,0:T(8,128)(2,1)}, u32[]{:S(2)}, u32[]{:S(2)}) collective-permute-start(bf16[512,1024]{1,0:T(8,128)(2,1)S(1)} %broadcast_select_fusion.refs_14_.refs_15_), channel_id=1, source_target_pairs={{0,1},{1,0},{2,3},{3,2},{4,5},{5,4},{6,7},{7,6},{8,9},{9,8},{10,11... | collective-permute-start | bytes 3145736 | tf_op jit(solution)/shard_map/ppermute | solution.py:234
  88.4 5.5 %collective-permute-start.14 = (bf16[512,1024]{1,0:T(8,128)(2,1)S(1)}, bf16[512,1024]{1,0:T(8,128)(2,1)}, u32[]{:S(2)}, u32[]{:S(2)}) collective-permute-start(bf16[512,1024]{1,0:T(8,128)(2,1)S(1)} %broadcast_select_fusion.1.refs_10_.refs_11_), channel_id=1, source_target_pairs={{0,1},{1,0},{2,3},{3,2},{4,5},{5,4},{6,7},{7,6},{8,9},{9,8},{10,11... | collective-permute-start | bytes 3145736 | tf_op jit(solution)/shard_map/ppermute | solution.py:234
  89.4 4.6 %collective-permute-start.15 = (bf16[512,1024]{1,0:T(8,128)(2,1)}, bf16[512,1024]{1,0:T(8,128)(2,1)}, u32[]{:S(2)}, u32[]{:S(2)}) collective-permute-start(bf16[512,1024]{1,0:T(8,128)(2,1)} %collective-permute-done.13.refs_11_.refs_12_), channel_id=1, source_target_pairs={{0,1},{1,0},{2,3},{3,2},{4,5},{5,4},{6,7},{7,6},{8,9},{9,8},{10,11... | collective-permute-start | bytes 3145736 | tf_op jit(solution)/shard_map/ppermute | solution.py:234
  90.5 24.4 %collective-permute-start.16 = (bf16[512,1024]{1,0:T(8,128)(2,1)S(1)}, bf16[512,1024]{1,0:T(8,128)(2,1)S(1)}, u32[]{:S(2)}, u32[]{:S(2)}) collective-permute-start(bf16[512,1024]{1,0:T(8,128)(2,1)S(1)} %broadcast_select_fusion.refs_14_.refs_15_), channel_id=1, source_target_pairs={{0,16},{16,0},{1,17},{17,1},{2,18},{18,2},{3,19},{19,3},{4,20},{20... | collective-permute-start | bytes 3145736 | tf_op jit(solution)/shard_map/ppermute | solution.py:237
  93.6 16.0 %copy-start.1 = (bf16[512,1024]{1,0:T(8,128)(2,1)}, bf16[512,1024]{1,0:T(8,128)(2,1)S(1)}, u32[]{:S(2)}) copy-start(bf16[512,1024]{1,0:T(8,128)(2,1)S(1)} %collective-permute-done.8.refs_3_) | copy-start | bytes 3145732
  93.6 25.0 %collective-permute-start.10 = (bf16[512,1024]{1,0:T(8,128)(2,1)}, bf16[512,1024]{1,0:T(8,128)(2,1)S(1)}, u32[]{:S(2)}, u32[]{:S(2)}) collective-permute-start(bf16[512,1024]{1,0:T(8,128)(2,1)} %slice.64), channel_id=1, source_target_pairs={{0,2},{2,0},{1,3},{3,1},{4,6},{6,4},{5,7},{7,5},{8,10},{10,8},{9,1... | collective-permute-start | bytes 3145736 | tf_op jit(solution)/shard_map/ppermute | solution.py:243
  109.6 6.5 %collective-permute-start.26 = (s32[512]{0:T(512)S(1)}, s32[512]{0:T(512)S(1)}, u32[]{:S(2)}, u32[]{:S(2)}) collective-permute-start(s32[512]{0:T(512)S(1)} %select_reduce_fusion), channel_id=1, source_target_pairs={{0,12},{4,8},{8,4},{12,0},{1,13},{5,9},{9,5},{13,1},{2,14},{6,10},... | collective-permute-start | bytes 6152 | tf_op jit(solution)/shard_map/ppermute | solution.py:279
  109.7 6.5 %collective-permute-start.25 = (s32[512]{0:T(512)S(1)}, s32[512]{0:T(512)S(1)}, u32[]{:S(2)}, u32[]{:S(2)}) collective-permute-start(s32[512]{0:T(512)S(1)} %select_reduce_fusion), channel_id=1, source_target_pairs={{0,8},{4,12},{8,0},{12,4},{1,9},{5,13},{9,1},{13,5},{2,10},{6,14},... | collective-permute-start | bytes 6152 | tf_op jit(solution)/shard_map/ppermute | solution.py:279
  111.3 4.9 %collective-permute-start.24 = (s32[512]{0:T(512)S(1)}, s32[512]{0:T(512)S(1)}, u32[]{:S(2)}, u32[]{:S(2)}) collective-permute-start(s32[512]{0:T(512)S(1)} %select_reduce_fusion), channel_id=1, source_target_pairs={{0,4},{4,0},{8,12},{12,8},{1,5},{5,1},{9,13},{13,9},{2,6},{6,2},{1... | collective-permute-start | bytes 6152 | tf_op jit(solution)/shard_map/ppermute | solution.py:279
  114.9 3.7 %copy-start.7 = (bf16[512,1024]{1,0:T(8,128)(2,1)}, bf16[512,1024]{1,0:T(8,128)(2,1)S(1)}, u32[]{:S(2)}) copy-start(bf16[512,1024]{1,0:T(8,128)(2,1)S(1)} %collective-permute-done.16.refs_16_) | copy-start | bytes 3145732
  114.9 3.7 %collective-permute-start.18 = (bf16[512,1024]{1,0:T(8,128)(2,1)S(1)}, bf16[512,1024]{1,0:T(8,128)(2,1)S(1)}, u32[]{:S(2)}, u32[]{:S(2)}) collective-permute-start(bf16[512,1024]{1,0:T(8,128)(2,1)S(1)} %collective-permute-done.16.refs_16_), channel_id=1, source_target_pairs={{0,1},{1,0},{2,3},{3,2},{4,5},{5,4},{6,7},{7,6},{8,9},{9,8},{10,11... | collective-permute-start | bytes 3145736 | tf_op jit(solution)/shard_map/ppermute | solution.py:234
  116.2 2.3 %collective-permute-start.27 = (s32[4,512]{1,0:T(4,128)S(1)}, s32[4,512]{1,0:T(4,128)S(1)}, u32[]{:S(2)}, u32[]{:S(2)}) collective-permute-start(s32[4,512]{1,0:T(4,128)S(1)} %pad_add_fusion), channel_id=1, source_target_pairs={{0,1},{1,0},{2,3},{3,2},{4,5},{5,4},{6,7},{7,6},{8,9},{9,8},{10,11... | collective-permute-start | bytes 24584 | tf_op jit(solution)/shard_map/ppermute | solution.py:234
  125.2 5.7 %collective-permute-start.28 = (bf16[256,1024]{1,0:T(8,128)(2,1)S(1)}, bf16[256,1024]{1,0:T(8,128)(2,1)S(1)}, u32[]{:S(2)}, u32[]{:S(2)}) collective-permute-start(bf16[256,1024]{1,0:T(8,128)(2,1)S(1)} %convolution_convert_fusion), channel_id=1, source_target_pairs={{0,1},{1,0},{2,3},{3,2},{4,5},{5,4},{6,7},{7,6},{8,9},{9,8},{10,11... | collective-permute-start | bytes 1572872 | tf_op jit(solution)/shard_map/ppermute | solution.py:391
  126.6 1.6 collective-permute-start.19
  128.1 9.5 %copy-start.9 = (f32[136,128]{1,0:T(8,128)}, f32[136,128]{1,0:T(8,128)S(1)}, u32[]{:S(2)}) copy-start(f32[136,128]{1,0:T(8,128)S(1)} %fusion.14.refs_0_) | copy-start | bytes 208900
  128.1 4.2 %collective-permute-start.20 = (f32[136,128]{1,0:T(8,128)S(1)}, f32[136,128]{1,0:T(8,128)S(1)}, u32[]{:S(2)}, u32[]{:S(2)}) collective-permute-start(f32[136,128]{1,0:T(8,128)S(1)} %fusion.14.refs_0_), channel_id=1, source_target_pairs={{0,4},{4,0},{8,12},{12,8},{1,5},{5,1},{9,13},{13,9},{2,6},{6,2},{1... | collective-permute-start | bytes 208904 | tf_op jit(solution)/shard_map/ppermute | solution.py:392
  128.2 5.5 %collective-permute-start.21 = (f32[136,128]{1,0:T(8,128)S(1)}, f32[136,128]{1,0:T(8,128)S(1)}, u32[]{:S(2)}, u32[]{:S(2)}) collective-permute-start(f32[136,128]{1,0:T(8,128)S(1)} %fusion.14.refs_0_), channel_id=1, source_target_pairs={{0,8},{4,12},{8,0},{12,4},{1,9},{5,13},{9,1},{13,5},{2,10},{6,14},... | collective-permute-start | bytes 208904 | tf_op jit(solution)/shard_map/ppermute | solution.py:392
  128.7 9.0 %collective-permute-start.22 = (f32[136,128]{1,0:T(8,128)S(1)}, f32[136,128]{1,0:T(8,128)S(1)}, u32[]{:S(2)}, u32[]{:S(2)}) collective-permute-start(f32[136,128]{1,0:T(8,128)S(1)} %fusion.14.refs_0_), channel_id=1, source_target_pairs={{0,12},{4,8},{8,4},{12,0},{1,13},{5,9},{9,5},{13,1},{2,14},{6,10},... | collective-permute-start | bytes 208904 | tf_op jit(solution)/shard_map/ppermute | solution.py:392
  131.0 22.5 %collective-permute-start.29 = (bf16[128,1024]{1,0:T(8,128)(2,1)S(1)}, bf16[128,1024]{1,0:T(8,128)(2,1)S(1)}, u32[]{:S(2)}, u32[]{:S(2)}) collective-permute-start(bf16[128,1024]{1,0:T(8,128)(2,1)S(1)} %bitcast.67), channel_id=1, source_target_pairs={{0,4},{4,0},{8,12},{12,8},{1,5},{5,1},{9,13},{13,9},{2,6},{6,2},{1... | collective-permute-start | bytes 786440 | tf_op jit(solution)/shard_map/ppermute | solution.py:396
  132.0 21.4 %collective-permute-start.30 = (bf16[128,1024]{1,0:T(8,128)(2,1)S(1)}, bf16[128,1024]{1,0:T(8,128)(2,1)S(1)}, u32[]{:S(2)}, u32[]{:S(2)}) collective-permute-start(bf16[128,1024]{1,0:T(8,128)(2,1)S(1)} %bitcast.66), channel_id=1, source_target_pairs={{0,8},{4,12},{8,0},{12,4},{1,9},{5,13},{9,1},{13,5},{2,10},{6,14},... | collective-permute-start | bytes 786440 | tf_op jit(solution)/shard_map/ppermute | solution.py:396
  132.4 5.3 %copy-start.11 = (f32[136,128]{1,0:T(8,128)}, f32[136,128]{1,0:T(8,128)S(1)}, u32[]{:S(2)}) copy-start(f32[136,128]{1,0:T(8,128)S(1)} %collective-permute-done.20.refs_1_) | copy-start | bytes 208900
  132.4 27.8 %collective-permute-start.31 = (bf16[128,1024]{1,0:T(8,128)(2,1)S(1)}, bf16[128,1024]{1,0:T(8,128)(2,1)S(1)}, u32[]{:S(2)}, u32[]{:S(2)}) collective-permute-start(bf16[128,1024]{1,0:T(8,128)(2,1)S(1)} %bitcast.65), channel_id=1, source_target_pairs={{0,12},{4,8},{8,4},{12,0},{1,13},{5,9},{9,5},{13,1},{2,14},{6,10},... | collective-permute-start | bytes 786440 | tf_op jit(solution)/shard_map/ppermute | solution.py:396
  133.7 4.0 %copy-start.12 = (f32[136,128]{1,0:T(8,128)}, f32[136,128]{1,0:T(8,128)S(1)}, u32[]{:S(2)}) copy-start(f32[136,128]{1,0:T(8,128)S(1)} %collective-permute-done.21.refs_2_) | copy-start | bytes 208900
  137.7 0.6 copy-start.13
  151.4 2.1 %collective-permute-start.23 = (f32[2,128,64]{2,1,0:T(8,128)}, f32[2,128,64]{2,1,0:T(8,128)S(1)}, u32[]{:S(2)}, u32[]{:S(2)}) collective-permute-start(f32[2,128,64]{2,1,0:T(8,128)} %shard_map.70.mine_ref), channel_id=1, source_target_pairs={{0,1},{1,0},{2,3},{3,2},{4,5},{5,4},{6,7},{7,6},{8,9},{9,8},{10,11... | collective-permute-start | bytes 196616 | tf_op jit(solution)/shard_map/ppermute | solution.py:410
  160.2 0.9 copy-start.2

commit v7 on v6

--- a/solution.py
+++ b/solution.py
@@ -217,7 +217,7 @@
         in_specs=specs,
         out_specs=vmem,
         scratch_shapes=scratch,
-        compiler_params=pltpu.CompilerParams(vmem_limit_bytes=36 << 20),
+        compiler_params=pltpu.CompilerParams(vmem_limit_bytes=33 << 20),
         cost_estimate=pl.CostEstimate(
             flops=2 * tokens * feats * width, bytes_accessed=16 << 20, transcendentals=0
         ),

time: 164 us -> 164 us (level)
  no operation moved by 1% of the time
where the time goes in v7:
time: 164 us; the launch traced here: 163 us
  waiting for transfers between devices  69.8 us (43%)
  starting transfers between devices  39 us (24%)
  Pallas kernels  36.7 us (22%)
  local copies, waits for them, and re-layouts  13.5 us (8%)
  other arithmetic  2.28 us (1%)
    ppermute x5, waiting for transfers between devices, along(): return lax.ppermute(value, 'seq', pairs)  32.2 us
    pallas_call x2, Pallas kernels, project(): pl.pallas_call(functools.partial(project_kernel, near, widths, last), out...  21.3 us
    ppermute x4, waiting for transfers between devices, far(): return lax.ppermute(value, 'head', SWAP)  19.4 us
    ppermute x5, starting transfers between devices, along(): return lax.ppermute(value, 'seq', pairs)  15.3 us
    pallas_call x1, Pallas kernels, solve(): pl.pallas_call(functools.partial(solve_kernel, 1.0 / token_total, len(par...  13 us
    ppermute x8, starting transfers between devices, sub(): return lax.ppermute(value, 'sub', SWAP)  9.44 us
    slice x4, local copies, waits for them, and re-layouts, part(): return value[:, bounds[i] * feats // 8:bounds[i + 1] * feats // 8]  9.15 us
    ppermute x3, waiting for transfers between devices, per_device(): lax.ppermute(pairs[d], 'seq', xor(seq, d))  6.77 us
  transfers between devices with their start and end apart: 32, of which 15 were waited for; matrix products, arithmetic and copies ran while one was open for 8% of the time, Pallas kernels for 18%

profile of v7, /device:TPU:11, one launch (start us, length us, event | category | flops | bytes accessed | tf_op | source)
XLA Modules:
  0.0 163.5 jit_solution(1508327847947739156)
XLA Ops:
  0.7 1.5 constant_dynamic-update-slice_fusion.1
  2.1 0.1 copy-done.8
  2.2 0.1 constant_dynamic-update-slice_fusion.refs_4_.refs_5_
  2.4 0.7 collective-permute-start.2
  3.2 0.2 collective-permute-start
  3.4 4.3 %collective-permute-start.1 = (bf16[512,1024]{1,0:T(8,128)(2,1)S(1)}, bf16[512,1024]{1,0:T(8,128)(2,1)}, u32[]{:S(2)}, u32[]{:S(2)}) collective-permute-start(bf16[512,1024]{1,0:T(8,128)(2,1)S(1)} %constant_dynamic-slice_fusion.1), channel_id=1, source_target_pairs={{4,8},{8,4},{5,9},{9,5},{6,10},{10,6},{7,11},{11,7},{20,24},{24,20... | collective-permute-start | bytes 3145736 | tf_op jit(solution)/shard_map/ppermute | solution.py:240
  7.8 2.3 %slice.61 = bf16[512,1024]{1,0:T(8,128)(2,1)} slice(bf16[512,4096]{1,0:T(8,128)(2,1)} %refs_0_.3), slice={[0:512], [0:1024]} | slice | bytes 2097152 | tf_op jit(solution)/shard_map/slice | solution.py:249
  10.1 0.3 collective-permute-start.5
  10.3 2.3 %slice.80 = bf16[512,1024]{1,0:T(8,128)(2,1)} slice(bf16[512,4096]{1,0:T(8,128)(2,1)} %refs_0_.3), slice={[0:512], [1024:2048]} | slice | bytes 2097152 | tf_op jit(solution)/shard_map/slice | solution.py:249
  12.6 1.2 collective-permute-start.6
  13.8 14.3 %collective-permute-done.refs_6_.refs_7_ = bf16[512,1024]{1,0:T(8,128)(2,1)} collective-permute-done((bf16[512,1024]{1,0:T(8,128)(2,1)S(1)}, bf16[512,1024]{1,0:T(8,128)(2,1)}, u32[]{:S(2)}, u32[]{:S(2)}) %collective-permute-start) | collective-permute-done | bytes 1048608 | tf_op jit(solution)/shard_map/ppermute | solution.py:240
  28.1 3.0 %collective-permute-done.1 = bf16[512,1024]{1,0:T(8,128)(2,1)} collective-permute-done((bf16[512,1024]{1,0:T(8,128)(2,1)S(1)}, bf16[512,1024]{1,0:T(8,128)(2,1)}, u32[]{:S(2)}, u32[]{:S(2)}) %collective-permute-start.1) | collective-permute-done | bytes 1048608 | tf_op jit(solution)/shard_map/ppermute | solution.py:240
  31.2 3.0 %collective-permute-start.3 = (bf16[512,1024]{1,0:T(8,128)(2,1)}, bf16[512,1024]{1,0:T(8,128)(2,1)S(1)}, u32[]{:S(2)}, u32[]{:S(2)}) collective-permute-start(bf16[512,1024]{1,0:T(8,128)(2,1)} %collective-permute-done.refs_6_.refs_7_), channel_id=1, source_target_pairs={{4,8},{8,4},{5,9},{9,5},{6,10},{10,6},{7,11},{11,7},{20,24},{24,20... | collective-permute-start | bytes 3145736 | tf_op jit(solution)/shard_map/ppermute | solution.py:240
  34.2 1.3 collective-permute-start.7
  35.5 2.3 %collective-permute-start.4 = (bf16[512,1024]{1,0:T(8,128)(2,1)}, bf16[512,1024]{1,0:T(8,128)(2,1)}, u32[]{:S(2)}, u32[]{:S(2)}) collective-permute-start(bf16[512,1024]{1,0:T(8,128)(2,1)} %collective-permute-done.1), channel_id=1, source_target_pairs={{4,0},{8,12},{5,1},{9,13},{6,2},{10,14},{7,3},{11,15},{20,16},{24,... | collective-permute-start | bytes 3145736 | tf_op jit(solution)/shard_map/ppermute | solution.py:240
  37.8 2.3 %slice.63 = bf16[512,1024]{1,0:T(8,128)(2,1)} slice(bf16[512,4096]{1,0:T(8,128)(2,1)} %refs_0_.3), slice={[0:512], [2048:3072]} | slice | bytes 2097152 | tf_op jit(solution)/shard_map/slice | solution.py:249
  40.1 16.9 %collective-permute-done.6.refs_2_ = bf16[512,1024]{1,0:T(8,128)(2,1)} collective-permute-done((bf16[512,1024]{1,0:T(8,128)(2,1)}, bf16[512,1024]{1,0:T(8,128)(2,1)}, u32[]{:S(2)}, u32[]{:S(2)}) %collective-permute-start.6) | collective-permute-done | bytes 1048608 | tf_op jit(solution)/shard_map/ppermute | solution.py:243
  57.0 0.3 collective-permute-done.3
  57.2 0.6 collective-permute-done.7.refs_7_.refs_8_
  57.8 0.3 collective-permute-done.4
  58.1 0.1 broadcast_select_fusion.1.refs_10_.refs_11_
  58.2 5.4 %collective-permute-start.9 = (bf16[512,1024]{1,0:T(8,128)(2,1)S(1)}, bf16[512,1024]{1,0:T(8,128)(2,1)S(1)}, u32[]{:S(2)}, u32[]{:S(2)}) collective-permute-start(bf16[512,1024]{1,0:T(8,128)(2,1)S(1)} %collective-permute-done.3), channel_id=1, source_target_pairs={{4,0},{8,12},{5,1},{9,13},{6,2},{10,14},{7,3},{11,15},{20,16},{24,... | collective-permute-start | bytes 3145736 | tf_op jit(solution)/shard_map/ppermute | solution.py:240
  63.6 0.3 collective-permute-start.13
  63.9 2.9 %collective-permute-start.11 = (bf16[512,1024]{1,0:T(8,128)(2,1)}, bf16[512,1024]{1,0:T(8,128)(2,1)}, u32[]{:S(2)}, u32[]{:S(2)}) collective-permute-start(bf16[512,1024]{1,0:T(8,128)(2,1)} %collective-permute-done.refs_6_.refs_7_), channel_id=1, source_target_pairs={{0,1},{1,0},{2,3},{3,2},{4,5},{5,4},{6,7},{7,6},{8,9},{9,8},{10,11... | collective-permute-start | bytes 3145736 | tf_op jit(solution)/shard_map/ppermute | solution.py:234
  66.8 2.3 %slice.64 = bf16[512,1024]{1,0:T(8,128)(2,1)} slice(bf16[512,4096]{1,0:T(8,128)(2,1)} %refs_0_.3), slice={[0:512], [3072:4096]} | slice | bytes 2097152 | tf_op jit(solution)/shard_map/slice | solution.py:249
  69.1 0.3 collective-permute-start.8
  69.4 14.3 %collective-permute-done.9 = bf16[512,1024]{1,0:T(8,128)(2,1)S(1)} collective-permute-done((bf16[512,1024]{1,0:T(8,128)(2,1)S(1)}, bf16[512,1024]{1,0:T(8,128)(2,1)S(1)}, u32[]{:S(2)}, u32[]{:S(2)}) %collective-permute-start.9) | collective-permute-done | bytes 1048608 | tf_op jit(solution)/shard_map/ppermute | solution.py:240
  83.7 1.3 broadcast_select_fusion.refs_14_.refs_15_
  85.0 3.3 %collective-permute-start.17 = (bf16[512,1024]{1,0:T(8,128)(2,1)S(1)}, bf16[512,1024]{1,0:T(8,128)(2,1)}, u32[]{:S(2)}, u32[]{:S(2)}) collective-permute-start(bf16[512,1024]{1,0:T(8,128)(2,1)S(1)} %broadcast_select_fusion.refs_14_.refs_15_), channel_id=1, source_target_pairs={{0,1},{1,0},{2,3},{3,2},{4,5},{5,4},{6,7},{7,6},{8,9},{9,8},{10,11... | collective-permute-start | bytes 3145736 | tf_op jit(solution)/shard_map/ppermute | solution.py:234
  88.4 1.0 collective-permute-start.14
  89.5 0.8 copy.32.refs_4_
  90.3 0.2 convert_reduce_fusion
  90.5 0.3 collective-permute-start.16
  90.8 0.2 select_reduce_fusion
  91.1 2.5 %collective-permute-done.8.refs_3_ = bf16[512,1024]{1,0:T(8,128)(2,1)S(1)} collective-permute-done((bf16[512,1024]{1,0:T(8,128)(2,1)}, bf16[512,1024]{1,0:T(8,128)(2,1)S(1)}, u32[]{:S(2)}, u32[]{:S(2)}) %collective-permute-start.8) | collective-permute-done | bytes 1048608 | tf_op jit(solution)/shard_map/ppermute | solution.py:243
  93.6 0.3 collective-permute-start.10
  93.8 0.2 collective-permute-done.15.refs_13_.refs_14_
  94.0 15.6 %shard_map.68.refs_19_ = f32[512,1024]{1,0:T(8,128)S(1)} custom-call(bf16[512,4096]{1,0:T(8,128)(2,1)} %refs_0_.3, bf16[512,1024]{1,0:T(8,128)(2,1)} %copy-done.6, bf16[512,1024]{1,0:T(8,128)(2,1)} %collective-permute-done.6.refs_2_, bf16[512,1024]{1,0:T(8,128)(2,1)S(1)} %collective-permute-done.8.refs_3_, bf16[1024,1024]{1,0:T(8,128)(2,1)} %copy-done.3, ...), custom_call_target="tpu_custom_call" | custom-call | flops 4294967296 | bytes 16777216 | tf_op jit(solution)/shard_map/pallas_call | solution.py:214
  109.7 1.6 collective-permute-start.25
  111.3 1.0 collective-permute-start.24
  112.3 2.5 %collective-permute-done.16.refs_16_ = bf16[512,1024]{1,0:T(8,128)(2,1)S(1)} collective-permute-done((bf16[512,1024]{1,0:T(8,128)(2,1)S(1)}, bf16[512,1024]{1,0:T(8,128)(2,1)S(1)}, u32[]{:S(2)}, u32[]{:S(2)}) %collective-permute-start.16) | collective-permute-done | bytes 1048608 | tf_op jit(solution)/shard_map/ppermute | solution.py:237
  114.9 1.3 collective-permute-start.18
  116.4 2.1 %collective-permute-done.27 = s32[4,512]{1,0:T(4,128)S(1)} collective-permute-done((s32[4,512]{1,0:T(4,128)S(1)}, s32[4,512]{1,0:T(4,128)S(1)}, u32[]{:S(2)}, u32[]{:S(2)}) %collective-permute-start.27) | collective-permute-done | bytes 8224 | tf_op jit(solution)/shard_map/ppermute | solution.py:234
  118.6 5.7 %shard_map.69 = bf16[512,1024]{1,0:T(8,128)(2,1)S(1)} custom-call(bf16[512,4096]{1,0:T(8,128)(2,1)} %refs_0_.3, bf16[512,1024]{1,0:T(8,128)(2,1)} %copy-done.6, bf16[512,1024]{1,0:T(8,128)(2,1)} %collective-permute-done.6.refs_2_, bf16[512,1024]{1,0:T(8,128)(2,1)} %copy-done.1, bf16[512,1024]{1,0:T(8,128)(2,1)S(1)} %collective-permute-done.10.refs_4_, ...), custom_call_target="tpu_custom_call" | custom-call | flops 4294967296 | bytes 16777216 | tf_op jit(solution)/shard_map/pallas_call | solution.py:214
  124.3 0.3 fusion.1
  124.7 0.5 convolution_convert_fusion
  125.2 1.3 collective-permute-start.28
  126.6 0.5 convolution_convert_fusion.1
  127.1 1.0 collective-permute-done.19
  128.2 0.4 collective-permute-start.21
  128.7 2.2 %collective-permute-start.22 = (f32[136,128]{1,0:T(8,128)S(1)}, f32[136,128]{1,0:T(8,128)S(1)}, u32[]{:S(2)}, u32[]{:S(2)}) collective-permute-start(f32[136,128]{1,0:T(8,128)S(1)} %fusion.14.refs_0_), channel_id=1, source_target_pairs={{0,12},{4,8},{8,4},{12,0},{1,13},{5,9},{9,5},{13,1},{2,14},{6,10},... | collective-permute-start | bytes 208904 | tf_op jit(solution)/shard_map/ppermute | solution.py:392
  130.9 0.1 pad_maximum_fusion
  131.0 1.0 collective-permute-start.29
  132.0 0.4 collective-permute-start.30
  132.4 1.3 collective-permute-start.31
  133.7 4.0 %collective-permute-done.22.refs_3_ = f32[136,128]{1,0:T(8,128)S(1)} collective-permute-done((f32[136,128]{1,0:T(8,128)S(1)}, f32[136,128]{1,0:T(8,128)S(1)}, u32[]{:S(2)}, u32[]{:S(2)}) %collective-permute-start.22) | collective-permute-done | bytes 69664 | tf_op jit(solution)/shard_map/ppermute | solution.py:392
  137.7 0.6 copy-done.13
  138.3 13.0 %shard_map.70.mine_ref = f32[2,128,64]{2,1,0:T(8,128)} custom-call(f32[136,128]{1,0:T(8,128)} %copy-done.9, f32[136,128]{1,0:T(8,128)} %copy-done.11, f32[136,128]{1,0:T(8,128)} %copy-done.12, f32[136,128]{1,0:T(8,128)} %copy-done.13, f32[2,128,64]{2,1,0:T(8,128)} %copy.32.refs_4_), custom_call_target="tpu_custom_call" | custom-call | flops 12582912000 | bytes 131072 | tf_op jit(solution)/shard_map/pallas_call | solution.py:93
  151.4 0.9 collective-permute-start.23
  152.2 0.1 copy.29.position_ref
  152.4 1.0 collective-permute-done.23.other_ref
  153.4 6.8 %collective-permute-done.31.refs_3_ = bf16[128,1024]{1,0:T(8,128)(2,1)S(1)} collective-permute-done((bf16[128,1024]{1,0:T(8,128)(2,1)S(1)}, bf16[128,1024]{1,0:T(8,128)(2,1)S(1)}, u32[]{:S(2)}, u32[]{:S(2)}) %collective-permute-start.31) | collective-permute-done | bytes 262176 | tf_op jit(solution)/shard_map/ppermute | solution.py:396
  160.2 0.9 copy-done.2
  161.1 2.4 %shard_map.71 = (bf16[512,256]{1,0:T(8,128)(2,1)}, bf16[512,512]{1,0:T(8,128)(2,1)}) custom-call(s32[512,1]{1,0:T(8,128)S(1)} %copy.29.position_ref, f32[2,128,64]{2,1,0:T(8,128)S(1)} %copy-done.2, f32[2,128,64]{2,1,0:T(8,128)S(1)} %collective-permute-done.23.other_ref, bf16[128,1024]{1,0:T(8,128)(2,1)S(1)} %bitcast.61, ...), custom_call_target="tpu_custom_call" | custom-call | tf_op jit(solution)/shard_map/pallas_call | solution.py:332
  (65 shorter events, 0.9 us)
Async XLA Ops:
  0.6 88.8 %copy-start = (f32[4,128,64]{1,2,0:T(8,128)S(1)}, f32[4,128,64]{1,2,0:T(8,128)}, u32[]{:S(2)}) copy-start(f32[4,128,64]{1,2,0:T(8,128)} %param.8) | copy-start | bytes 393220
  0.6 1.6 copy-start.8
  2.4 7.7 %copy-start.3 = (bf16[1024,1024]{1,0:T(8,128)(2,1)}, bf16[1024,1024]{1,0:T(8,128)(2,1)S(1)}, u32[]{:S(2)}) copy-start(bf16[1024,1024]{1,0:T(8,128)(2,1)S(1)} %constant_dynamic-update-slice_fusion.refs_4_.refs_5_) | copy-start | bytes 6291460
  2.4 28.8 %collective-permute-start.2 = (bf16[1024,1024]{1,0:T(8,128)(2,1)S(1)}, bf16[1024,1024]{1,0:T(8,128)(2,1)}, u32[]{:S(2)}, u32[]{:S(2)}) collective-permute-start(bf16[1024,1024]{1,0:T(8,128)(2,1)S(1)} %constant_dynamic-update-slice_fusion.refs_4_.refs_5_), channel_id=1, source_target_pairs={{0,1},{1,0},{2,3},{3,2},{4,5},{5,4},{6,7},{7,6},{8,9},{9,8},{10,11... | collective-permute-start | bytes 6291464 | tf_op jit(solution)/shard_map/ppermute | solution.py:234
  3.2 24.9 %collective-permute-start = (bf16[512,1024]{1,0:T(8,128)(2,1)S(1)}, bf16[512,1024]{1,0:T(8,128)(2,1)}, u32[]{:S(2)}, u32[]{:S(2)}) collective-permute-start(bf16[512,1024]{1,0:T(8,128)(2,1)S(1)} %constant_dynamic-slice_fusion.1), channel_id=1, source_target_pairs={{0,4},{4,0},{8,12},{12,8},{1,5},{5,1},{9,13},{13,9},{2,6},{6,2},{1... | collective-permute-start | bytes 3145736 | tf_op jit(solution)/shard_map/ppermute | solution.py:240
  3.4 27.7 %collective-permute-start.1 = (bf16[512,1024]{1,0:T(8,128)(2,1)S(1)}, bf16[512,1024]{1,0:T(8,128)(2,1)}, u32[]{:S(2)}, u32[]{:S(2)}) collective-permute-start(bf16[512,1024]{1,0:T(8,128)(2,1)S(1)} %constant_dynamic-slice_fusion.1), channel_id=1, source_target_pairs={{4,8},{8,4},{5,9},{9,5},{6,10},{10,6},{7,11},{11,7},{20,24},{24,20... | collective-permute-start | bytes 3145736 | tf_op jit(solution)/shard_map/ppermute | solution.py:240
  10.1 30.0 %collective-permute-start.5 = (bf16[512,1024]{1,0:T(8,128)(2,1)}, bf16[512,1024]{1,0:T(8,128)(2,1)S(1)}, u32[]{:S(2)}, u32[]{:S(2)}) collective-permute-start(bf16[512,1024]{1,0:T(8,128)(2,1)} %slice.61), channel_id=1, source_target_pairs={{0,2},{2,0},{1,3},{3,1},{4,6},{6,4},{5,7},{7,5},{8,10},{10,8},{9,1... | collective-permute-start | bytes 3145736 | tf_op jit(solution)/shard_map/ppermute | solution.py:243
  12.6 44.4 %collective-permute-start.6 = (bf16[512,1024]{1,0:T(8,128)(2,1)}, bf16[512,1024]{1,0:T(8,128)(2,1)}, u32[]{:S(2)}, u32[]{:S(2)}) collective-permute-start(bf16[512,1024]{1,0:T(8,128)(2,1)} %slice.80), channel_id=1, source_target_pairs={{0,2},{2,0},{1,3},{3,1},{4,6},{6,4},{5,7},{7,5},{8,10},{10,8},{9,1... | collective-permute-start | bytes 3145736 | tf_op jit(solution)/shard_map/ppermute | solution.py:243
  31.2 26.1 %collective-permute-start.3 = (bf16[512,1024]{1,0:T(8,128)(2,1)}, bf16[512,1024]{1,0:T(8,128)(2,1)S(1)}, u32[]{:S(2)}, u32[]{:S(2)}) collective-permute-start(bf16[512,1024]{1,0:T(8,128)(2,1)} %collective-permute-done.refs_6_.refs_7_), channel_id=1, source_target_pairs={{4,8},{8,4},{5,9},{9,5},{6,10},{10,6},{7,11},{11,7},{20,24},{24,20... | collective-permute-start | bytes 3145736 | tf_op jit(solution)/shard_map/ppermute | solution.py:240
  34.2 23.6 %collective-permute-start.7 = (bf16[512,1024]{1,0:T(8,128)(2,1)}, bf16[512,1024]{1,0:T(8,128)(2,1)}, u32[]{:S(2)}, u32[]{:S(2)}) collective-permute-start(bf16[512,1024]{1,0:T(8,128)(2,1)} %collective-permute-done.refs_6_.refs_7_), channel_id=1, source_target_pairs={{0,16},{16,0},{1,17},{17,1},{2,18},{18,2},{3,19},{19,3},{4,20},{20... | collective-permute-start | bytes 3145736 | tf_op jit(solution)/shard_map/ppermute | solution.py:237
  35.5 22.6 %collective-permute-start.4 = (bf16[512,1024]{1,0:T(8,128)(2,1)}, bf16[512,1024]{1,0:T(8,128)(2,1)}, u32[]{:S(2)}, u32[]{:S(2)}) collective-permute-start(bf16[512,1024]{1,0:T(8,128)(2,1)} %collective-permute-done.1), channel_id=1, source_target_pairs={{4,0},{8,12},{5,1},{9,13},{6,2},{10,14},{7,3},{11,15},{20,16},{24,... | collective-permute-start | bytes 3145736 | tf_op jit(solution)/shard_map/ppermute | solution.py:240
  40.1 26.8 %copy-start.6 = (bf16[512,1024]{1,0:T(8,128)(2,1)}, bf16[512,1024]{1,0:T(8,128)(2,1)S(1)}, u32[]{:S(2)}) copy-start(bf16[512,1024]{1,0:T(8,128)(2,1)S(1)} %collective-permute-done.5.refs_1_) | copy-start | bytes 3145732
  58.2 30.1 %copy-start.4 = (bf16[512,1024]{1,0:T(8,128)(2,1)}, bf16[512,1024]{1,0:T(8,128)(2,1)S(1)}, u32[]{:S(2)}) copy-start(bf16[512,1024]{1,0:T(8,128)(2,1)S(1)} %broadcast_select_fusion.1.refs_10_.refs_11_) | copy-start | bytes 3145732
  58.2 25.4 %collective-permute-start.9 = (bf16[512,1024]{1,0:T(8,128)(2,1)S(1)}, bf16[512,1024]{1,0:T(8,128)(2,1)S(1)}, u32[]{:S(2)}, u32[]{:S(2)}) collective-permute-start(bf16[512,1024]{1,0:T(8,128)(2,1)S(1)} %collective-permute-done.3), channel_id=1, source_target_pairs={{4,0},{8,12},{5,1},{9,13},{6,2},{10,14},{7,3},{11,15},{20,16},{24,... | collective-permute-start | bytes 3145736 | tf_op jit(solution)/shard_map/ppermute | solution.py:240
  63.6 24.7 %collective-permute-start.13 = (bf16[512,1024]{1,0:T(8,128)(2,1)S(1)}, bf16[512,1024]{1,0:T(8,128)(2,1)}, u32[]{:S(2)}, u32[]{:S(2)}) collective-permute-start(bf16[512,1024]{1,0:T(8,128)(2,1)S(1)} %broadcast_select_fusion.1.refs_10_.refs_11_), channel_id=1, source_target_pairs={{0,16},{16,0},{1,17},{17,1},{2,18},{18,2},{3,19},{19,3},{4,20},{20... | collective-permute-start | bytes 3145736 | tf_op jit(solution)/shard_map/ppermute | solution.py:237
  63.9 25.5 %collective-permute-start.11 = (bf16[512,1024]{1,0:T(8,128)(2,1)}, bf16[512,1024]{1,0:T(8,128)(2,1)}, u32[]{:S(2)}, u32[]{:S(2)}) collective-permute-start(bf16[512,1024]{1,0:T(8,128)(2,1)} %collective-permute-done.refs_6_.refs_7_), channel_id=1, source_target_pairs={{0,1},{1,0},{2,3},{3,2},{4,5},{5,4},{6,7},{7,6},{8,9},{9,8},{10,11... | collective-permute-start | bytes 3145736 | tf_op jit(solution)/shard_map/ppermute | solution.py:234
  66.8 23.7 %collective-permute-start.12 = (bf16[512,1024]{1,0:T(8,128)(2,1)}, bf16[512,1024]{1,0:T(8,128)(2,1)}, u32[]{:S(2)}, u32[]{:S(2)}) collective-permute-start(bf16[512,1024]{1,0:T(8,128)(2,1)} %collective-permute-done.7.refs_7_.refs_8_), channel_id=1, source_target_pairs={{0,1},{1,0},{2,3},{3,2},{4,5},{5,4},{6,7},{7,6},{8,9},{9,8},{10,11... | collective-permute-start | bytes 3145736 | tf_op jit(solution)/shard_map/ppermute | solution.py:234
  69.1 21.1 %copy-start.10 = (s32[512]{0:T(512)S(1)}, s32[512]{0:T(512)}, u32[]{:S(2)}) copy-start(s32[512]{0:T(512)} %param.9) | copy-start | bytes 6148
  69.1 24.4 %collective-permute-start.8 = (bf16[512,1024]{1,0:T(8,128)(2,1)}, bf16[512,1024]{1,0:T(8,128)(2,1)S(1)}, u32[]{:S(2)}, u32[]{:S(2)}) collective-permute-start(bf16[512,1024]{1,0:T(8,128)(2,1)} %slice.63), channel_id=1, source_target_pairs={{0,2},{2,0},{1,3},{3,1},{4,6},{6,4},{5,7},{7,5},{8,10},{10,8},{9,1... | collective-permute-start | bytes 3145736 | tf_op jit(solution)/shard_map/ppermute | solution.py:243
  85.0 9.0 %copy-start.5 = (bf16[512,1024]{1,0:T(8,128)(2,1)}, bf16[512,1024]{1,0:T(8,128)(2,1)S(1)}, u32[]{:S(2)}) copy-start(bf16[512,1024]{1,0:T(8,128)(2,1)S(1)} %broadcast_select_fusion.refs_14_.refs_15_) | copy-start | bytes 3145732
  85.0 8.8 %collective-permute-start.17 = (bf16[512,1024]{1,0:T(8,128)(2,1)S(1)}, bf16[512,1024]{1,0:T(8,128)(2,1)}, u32[]{:S(2)}, u32[]{:S(2)}) collective-permute-start(bf16[512,1024]{1,0:T(8,128)(2,1)S(1)} %broadcast_select_fusion.refs_14_.refs_15_), channel_id=1, source_target_pairs={{0,1},{1,0},{2,3},{3,2},{4,5},{5,4},{6,7},{7,6},{8,9},{9,8},{10,11... | collective-permute-start | bytes 3145736 | tf_op jit(solution)/shard_map/ppermute | solution.py:234
  88.4 5.5 %collective-permute-start.14 = (bf16[512,1024]{1,0:T(8,128)(2,1)S(1)}, bf16[512,1024]{1,0:T(8,128)(2,1)}, u32[]{:S(2)}, u32[]{:S(2)}) collective-permute-start(bf16[512,1024]{1,0:T(8,128)(2,1)S(1)} %broadcast_select_fusion.1.refs_10_.refs_11_), channel_id=1, source_target_pairs={{0,1},{1,0},{2,3},{3,2},{4,5},{5,4},{6,7},{7,6},{8,9},{9,8},{10,11... | collective-permute-start | bytes 3145736 | tf_op jit(solution)/shard_map/ppermute | solution.py:234
  89.4 4.6 %collective-permute-start.15 = (bf16[512,1024]{1,0:T(8,128)(2,1)}, bf16[512,1024]{1,0:T(8,128)(2,1)}, u32[]{:S(2)}, u32[]{:S(2)}) collective-permute-start(bf16[512,1024]{1,0:T(8,128)(2,1)} %collective-permute-done.13.refs_11_.refs_12_), channel_id=1, source_target_pairs={{0,1},{1,0},{2,3},{3,2},{4,5},{5,4},{6,7},{7,6},{8,9},{9,8},{10,11... | collective-permute-start | bytes 3145736 | tf_op jit(solution)/shard_map/ppermute | solution.py:234
  90.5 24.4 %collective-permute-start.16 = (bf16[512,1024]{1,0:T(8,128)(2,1)S(1)}, bf16[512,1024]{1,0:T(8,128)(2,1)S(1)}, u32[]{:S(2)}, u32[]{:S(2)}) collective-permute-start(bf16[512,1024]{1,0:T(8,128)(2,1)S(1)} %broadcast_select_fusion.refs_14_.refs_15_), channel_id=1, source_target_pairs={{0,16},{16,0},{1,17},{17,1},{2,18},{18,2},{3,19},{19,3},{4,20},{20... | collective-permute-start | bytes 3145736 | tf_op jit(solution)/shard_map/ppermute | solution.py:237
  93.6 16.0 %copy-start.1 = (bf16[512,1024]{1,0:T(8,128)(2,1)}, bf16[512,1024]{1,0:T(8,128)(2,1)S(1)}, u32[]{:S(2)}) copy-start(bf16[512,1024]{1,0:T(8,128)(2,1)S(1)} %collective-permute-done.8.refs_3_) | copy-start | bytes 3145732
  93.6 25.0 %collective-permute-start.10 = (bf16[512,1024]{1,0:T(8,128)(2,1)}, bf16[512,1024]{1,0:T(8,128)(2,1)S(1)}, u32[]{:S(2)}, u32[]{:S(2)}) collective-permute-start(bf16[512,1024]{1,0:T(8,128)(2,1)} %slice.64), channel_id=1, source_target_pairs={{0,2},{2,0},{1,3},{3,1},{4,6},{6,4},{5,7},{7,5},{8,10},{10,8},{9,1... | collective-permute-start | bytes 3145736 | tf_op jit(solution)/shard_map/ppermute | solution.py:243
  109.6 6.5 %collective-permute-start.26 = (s32[512]{0:T(512)S(1)}, s32[512]{0:T(512)S(1)}, u32[]{:S(2)}, u32[]{:S(2)}) collective-permute-start(s32[512]{0:T(512)S(1)} %select_reduce_fusion), channel_id=1, source_target_pairs={{0,12},{4,8},{8,4},{12,0},{1,13},{5,9},{9,5},{13,1},{2,14},{6,10},... | collective-permute-start | bytes 6152 | tf_op jit(solution)/shard_map/ppermute | solution.py:279
  109.7 6.5 %collective-permute-start.25 = (s32[512]{0:T(512)S(1)}, s32[512]{0:T(512)S(1)}, u32[]{:S(2)}, u32[]{:S(2)}) collective-permute-start(s32[512]{0:T(512)S(1)} %select_reduce_fusion), channel_id=1, source_target_pairs={{0,8},{4,12},{8,0},{12,4},{1,9},{5,13},{9,1},{13,5},{2,10},{6,14},... | collective-permute-start | bytes 6152 | tf_op jit(solution)/shard_map/ppermute | solution.py:279
  111.3 4.9 %collective-permute-start.24 = (s32[512]{0:T(512)S(1)}, s32[512]{0:T(512)S(1)}, u32[]{:S(2)}, u32[]{:S(2)}) collective-permute-start(s32[512]{0:T(512)S(1)} %select_reduce_fusion), channel_id=1, source_target_pairs={{0,4},{4,0},{8,12},{12,8},{1,5},{5,1},{9,13},{13,9},{2,6},{6,2},{1... | collective-permute-start | bytes 6152 | tf_op jit(solution)/shard_map/ppermute | solution.py:279
  114.9 3.7 %copy-start.7 = (bf16[512,1024]{1,0:T(8,128)(2,1)}, bf16[512,1024]{1,0:T(8,128)(2,1)S(1)}, u32[]{:S(2)}) copy-start(bf16[512,1024]{1,0:T(8,128)(2,1)S(1)} %collective-permute-done.16.refs_16_) | copy-start | bytes 3145732
  114.9 3.7 %collective-permute-start.18 = (bf16[512,1024]{1,0:T(8,128)(2,1)S(1)}, bf16[512,1024]{1,0:T(8,128)(2,1)S(1)}, u32[]{:S(2)}, u32[]{:S(2)}) collective-permute-start(bf16[512,1024]{1,0:T(8,128)(2,1)S(1)} %collective-permute-done.16.refs_16_), channel_id=1, source_target_pairs={{0,1},{1,0},{2,3},{3,2},{4,5},{5,4},{6,7},{7,6},{8,9},{9,8},{10,11... | collective-permute-start | bytes 3145736 | tf_op jit(solution)/shard_map/ppermute | solution.py:234
  116.2 2.3 %collective-permute-start.27 = (s32[4,512]{1,0:T(4,128)S(1)}, s32[4,512]{1,0:T(4,128)S(1)}, u32[]{:S(2)}, u32[]{:S(2)}) collective-permute-start(s32[4,512]{1,0:T(4,128)S(1)} %pad_add_fusion), channel_id=1, source_target_pairs={{0,1},{1,0},{2,3},{3,2},{4,5},{5,4},{6,7},{7,6},{8,9},{9,8},{10,11... | collective-permute-start | bytes 24584 | tf_op jit(solution)/shard_map/ppermute | solution.py:234
  125.2 5.7 %collective-permute-start.28 = (bf16[256,1024]{1,0:T(8,128)(2,1)S(1)}, bf16[256,1024]{1,0:T(8,128)(2,1)S(1)}, u32[]{:S(2)}, u32[]{:S(2)}) collective-permute-start(bf16[256,1024]{1,0:T(8,128)(2,1)S(1)} %convolution_convert_fusion), channel_id=1, source_target_pairs={{0,1},{1,0},{2,3},{3,2},{4,5},{5,4},{6,7},{7,6},{8,9},{9,8},{10,11... | collective-permute-start | bytes 1572872 | tf_op jit(solution)/shard_map/ppermute | solution.py:391
  126.6 1.6 collective-permute-start.19
  128.1 9.5 %copy-start.9 = (f32[136,128]{1,0:T(8,128)}, f32[136,128]{1,0:T(8,128)S(1)}, u32[]{:S(2)}) copy-start(f32[136,128]{1,0:T(8,128)S(1)} %fusion.14.refs_0_) | copy-start | bytes 208900
  128.1 4.2 %collective-permute-start.20 = (f32[136,128]{1,0:T(8,128)S(1)}, f32[136,128]{1,0:T(8,128)S(1)}, u32[]{:S(2)}, u32[]{:S(2)}) collective-permute-start(f32[136,128]{1,0:T(8,128)S(1)} %fusion.14.refs_0_), channel_id=1, source_target_pairs={{0,4},{4,0},{8,12},{12,8},{1,5},{5,1},{9,13},{13,9},{2,6},{6,2},{1... | collective-permute-start | bytes 208904 | tf_op jit(solution)/shard_map/ppermute | solution.py:392
  128.2 5.5 %collective-permute-start.21 = (f32[136,128]{1,0:T(8,128)S(1)}, f32[136,128]{1,0:T(8,128)S(1)}, u32[]{:S(2)}, u32[]{:S(2)}) collective-permute-start(f32[136,128]{1,0:T(8,128)S(1)} %fusion.14.refs_0_), channel_id=1, source_target_pairs={{0,8},{4,12},{8,0},{12,4},{1,9},{5,13},{9,1},{13,5},{2,10},{6,14},... | collective-permute-start | bytes 208904 | tf_op jit(solution)/shard_map/ppermute | solution.py:392
  128.7 9.0 %collective-permute-start.22 = (f32[136,128]{1,0:T(8,128)S(1)}, f32[136,128]{1,0:T(8,128)S(1)}, u32[]{:S(2)}, u32[]{:S(2)}) collective-permute-start(f32[136,128]{1,0:T(8,128)S(1)} %fusion.14.refs_0_), channel_id=1, source_target_pairs={{0,12},{4,8},{8,4},{12,0},{1,13},{5,9},{9,5},{13,1},{2,14},{6,10},... | collective-permute-start | bytes 208904 | tf_op jit(solution)/shard_map/ppermute | solution.py:392
  131.0 22.5 %collective-permute-start.29 = (bf16[128,1024]{1,0:T(8,128)(2,1)S(1)}, bf16[128,1024]{1,0:T(8,128)(2,1)S(1)}, u32[]{:S(2)}, u32[]{:S(2)}) collective-permute-start(bf16[128,1024]{1,0:T(8,128)(2,1)S(1)} %bitcast.67), channel_id=1, source_target_pairs={{0,4},{4,0},{8,12},{12,8},{1,5},{5,1},{9,13},{13,9},{2,6},{6,2},{1... | collective-permute-start | bytes 786440 | tf_op jit(solution)/shard_map/ppermute | solution.py:396
  132.0 21.4 %collective-permute-start.30 = (bf16[128,1024]{1,0:T(8,128)(2,1)S(1)}, bf16[128,1024]{1,0:T(8,128)(2,1)S(1)}, u32[]{:S(2)}, u32[]{:S(2)}) collective-permute-start(bf16[128,1024]{1,0:T(8,128)(2,1)S(1)} %bitcast.66), channel_id=1, source_target_pairs={{0,8},{4,12},{8,0},{12,4},{1,9},{5,13},{9,1},{13,5},{2,10},{6,14},... | collective-permute-start | bytes 786440 | tf_op jit(solution)/shard_map/ppermute | solution.py:396
  132.4 5.3 %copy-start.11 = (f32[136,128]{1,0:T(8,128)}, f32[136,128]{1,0:T(8,128)S(1)}, u32[]{:S(2)}) copy-start(f32[136,128]{1,0:T(8,128)S(1)} %collective-permute-done.20.refs_1_) | copy-start | bytes 208900
  132.4 27.8 %collective-permute-start.31 = (bf16[128,1024]{1,0:T(8,128)(2,1)S(1)}, bf16[128,1024]{1,0:T(8,128)(2,1)S(1)}, u32[]{:S(2)}, u32[]{:S(2)}) collective-permute-start(bf16[128,1024]{1,0:T(8,128)(2,1)S(1)} %bitcast.65), channel_id=1, source_target_pairs={{0,12},{4,8},{8,4},{12,0},{1,13},{5,9},{9,5},{13,1},{2,14},{6,10},... | collective-permute-start | bytes 786440 | tf_op jit(solution)/shard_map/ppermute | solution.py:396
  133.7 4.0 %copy-start.12 = (f32[136,128]{1,0:T(8,128)}, f32[136,128]{1,0:T(8,128)S(1)}, u32[]{:S(2)}) copy-start(f32[136,128]{1,0:T(8,128)S(1)} %collective-permute-done.21.refs_2_) | copy-start | bytes 208900
  137.7 0.6 copy-start.13
  151.4 2.1 %collective-permute-start.23 = (f32[2,128,64]{2,1,0:T(8,128)}, f32[2,128,64]{2,1,0:T(8,128)S(1)}, u32[]{:S(2)}, u32[]{:S(2)}) collective-permute-start(f32[2,128,64]{2,1,0:T(8,128)} %shard_map.70.mine_ref), channel_id=1, source_target_pairs={{0,1},{1,0},{2,3},{3,2},{4,5},{5,4},{6,7},{7,6},{8,9},{9,8},{10,11... | collective-permute-start | bytes 196616 | tf_op jit(solution)/shard_map/ppermute | solution.py:410
  160.2 0.9 copy-start.2
